TPU v7x, 256 devices: a whole 4x4x8 slice. The times are simulated.
256 devices in a mesh: tm: 16 (over z, core), sx: 4 (over x), sy: 4 (over y).
Axes of the slice: x: 4, y: 4, z: 8, core: 2. Of those that a mesh axis runs over, the one named last changes fastest.
Arguments:
- slices_state: float32 [16, 64, 16, 16, 128], P('tm', None, 'sx', 'sy'), may hold values from -6 to 6
- forcing: float32 [16, 64, 16, 16, 128], P('tm', None, 'sx', 'sy'), may hold values from -0.6 to 0.6
- initial: float32 [64, 16, 16, 128], P(None, 'sx', 'sy'), may hold values from -6 to 6
- volume: float32 [64, 64], replicated, may hold values from -0.06 to 0.06
- lift: float32 [6, 64, 16], replicated, may hold values from -0.024 to 0.024
Outputs:
- corrected: float32 [16, 64, 16, 16, 128], P('tm', None, 'sx', 'sy')
- residual: float32 [16, 64, 16, 16, 128], P('tm', None, 'sx', 'sy')
All inputs are finite; a program needn't handle non-finite values.
Results may differ from a plain program's by a relative error of at most 0.00018.
Values sent between devices are 32-bit elements; how exact they have to be, the bound alone decides.
No kernel may reach another device: no remote copies, remote signals or barrier semaphores. Data moves between devices by JAX's collectives and lax.ppermute only.
A program may use at most 64 MiB of HBM per device.

v0:
```python
import functools

import jax
import jax.numpy as jnp
from jax import lax
from jax.experimental import pallas as pl
from jax.experimental.pallas import tpu as pltpu
from jax.sharding import Mesh, PartitionSpec as P

F32, BF16 = jnp.float32, jnp.bfloat16
AXES = ("tg", "tj", "sx", "sy")
FLAG = pl.BlockSpec(memory_space=pltpu.SMEM)
VM = pl.BlockSpec(memory_space=pltpu.VMEM)
PARAMS = pltpu.CompilerParams(vmem_limit_bytes=40 << 20)
XB, XA, YB, YA, ZB, ZA, G0, G1, G2, G3, FIRST, LAST = range(12)


def ring_of_slabs():
    path = []
    for x in range(4):
        path += [(0, x, y if x % 2 == 0 else 3 - y) for y in range(4)]
    path += [(1, x, y) for _, x, y in reversed(path)]
    return [(2 * c + k) * 16 + 4 * x + y for c, x, y in path for k in range(2)]


DEVICE = ring_of_slabs()
SLAB = [DEVICE.index(d) for d in range(64)]


def call(kernel, out, flops, nbytes, scratch=(), smem=True):
    def run(*args):
        specs = [VM] * len(args)
        if smem:
            specs[0] = FLAG
        return pl.pallas_call(
            kernel,
            out_shape=[jax.ShapeDtypeStruct(s, d) for s, d in out],
            in_specs=specs,
            out_specs=[VM] * len(out),
            scratch_shapes=list(scratch),
            compiler_params=PARAMS,
            cost_estimate=pl.CostEstimate(flops=flops, bytes_accessed=nbytes, transcendentals=0),
        )(*args)

    return run


def split(value):
    high = value.astype(BF16)
    return high, (value - high.astype(F32)).astype(BF16)


def weights_kernel(w_ref, o_ref):
    high, low = split(w_ref[...])
    o_ref[:, 0:160] = high
    o_ref[:, 160:320] = high
    o_ref[:, 320:480] = low


def product(w, parts):
    high, low = split(jnp.concatenate(parts, 0))
    return jnp.dot(w, jnp.concatenate([high, low, high], 0), preferred_element_type=F32)


def y_trace(ref, b, t):
    return jnp.concatenate([ref[t, 16 * a + 4 * b : 16 * a + 4 * b + 4, :] for a in range(4)], 0)


def z_trace(ref, c, t):
    return ref[t, pl.ds(c, 16, stride=4), :]


def tiles(ref, rows, which):
    return jnp.concatenate([ref[t, rows, :] for t in which], 1)


def lanes(shape):
    return lax.broadcasted_iota(jnp.int32, shape, 1)


ALL = slice(None)


def given(ref, t):
    return ref[pl.ds(t, 64, stride=16), :]


def emit_faces(ref, xp, xm, yp, ym):
    for i in range(4):
        xp[i] = ref[12 + i, 48:64, :]
        xm[i] = ref[i, 0:16, :]
        yp[i] = y_trace(ref, 3, 4 * i + 3)
        ym[i] = y_trace(ref, 0, 4 * i)


def gather(flags, which, initial, state, held):
    @pl.when(flags[which] == 1.0)
    def _():
        for t in range(16):
            held[t] = given(initial, t)

    @pl.when(flags[which] == 0.0)
    def _():
        for t in range(16):
            held[t] = given(state, t)


def faces_kernel(flags, initial, state, xp, xm, yp, ym, held):
    gather(flags, LAST, initial, state, held)
    emit_faces(held, xp, xm, yp, ym)


def fine_step(flags, v, source, xb, xa, yb, ya, w, store):
    weight = w[...]
    lane = lanes((16, 128))
    for i in range(4):
        row = [4 * i + j for j in range(4)]
        own = tiles(v, ALL, row)
        if i == 0:
            below_x = tiles(xb, ALL, range(4)) * flags[XB]
        else:
            below_x = tiles(v, slice(48, 64), [t - 4 for t in row])
        if i == 3:
            above_x = tiles(xa, ALL, range(4)) * flags[XA]
        else:
            above_x = tiles(v, slice(0, 16), [t + 4 for t in row])
        below_y = jnp.concatenate([yb[i] * flags[YB]] + [y_trace(v, 3, t) for t in row[:3]], 1)
        above_y = jnp.concatenate([y_trace(v, 0, t) for t in row[1:]] + [ya[i] * flags[YA]], 1)
        below_z = [jnp.where(lane == 0, 0.0, pltpu.roll(z_trace(v, 3, t), 1, 1)) for t in row]
        above_z = [jnp.where(lane == 127, 0.0, pltpu.roll(z_trace(v, 0, t), 127, 1)) for t in row]
        mixed = product(
            weight,
            [own, below_x, above_x, below_y, above_y]
            + [jnp.concatenate(below_z, 1), jnp.concatenate(above_z, 1)],
        )
        value = (own - 0.1 * own) + mixed
        for j, t in enumerate(row):
            store(t, value[:, 128 * j : 128 * j + 128] + given(source, t))


def first_fine_kernel(flags, v, source, xb, xa, yb, ya, w, initial, out, xp, xm, yp, ym, held):
    gather(flags, FIRST, initial, v, held)
    fine_kernel(flags, held, source, xb, xa, yb, ya, w, out, xp, xm, yp, ym)


def fine_kernel(flags, v, source, xb, xa, yb, ya, w, out, xp, xm, yp, ym):
    def store(t, value):
        out[t] = value

    fine_step(flags, v, source, xb, xa, yb, ya, w, store)
    emit_faces(out, xp, xm, yp, ym)


def residual_kernel(flags, v, source, xb, xa, yb, ya, w, state, out, packed, held):
    def store(t, value):
        value = value - given(state, t)
        out[pl.ds(t, 64, stride=16), :] = value
        held[t] = value

    fine_step(flags, v, source, xb, xa, yb, ya, w, store)
    for m in range(8):
        value = jnp.concatenate([held[2 * m], held[2 * m + 1]], 0).T
        packed[pl.ds(m, 128, stride=8), :] = value


def corrected_kernel(received, state, out):
    for m in range(8):
        block = received[pl.ds(m, 128, stride=8), :].T
        for low in range(2):
            t = 2 * m + low
            out[pl.ds(t, 64, stride=16), :] = block[64 * low : 64 * low + 64] + given(state, t)


def coarse_plane(weight, ref, p, below_z, above_z):
    even, odd = 2 * p, 2 * p + 1
    own = tiles(ref, ALL, (even, odd))
    lane = lanes((16, 128))
    x_high, y_high, x_low, y_low = lane // 32, lane // 8 % 4, lane // 2 % 4, lane % 2

    def moved(value, near, first, far, edge):
        away = jnp.where(edge, 0.0, pltpu.roll(value, far, 1))
        return jnp.where(first, away, pltpu.roll(value, near, 1))

    low_x, top_x = x_low == 0, x_low == 3
    low_y, top_y = y_low == 0, y_low == 1
    below_x = [moved(ref[t, 48:64, :], 2, low_x, 26, x_high == 0) for t in (even, odd)]
    above_x = [moved(ref[t, 0:16, :], 126, top_x, 102, x_high == 3) for t in (even, odd)]
    below_y = [
        moved(y_trace(ref, 3, odd), 1, low_y, 7, y_high == 0),
        y_trace(ref, 3, even),
    ]
    above_y = [
        y_trace(ref, 0, odd),
        moved(y_trace(ref, 0, even), 127, top_y, 121, y_high == 3),
    ]
    sides = [jnp.concatenate(pair, 1) for pair in (below_x, above_x, below_y, above_y)]
    mixed = product(weight, [own] + sides + [below_z, above_z])
    return (own - 0.4 * own) + 4.0 * mixed


def plane(ref, p):
    return tiles(ref, ALL, (2 * p, 2 * p + 1))


def put(ref, p, value, rows=ALL):
    ref[2 * p, rows, :] = value[:, 0:128]
    ref[2 * p + 1, rows, :] = value[:, 128:256]


def z_plane(ref, c, p):
    return jnp.concatenate([z_trace(ref, c, 2 * p), z_trace(ref, c, 2 * p + 1)], 1)


def emit_wide(ref, up, down):
    put(up, 0, plane(ref, 1), slice(0, 64))
    put(up, 0, z_plane(ref, 3, 0), slice(64, 80))
    put(down, 0, plane(ref, 0), slice(0, 64))
    put(down, 0, z_plane(ref, 0, 1), slice(64, 80))


def pair_steps(flags, v, below, above, w, extended, first, add_first, add_second, add_halo):
    weight = w[...]
    has_below, has_above = flags[ZB], flags[ZA]
    both = (0, 1)
    put(extended, 0, tiles(below, slice(0, 64), both) * has_below)
    put(extended, 1, plane(v, 0))
    put(extended, 2, plane(v, 1))
    put(extended, 3, tiles(above, slice(0, 64), both) * has_above)
    for p in range(4):
        if p == 0:
            lower = tiles(below, slice(64, 80), both) * has_below
        else:
            lower = z_plane(extended, 3, p - 1)
        if p == 3:
            upper = tiles(above, slice(64, 80), both) * has_above
        else:
            upper = z_plane(extended, 0, p + 1)
        value = coarse_plane(weight, extended, p, lower, upper)
        if p == 0:
            if add_halo:
                value = value + tiles(below, slice(80, 144), both)
            value = value * has_below
        elif p == 3:
            if add_halo:
                value = value + tiles(above, slice(80, 144), both)
            value = value * has_above
        elif add_first is not None:
            value = value + add_first(p - 1)
        put(first, p, value)
    result = []
    for p in (1, 2):
        value = coarse_plane(weight, first, p, z_plane(first, 3, p - 1), z_plane(first, 0, p + 1))
        result.append(value if add_second is None else value + add_second(p - 1))
    return result


def local_first_kernel(received, r, up, down):
    for q in range(8):
        at = [SLAB[q // 2 * 16 + s] * 16 + 8 * (q % 2) for s in range(16)]
        block = jnp.concatenate([received[a : a + 8, :] for a in at], 0).T
        r[2 * q] = block[0:64]
        r[2 * q + 1] = block[64:128]
    emit_wide(r, up, down)
    put(up, 0, plane(r, 3), slice(80, 144))
    put(down, 0, plane(r, 2), slice(80, 144))


def local_pair_kernel(flags, r, below, above, w, out, up, down, extended, first):
    result = pair_steps(
        flags, r, below, above, w, extended, first,
        lambda p: plane(r, 2 + p), lambda p: plane(r, 4 + p), True,
    )
    for p in range(2):
        put(out, p, plane(r, p))
        put(out, 2 + p, plane(first, 1 + p))
        put(out, 4 + p, result[p])
    put(up, 0, z_plane(out, 3, 5))
    put(down, 0, z_plane(out, 0, 4))


def local_last_kernel(flags, e, r, below, above, w, out, up, down):
    weight = w[...]
    for p in range(2):
        lower = plane(below, 0) * flags[ZB] if p == 0 else z_plane(e, 3, 4)
        upper = plane(above, 0) * flags[ZA] if p == 1 else z_plane(e, 0, 5)
        put(out, p, coarse_plane(weight, e, 4 + p, lower, upper) + plane(r, 6 + p))
    emit_wide(out, up, down)


def chain_kernel(flags, v, below, above, w, out, up, down, extended, first):
    result = pair_steps(flags, v, below, above, w, extended, first, None, None, False)
    for p in range(2):
        put(out, p, result[p])
    emit_wide(out, up, down)


def chain_add_kernel(flags, v, below, above, w, add, own, out, ship, up, down, extended, first):
    result = pair_steps(
        flags, v, below, above, w, extended, first, None, lambda p: plane(add, p), False
    )
    for p in range(2):
        put(out, p, result[p])
        put(ship, p, result[p] * flags[G0] + plane(own, p) * (1.0 - flags[G0]))
    emit_wide(out, up, down)


def pick_kernel(flags, one, two, three, out, up, down):
    out[...] = one[...] * flags[G1] + two[...] * flags[G2] + three[...] * flags[G3]
    emit_wide(out, up, down)


def last_first_kernel(flags, v, below, above, w, e, out, tail, up, down, extended, first):
    result = pair_steps(flags, v, below, above, w, extended, first, None, None, False)
    for p in range(2):
        put(out, p, plane(first, 1 + p) + plane(e, p))
        put(tail, p, result[p])
        put(out, 2 + p, result[p] + plane(e, 2 + p))
    emit_wide(tail, up, down)


def last_second_kernel(flags, v, below, above, w, e, e3, head, packed, extended, first):
    result = pair_steps(flags, v, below, above, w, extended, first, None, None, False)
    for q in range(8):
        if q < 4:
            block = jnp.concatenate([head[2 * q], head[2 * q + 1]], 0)
        else:
            p = q % 2
            value = plane(first, 1 + p) + plane(e, 4 + p) if q < 6 else result[p] + plane(e3, p)
            block = jnp.concatenate([value[:, 0:128], value[:, 128:256]], 0)
        block = block.T
        for s in range(16):
            at = SLAB[q // 2 * 16 + s] * 16 + 8 * (q % 2)
            packed[at : at + 8, :] = block[8 * s : 8 * s + 8]


def index_of(t, x, y):
    return (t * 4 + x) * 4 + y


def ring(dt, dx, dy):
    return [
        (index_of(t, x, y), index_of((t + dt) % 16, (x + dx) % 4, (y + dy) % 4))
        for t in range(16)
        for x in range(4)
        for y in range(4)
    ]


def slab_ring(ds):
    return [
        (64 * g + DEVICE[s], 64 * g + DEVICE[(s + ds) % 64]) for g in range(4) for s in range(64)
    ]


def group_swap(mask):
    return [(64 * g + s, 64 * (g ^ mask) + s) for g in range(4) for s in range(64)]


def send(value, pairs):
    return lax.ppermute(value, AXES, pairs)


def local(slices_state, forcing, initial, volume, lift):
    tg, tj = lax.axis_index("tg"), lax.axis_index("tj")
    sx, sy = lax.axis_index("sx"), lax.axis_index("sy")
    corner = (sx == 0) & (sy == 0)
    tm = tg * 4 + tj
    flags = jnp.stack(
        [sx > 0, sx < 3, sy > 0, sy < 3, ~(corner & (tj == 0)), ~(corner & (tj == 3))]
        + [tg == 0, tg == 1, tg == 2, tg == 3, tm == 0, tm == 15]
    ).astype(F32)
    lift_flat = jnp.transpose(lift, (1, 0, 2)).reshape(64, 96)
    w = jnp.concatenate([volume, lift_flat], 1)
    face, wide, trace = ((4, 16, 128), F32), ((2, 80, 128), F32), ((2, 16, 128), F32)
    whole, two, rows = ((16, 64, 128), F32), ((4, 64, 128), F32), ((1024, 128), F32)
    (w,) = call(weights_kernel, [((64, 480), BF16)], 0, 1 << 17, smem=False)(w)

    state = slices_state.reshape(1024, 128)
    source = forcing.reshape(1024, 128)
    start = initial.reshape(1024, 128)
    block = pltpu.VMEM((16, 64, 128), F32)
    faces = call(faces_kernel, [face] * 4, 0, 1 << 19, [block])(flags, start, state)
    fine_cost = (2 * 64 * 480 * 2048, 3 << 19)
    v = send(state, ring(1, 0, 0))
    hops = (ring(1, 1, 0), ring(1, -1, 0), ring(1, 0, 1), ring(1, 0, -1))
    for step in range(3):
        xb, xa, yb, ya = [send(f, pairs) for f, pairs in zip(faces, hops)]
        kernel, held, more = (fine_kernel, [], []) if step else (first_fine_kernel, [block], [start])
        v, *faces = call(kernel, [whole] + [face] * 4, *fine_cost, held)(
            flags, v, source, xb, xa, yb, ya, w, *more
        )
        hops = (ring(0, 1, 0), ring(0, -1, 0), ring(0, 0, 1), ring(0, 0, -1))
    xb, xa, yb, ya = [send(f, pairs) for f, pairs in zip(faces, hops)]
    resid, packed = call(residual_kernel, [rows, rows], *fine_cost, [block])(
        flags, v, source, xb, xa, yb, ya, w, state
    )

    peers = [[64 * g + d for d in DEVICE] for g in range(4)]

    def traded(value):
        return lax.all_to_all(value, AXES, 0, 0, axis_index_groups=peers, tiled=True)

    received = traded(packed)

    up_ring, down_ring = slab_ring(1), slab_ring(-1)

    def exchange(pair):
        up, down = pair
        return send(up, up_ring), send(down, down_ring)

    pair_cost = (2 * 64 * 480 * 1536, 1 << 19)
    scratch = [pltpu.VMEM((8, 64, 128), F32), pltpu.VMEM((8, 64, 128), F32)]
    r, *pair = call(
        local_first_kernel, [whole] + [((2, 144, 128), F32)] * 2, 0, 1 << 20, smem=False
    )(received)
    e, *pair = call(local_pair_kernel, [((12, 64, 128), F32), trace, trace], *pair_cost, scratch)(
        flags, r, *exchange(pair), w
    )
    e3, *pair = call(local_last_kernel, [two, wide, wide], *pair_cost)(
        flags, e, r, *exchange(pair), w
    )
    halo = exchange(pair)
    swap_1 = send(e3, group_swap(1))
    chain = call(chain_kernel, [two, wide, wide], *pair_cost, scratch)
    chain_add = call(chain_add_kernel, [two, two, wide, wide], *pair_cost, scratch)
    x, *pair = chain(flags, e3, *halo, w)
    e7, ship, *pair = chain_add(flags, x, *exchange(pair), w, swap_1, e3)
    halo = exchange(pair)
    swap_2 = send(ship, group_swap(2))
    x, *pair = chain(flags, e7, *halo, w)
    e11, ship, *pair = chain_add(flags, x, *exchange(pair), w, swap_2, e3)
    swap_3 = send(ship, group_swap(3))
    x, *pair = call(pick_kernel, [two, wide, wide], 0, 1 << 18)(flags, swap_1, swap_2, swap_3)
    head, x, *pair = call(
        last_first_kernel, [((8, 64, 128), F32), two, wide, wide], *pair_cost, scratch
    )(flags, x, *exchange(pair), w, e)
    (packed,) = call(last_second_kernel, [rows], *pair_cost, scratch)(
        flags, x, *exchange(pair), w, e, e3, head
    )
    received = traded(packed)
    (corrected,) = call(corrected_kernel, [rows], 0, 3 << 19, smem=False)(received, state)
    shape = (1, 64, 4, 4, 128)
    return corrected.reshape(shape), resid.reshape(shape)


def solution(mesh):
    fine = Mesh(mesh.devices.reshape(4, 4, 4, 4), AXES)
    time = ("tg", "tj")
    placed = (
        P(time, None, "sx", "sy", None),
        P(time, None, "sx", "sy", None),
        P(None, "sx", "sy", None),
        P(),
        P(),
    )
    return jax.shard_map(
        local,
        mesh=fine,
        in_specs=placed,
        out_specs=(P(time, None, "sx", "sy", None), P(time, None, "sx", "sy", None)),
        check_vma=False,
    )
```

profile of v0, /device:TPU:1, one launch (start us, length us, event | category | flops | bytes accessed | tf_op | source)
XLA Modules:
  0.0 143.8 jit_solution(17254606526495738457)
XLA Ops:
  0.6 3.0 %collective-permute-start = (f32[1024,128]{1,0:T(8,128)}, f32[1024,128]{1,0:T(8,128)S(1)}, u32[]{:S(2)}, u32[]{:S(2)}) collective-permute-start(f32[1024,128]{1,0:T(8,128)} %bitcast.28), channel_id=1, source_target_pairs={{0,16},{1,17},{2,18},{3,19},{4,20},{5,21},{6,22},{7,23},{8,24},{9,... | collective-permute-start | bytes 1572872 | tf_op jit(solution)/shard_map/ppermute | solution.py:360
  3.8 1.0 copy-done.1
  4.8 1.0 copy-done.3
  5.9 0.6 shard_map.68
  6.5 1.1 collective-permute-start.1
  7.6 3.3 %collective-permute-start.2 = (f32[4,16,128]{2,1,0:T(8,128)S(1)}, f32[4,16,128]{2,1,0:T(8,128)S(1)}, u32[]{:S(2)}, u32[]{:S(2)}) collective-permute-start(f32[4,16,128]{2,1,0:T(8,128)S(1)} %get-tuple-element.51), channel_id=1, source_target_pairs={{0,28},{1,29},{2,30},{3,31},{4,16},{5,17},{6,18},{7,19},{8,20},{9,... | collective-permute-start | bytes 98312 | tf_op jit(solution)/shard_map/ppermute | solution.py:360
  10.9 1.2 collective-permute-start.3
  12.1 3.1 %collective-permute-start.4 = (f32[4,16,128]{2,1,0:T(8,128)S(1)}, f32[4,16,128]{2,1,0:T(8,128)S(1)}, u32[]{:S(2)}, u32[]{:S(2)}) collective-permute-start(f32[4,16,128]{2,1,0:T(8,128)S(1)} %get-tuple-element.53), channel_id=1, source_target_pairs={{0,19},{1,16},{2,17},{3,18},{4,23},{5,20},{6,21},{7,22},{8,27},{9,... | collective-permute-start | bytes 98312 | tf_op jit(solution)/shard_map/ppermute | solution.py:360
  15.3 0.7 copy-done.6
  16.2 1.4 shard_map.70
  17.7 2.7 %collective-permute-start.6 = (f32[4,16,128]{2,1,0:T(8,128)S(1)}, f32[4,16,128]{2,1,0:T(8,128)S(1)}, u32[]{:S(2)}, u32[]{:S(2)}) collective-permute-start(f32[4,16,128]{2,1,0:T(8,128)S(1)} %get-tuple-element.56), channel_id=1, source_target_pairs={{0,12},{1,13},{2,14},{3,15},{4,0},{5,1},{6,2},{7,3},{8,4},{9,5},{1... | collective-permute-start | bytes 98312 | tf_op jit(solution)/shard_map/ppermute | solution.py:360
  20.4 0.8 collective-permute-start.7
  21.1 1.9 %collective-permute-start.8 = (f32[4,16,128]{2,1,0:T(8,128)S(1)}, f32[4,16,128]{2,1,0:T(8,128)S(1)}, u32[]{:S(2)}, u32[]{:S(2)}) collective-permute-start(f32[4,16,128]{2,1,0:T(8,128)S(1)} %get-tuple-element.58), channel_id=1, source_target_pairs={{0,3},{1,0},{2,1},{3,2},{4,7},{5,4},{6,5},{7,6},{8,11},{9,8},{10,9... | collective-permute-start | bytes 98312 | tf_op jit(solution)/shard_map/ppermute | solution.py:360
  23.0 1.3 collective-permute-done.7.yb
  24.3 1.2 shard_map.71
  25.6 2.7 %collective-permute-start.10 = (f32[4,16,128]{2,1,0:T(8,128)S(1)}, f32[4,16,128]{2,1,0:T(8,128)S(1)}, u32[]{:S(2)}, u32[]{:S(2)}) collective-permute-start(f32[4,16,128]{2,1,0:T(8,128)S(1)} %get-tuple-element.61), channel_id=1, source_target_pairs={{0,12},{1,13},{2,14},{3,15},{4,0},{5,1},{6,2},{7,3},{8,4},{9,5},{1... | collective-permute-start | bytes 98312 | tf_op jit(solution)/shard_map/ppermute | solution.py:360
  28.3 0.9 collective-permute-start.11
  29.2 1.8 %collective-permute-start.12 = (f32[4,16,128]{2,1,0:T(8,128)S(1)}, f32[4,16,128]{2,1,0:T(8,128)S(1)}, u32[]{:S(2)}, u32[]{:S(2)}) collective-permute-start(f32[4,16,128]{2,1,0:T(8,128)S(1)} %get-tuple-element.63), channel_id=1, source_target_pairs={{0,3},{1,0},{2,1},{3,2},{4,7},{5,4},{6,5},{7,6},{8,11},{9,8},{10,9... | collective-permute-start | bytes 98312 | tf_op jit(solution)/shard_map/ppermute | solution.py:360
  31.0 1.3 collective-permute-done.11.yb
  32.3 1.2 shard_map.72
  33.5 0.3 collective-permute-start.13
  33.7 2.7 %collective-permute-start.14 = (f32[4,16,128]{2,1,0:T(8,128)S(1)}, f32[4,16,128]{2,1,0:T(8,128)S(1)}, u32[]{:S(2)}, u32[]{:S(2)}) collective-permute-start(f32[4,16,128]{2,1,0:T(8,128)S(1)} %get-tuple-element.66), channel_id=1, source_target_pairs={{0,12},{1,13},{2,14},{3,15},{4,0},{5,1},{6,2},{7,3},{8,4},{9,5},{1... | collective-permute-start | bytes 98312 | tf_op jit(solution)/shard_map/ppermute | solution.py:360
  36.4 1.0 collective-permute-start.15
  37.4 1.7 %collective-permute-start.16 = (f32[4,16,128]{2,1,0:T(8,128)S(1)}, f32[4,16,128]{2,1,0:T(8,128)S(1)}, u32[]{:S(2)}, u32[]{:S(2)}) collective-permute-start(f32[4,16,128]{2,1,0:T(8,128)S(1)} %get-tuple-element.68), channel_id=1, source_target_pairs={{0,3},{1,0},{2,1},{3,2},{4,7},{5,4},{6,5},{7,6},{8,11},{9,8},{10,9... | collective-permute-start | bytes 98312 | tf_op jit(solution)/shard_map/ppermute | solution.py:360
  39.1 1.3 collective-permute-done.15.yb
  40.4 2.3 %shard_map.73 = (f32[1024,128]{1,0:T(8,128)}, f32[1024,128]{1,0:T(8,128)S(1)}) custom-call(f32[12]{0:T(128)S(1)} %convert_element_type.3.flags, f32[16,64,128]{2,1,0:T(8,128)S(1)} %get-tuple-element.64.v, f32[1024,128]{1,0:T(8,128)S(1)} %bitcast.27, f32[4,16,128]{2,1,0:T(8,128)S(1)} %collective-permute-done.13.xb, ...), custom_call_target="tpu_custom_call" | custom-call | flops 125829120 | bytes 1572864 | tf_op jit(solution)/shard_map/pallas_call | solution.py:35
  42.6 23.9 %all_to_all.22 = f32[64,16,128]{2,1,0:T(8,128)S(1)} all-to-all(f32[64,16,128]{2,1,0:T(8,128)S(1)} %bitcast.37), channel_id=1, replica_groups={{0,16,1,17,2,18,3,19,7,23,6,22,5,21,4,20,8,24,9,25,10,26,11,27,15,31,14..., dimensions={0} | all-to-all | bytes 1048576 | tf_op jit(solution)/shard_map/all_to_all | solution.py:401
  66.6 0.2 shard_map.74
  66.8 0.9 collective-permute-start.17
  67.8 2.0 %collective-permute-done.17.below = f32[2,144,128]{2,1,0:T(8,128)S(1)} collective-permute-done((f32[2,144,128]{2,1,0:T(8,128)S(1)}, f32[2,144,128]{2,1,0:T(8,128)S(1)}, u32[]{:S(2)}, u32[]{:S(2)}) %collective-permute-start.17) | collective-permute-done | bytes 147488 | tf_op jit(solution)/shard_map/ppermute | solution.py:360
  69.7 2.5 %collective-permute-done.18.above = f32[2,144,128]{2,1,0:T(8,128)S(1)} collective-permute-done((f32[2,144,128]{2,1,0:T(8,128)S(1)}, f32[2,144,128]{2,1,0:T(8,128)S(1)}, u32[]{:S(2)}, u32[]{:S(2)}) %collective-permute-start.18) | collective-permute-done | bytes 147488 | tf_op jit(solution)/shard_map/ppermute | solution.py:360
  72.2 1.2 shard_map.75
  73.5 0.5 collective-permute-start.20
  74.0 0.7 collective-permute-done.19.below
  74.7 2.1 %collective-permute-done.20.above = f32[2,16,128]{2,1,0:T(8,128)S(1)} collective-permute-done((f32[2,16,128]{2,1,0:T(8,128)S(1)}, f32[2,16,128]{2,1,0:T(8,128)S(1)}, u32[]{:S(2)}, u32[]{:S(2)}) %collective-permute-start.20) | collective-permute-done | bytes 16416 | tf_op jit(solution)/shard_map/ppermute | solution.py:360
  76.7 0.9 shard_map.76
  77.7 0.5 collective-permute-start.23
  78.2 3.3 %collective-permute-start.21 = (f32[4,64,128]{2,1,0:T(8,128)S(1)}, f32[4,64,128]{2,1,0:T(8,128)S(1)}, u32[]{:S(2)}, u32[]{:S(2)}) collective-permute-start(f32[4,64,128]{2,1,0:T(8,128)S(1)} %get-tuple-element.76.v.own.e3), channel_id=1, source_target_pairs={{0,64},{1,65},{2,66},{3,67},{4,68},{5,69},{6,70},{7,71},{8,72},{9,... | collective-permute-start | bytes 393224 | tf_op jit(solution)/shard_map/ppermute | solution.py:360
  81.6 1.2 shard_map.77
  82.8 1.5 %collective-permute-start.24 = (f32[2,80,128]{2,1,0:T(8,128)S(1)}, f32[2,80,128]{2,1,0:T(8,128)S(1)}, u32[]{:S(2)}, u32[]{:S(2)}) collective-permute-start(f32[2,80,128]{2,1,0:T(8,128)S(1)} %get-tuple-element.80), channel_id=1, source_target_pairs={{0,16},{16,1},{1,17},{17,2},{2,18},{18,3},{3,19},{19,7},{7,23},{23... | collective-permute-start | bytes 245768 | tf_op jit(solution)/shard_map/ppermute | solution.py:360
  84.4 0.4 collective-permute-start.25
  84.7 1.1 collective-permute-done.24.below
  85.9 2.7 %collective-permute-done.25.above = f32[2,80,128]{2,1,0:T(8,128)S(1)} collective-permute-done((f32[2,80,128]{2,1,0:T(8,128)S(1)}, f32[2,80,128]{2,1,0:T(8,128)S(1)}, u32[]{:S(2)}, u32[]{:S(2)}) %collective-permute-start.25) | collective-permute-done | bytes 81952 | tf_op jit(solution)/shard_map/ppermute | solution.py:360
  88.5 1.2 shard_map.78
  89.7 1.1 collective-permute-start.27
  90.8 0.2 collective-permute-start.28
  91.0 3.9 %collective-permute-start.26 = (f32[4,64,128]{2,1,0:T(8,128)S(1)}, f32[4,64,128]{2,1,0:T(8,128)S(1)}, u32[]{:S(2)}, u32[]{:S(2)}) collective-permute-start(f32[4,64,128]{2,1,0:T(8,128)S(1)} %get-tuple-element.82), channel_id=1, source_target_pairs={{0,128},{1,129},{2,130},{3,131},{4,132},{5,133},{6,134},{7,135},{8... | collective-permute-start | bytes 393224 | tf_op jit(solution)/shard_map/ppermute | solution.py:360
  94.8 1.2 shard_map.79
  96.1 2.1 %collective-permute-start.29 = (f32[2,80,128]{2,1,0:T(8,128)S(1)}, f32[2,80,128]{2,1,0:T(8,128)S(1)}, u32[]{:S(2)}, u32[]{:S(2)}) collective-permute-start(f32[2,80,128]{2,1,0:T(8,128)S(1)} %get-tuple-element.87), channel_id=1, source_target_pairs={{0,16},{16,1},{1,17},{17,2},{2,18},{18,3},{3,19},{19,7},{7,23},{23... | collective-permute-start | bytes 245768 | tf_op jit(solution)/shard_map/ppermute | solution.py:360
  98.2 4.8 %collective-permute-done.26.add.two = f32[4,64,128]{2,1,0:T(8,128)S(1)} collective-permute-done((f32[4,64,128]{2,1,0:T(8,128)S(1)}, f32[4,64,128]{2,1,0:T(8,128)S(1)}, u32[]{:S(2)}, u32[]{:S(2)}) %collective-permute-start.26) | collective-permute-done | bytes 131104 | tf_op jit(solution)/shard_map/ppermute | solution.py:360
  103.0 1.9 %shard_map.80 = (f32[4,64,128]{2,1,0:T(8,128)}, f32[4,64,128]{2,1,0:T(8,128)S(1)}, f32[2,80,128]{2,1,0:T(8,128)}, f32[2,80,128]{2,1,0:T(8,128)}) custom-call(f32[12]{0:T(128)S(1)} %convert_element_type.3.flags, f32[4,64,128]{2,1,0:T(8,128)S(1)} %get-tuple-element.86.v, f32[2,80,128]{2,1,0:T(8,128)S(1)} %collective-permute-done.29.below, ...), custom_call_target="tpu_custom_call" | custom-call | flops 94371840 | bytes 524288 | tf_op jit(solution)/shard_map/pallas_call | solution.py:35
  104.9 6.0 %collective-permute-done.31.three = f32[4,64,128]{2,1,0:T(8,128)S(1)} collective-permute-done((f32[4,64,128]{2,1,0:T(8,128)S(1)}, f32[4,64,128]{2,1,0:T(8,128)S(1)}, u32[]{:S(2)}, u32[]{:S(2)}) %collective-permute-start.31) | collective-permute-done | bytes 131104 | tf_op jit(solution)/shard_map/ppermute | solution.py:360
  110.9 0.6 shard_map.81
  111.5 2.4 %collective-permute-start.32 = (f32[2,80,128]{2,1,0:T(8,128)S(1)}, f32[2,80,128]{2,1,0:T(8,128)S(1)}, u32[]{:S(2)}, u32[]{:S(2)}) collective-permute-start(f32[2,80,128]{2,1,0:T(8,128)S(1)} %get-tuple-element.91), channel_id=1, source_target_pairs={{0,16},{16,1},{1,17},{17,2},{2,18},{18,3},{3,19},{19,7},{7,23},{23... | collective-permute-start | bytes 245768 | tf_op jit(solution)/shard_map/ppermute | solution.py:360
  113.9 0.4 collective-permute-start.33
  114.4 1.1 collective-permute-done.32.below
  115.4 2.4 %collective-permute-done.33.above = f32[2,80,128]{2,1,0:T(8,128)S(1)} collective-permute-done((f32[2,80,128]{2,1,0:T(8,128)S(1)}, f32[2,80,128]{2,1,0:T(8,128)S(1)}, u32[]{:S(2)}, u32[]{:S(2)}) %collective-permute-start.33) | collective-permute-done | bytes 81952 | tf_op jit(solution)/shard_map/ppermute | solution.py:360
  117.8 1.2 shard_map.82
  119.1 1.7 %collective-permute-start.35 = (f32[2,80,128]{2,1,0:T(8,128)S(1)}, f32[2,80,128]{2,1,0:T(8,128)S(1)}, u32[]{:S(2)}, u32[]{:S(2)}) collective-permute-start(f32[2,80,128]{2,1,0:T(8,128)S(1)} %get-tuple-element.95), channel_id=1, source_target_pairs={{0,48},{16,0},{1,16},{17,1},{2,17},{18,2},{3,18},{19,3},{7,19},{23... | collective-permute-start | bytes 245768 | tf_op jit(solution)/shard_map/ppermute | solution.py:360
  120.8 0.7 collective-permute-done.34.below
  121.5 1.6 %collective-permute-done.35.above = f32[2,80,128]{2,1,0:T(8,128)S(1)} collective-permute-done((f32[2,80,128]{2,1,0:T(8,128)S(1)}, f32[2,80,128]{2,1,0:T(8,128)S(1)}, u32[]{:S(2)}, u32[]{:S(2)}) %collective-permute-start.35) | collective-permute-done | bytes 81952 | tf_op jit(solution)/shard_map/ppermute | solution.py:360
  123.0 1.3 shard_map.83
  124.3 18.3 %all_to_all.23 = f32[64,16,128]{2,1,0:T(8,128)S(1)} all-to-all(f32[64,16,128]{2,1,0:T(8,128)S(1)} %bitcast.33), channel_id=1, replica_groups={{0,16,1,17,2,18,3,19,7,23,6,22,5,21,4,20,8,24,9,25,10,26,11,27,15,31,14..., dimensions={0} | all-to-all | bytes 1048576 | tf_op jit(solution)/shard_map/all_to_all | solution.py:401
  142.7 1.1 shard_map.84
  (45 shorter events, 1.2 us)
Async XLA Ops:
  0.6 15.6 %collective-permute-start = (f32[1024,128]{1,0:T(8,128)}, f32[1024,128]{1,0:T(8,128)S(1)}, u32[]{:S(2)}, u32[]{:S(2)}) collective-permute-start(f32[1024,128]{1,0:T(8,128)} %bitcast.28), channel_id=1, source_target_pairs={{0,16},{1,17},{2,18},{3,19},{4,20},{5,21},{6,22},{7,23},{8,24},{9,... | collective-permute-start | bytes 1572872 | tf_op jit(solution)/shard_map/ppermute | solution.py:360
  3.7 11.5 %copy-start.5 = (f32[6,64,16]{1,2,0:T(8,128)S(1)}, f32[6,64,16]{1,2,0:T(8,128)}, u32[]{:S(2)}) copy-start(f32[6,64,16]{1,2,0:T(8,128)} %param.9) | copy-start | bytes 73732
  3.8 1.0 copy-start.1
  4.8 1.0 copy-start.3
  5.9 10.4 %copy-start = (f32[1,64,4,4,128]{4,3,2,1,0:T(4,128)S(1)}, f32[1,64,4,4,128]{4,3,2,1,0:T(4,128)}, u32[]{:S(2)}) copy-start(f32[1,64,4,4,128]{4,3,2,1,0:T(4,128)} %param.6) | copy-start | bytes 1572868
  5.9 10.4 %copy-start.4 = (f32[64,4,4,128]{3,2,1,0:T(4,128)S(1)}, f32[64,4,4,128]{3,2,1,0:T(4,128)}, u32[]{:S(2)}) copy-start(f32[64,4,4,128]{3,2,1,0:T(4,128)} %param.7) | copy-start | bytes 1572868
  6.5 9.6 %collective-permute-start.1 = (f32[4,16,128]{2,1,0:T(8,128)S(1)}, f32[4,16,128]{2,1,0:T(8,128)S(1)}, u32[]{:S(2)}, u32[]{:S(2)}) collective-permute-start(f32[4,16,128]{2,1,0:T(8,128)S(1)} %get-tuple-element.50), channel_id=1, source_target_pairs={{0,20},{1,21},{2,22},{3,23},{4,24},{5,25},{6,26},{7,27},{8,28},{9,... | collective-permute-start | bytes 98312 | tf_op jit(solution)/shard_map/ppermute | solution.py:360
  7.6 8.6 %collective-permute-start.2 = (f32[4,16,128]{2,1,0:T(8,128)S(1)}, f32[4,16,128]{2,1,0:T(8,128)S(1)}, u32[]{:S(2)}, u32[]{:S(2)}) collective-permute-start(f32[4,16,128]{2,1,0:T(8,128)S(1)} %get-tuple-element.51), channel_id=1, source_target_pairs={{0,28},{1,29},{2,30},{3,31},{4,16},{5,17},{6,18},{7,19},{8,20},{9,... | collective-permute-start | bytes 98312 | tf_op jit(solution)/shard_map/ppermute | solution.py:360
  10.9 5.3 %collective-permute-start.3 = (f32[4,16,128]{2,1,0:T(8,128)S(1)}, f32[4,16,128]{2,1,0:T(8,128)S(1)}, u32[]{:S(2)}, u32[]{:S(2)}) collective-permute-start(f32[4,16,128]{2,1,0:T(8,128)S(1)} %get-tuple-element.52), channel_id=1, source_target_pairs={{0,17},{1,18},{2,19},{3,16},{4,21},{5,22},{6,23},{7,20},{8,25},{9,... | collective-permute-start | bytes 98312 | tf_op jit(solution)/shard_map/ppermute | solution.py:360
  12.1 4.1 %collective-permute-start.4 = (f32[4,16,128]{2,1,0:T(8,128)S(1)}, f32[4,16,128]{2,1,0:T(8,128)S(1)}, u32[]{:S(2)}, u32[]{:S(2)}) collective-permute-start(f32[4,16,128]{2,1,0:T(8,128)S(1)} %get-tuple-element.53), channel_id=1, source_target_pairs={{0,19},{1,16},{2,17},{3,18},{4,23},{5,20},{6,21},{7,22},{8,27},{9,... | collective-permute-start | bytes 98312 | tf_op jit(solution)/shard_map/ppermute | solution.py:360
  15.2 0.8 copy-start.6
  17.6 5.4 %collective-permute-start.5 = (f32[4,16,128]{2,1,0:T(8,128)S(1)}, f32[4,16,128]{2,1,0:T(8,128)S(1)}, u32[]{:S(2)}, u32[]{:S(2)}) collective-permute-start(f32[4,16,128]{2,1,0:T(8,128)S(1)} %get-tuple-element.55), channel_id=1, source_target_pairs={{0,4},{1,5},{2,6},{3,7},{4,8},{5,9},{6,10},{7,11},{8,12},{9,13},{1... | collective-permute-start | bytes 98312 | tf_op jit(solution)/shard_map/ppermute | solution.py:360
  17.7 5.3 %collective-permute-start.6 = (f32[4,16,128]{2,1,0:T(8,128)S(1)}, f32[4,16,128]{2,1,0:T(8,128)S(1)}, u32[]{:S(2)}, u32[]{:S(2)}) collective-permute-start(f32[4,16,128]{2,1,0:T(8,128)S(1)} %get-tuple-element.56), channel_id=1, source_target_pairs={{0,12},{1,13},{2,14},{3,15},{4,0},{5,1},{6,2},{7,3},{8,4},{9,5},{1... | collective-permute-start | bytes 98312 | tf_op jit(solution)/shard_map/ppermute | solution.py:360
  20.4 4.0 %collective-permute-start.7 = (f32[4,16,128]{2,1,0:T(8,128)S(1)}, f32[4,16,128]{2,1,0:T(8,128)S(1)}, u32[]{:S(2)}, u32[]{:S(2)}) collective-permute-start(f32[4,16,128]{2,1,0:T(8,128)S(1)} %get-tuple-element.57), channel_id=1, source_target_pairs={{0,1},{1,2},{2,3},{3,0},{4,5},{5,6},{6,7},{7,4},{8,9},{9,10},{10,1... | collective-permute-start | bytes 98312 | tf_op jit(solution)/shard_map/ppermute | solution.py:360
  21.1 3.2 %collective-permute-start.8 = (f32[4,16,128]{2,1,0:T(8,128)S(1)}, f32[4,16,128]{2,1,0:T(8,128)S(1)}, u32[]{:S(2)}, u32[]{:S(2)}) collective-permute-start(f32[4,16,128]{2,1,0:T(8,128)S(1)} %get-tuple-element.58), channel_id=1, source_target_pairs={{0,3},{1,0},{2,1},{3,2},{4,7},{5,4},{6,5},{7,6},{8,11},{9,8},{10,9... | collective-permute-start | bytes 98312 | tf_op jit(solution)/shard_map/ppermute | solution.py:360
  25.5 5.4 %collective-permute-start.9 = (f32[4,16,128]{2,1,0:T(8,128)S(1)}, f32[4,16,128]{2,1,0:T(8,128)S(1)}, u32[]{:S(2)}, u32[]{:S(2)}) collective-permute-start(f32[4,16,128]{2,1,0:T(8,128)S(1)} %get-tuple-element.60), channel_id=1, source_target_pairs={{0,4},{1,5},{2,6},{3,7},{4,8},{5,9},{6,10},{7,11},{8,12},{9,13},{1... | collective-permute-start | bytes 98312 | tf_op jit(solution)/shard_map/ppermute | solution.py:360
  25.6 5.3 %collective-permute-start.10 = (f32[4,16,128]{2,1,0:T(8,128)S(1)}, f32[4,16,128]{2,1,0:T(8,128)S(1)}, u32[]{:S(2)}, u32[]{:S(2)}) collective-permute-start(f32[4,16,128]{2,1,0:T(8,128)S(1)} %get-tuple-element.61), channel_id=1, source_target_pairs={{0,12},{1,13},{2,14},{3,15},{4,0},{5,1},{6,2},{7,3},{8,4},{9,5},{1... | collective-permute-start | bytes 98312 | tf_op jit(solution)/shard_map/ppermute | solution.py:360
  28.3 4.0 %collective-permute-start.11 = (f32[4,16,128]{2,1,0:T(8,128)S(1)}, f32[4,16,128]{2,1,0:T(8,128)S(1)}, u32[]{:S(2)}, u32[]{:S(2)}) collective-permute-start(f32[4,16,128]{2,1,0:T(8,128)S(1)} %get-tuple-element.62), channel_id=1, source_target_pairs={{0,1},{1,2},{2,3},{3,0},{4,5},{5,6},{6,7},{7,4},{8,9},{9,10},{10,1... | collective-permute-start | bytes 98312 | tf_op jit(solution)/shard_map/ppermute | solution.py:360
  29.2 3.1 %collective-permute-start.12 = (f32[4,16,128]{2,1,0:T(8,128)S(1)}, f32[4,16,128]{2,1,0:T(8,128)S(1)}, u32[]{:S(2)}, u32[]{:S(2)}) collective-permute-start(f32[4,16,128]{2,1,0:T(8,128)S(1)} %get-tuple-element.63), channel_id=1, source_target_pairs={{0,3},{1,0},{2,1},{3,2},{4,7},{5,4},{6,5},{7,6},{8,11},{9,8},{10,9... | collective-permute-start | bytes 98312 | tf_op jit(solution)/shard_map/ppermute | solution.py:360
  32.3 8.1 %copy-start.2 = (f32[1,64,4,4,128]{4,3,2,1,0:T(4,128)S(1)}, f32[1,64,4,4,128]{4,3,2,1,0:T(4,128)}, u32[]{:S(2)}) copy-start(f32[1,64,4,4,128]{4,3,2,1,0:T(4,128)} %param.5) | copy-start | bytes 1572868
  33.5 5.6 %collective-permute-start.13 = (f32[4,16,128]{2,1,0:T(8,128)S(1)}, f32[4,16,128]{2,1,0:T(8,128)S(1)}, u32[]{:S(2)}, u32[]{:S(2)}) collective-permute-start(f32[4,16,128]{2,1,0:T(8,128)S(1)} %get-tuple-element.65), channel_id=1, source_target_pairs={{0,4},{1,5},{2,6},{3,7},{4,8},{5,9},{6,10},{7,11},{8,12},{9,13},{1... | collective-permute-start | bytes 98312 | tf_op jit(solution)/shard_map/ppermute | solution.py:360
  33.7 5.3 %collective-permute-start.14 = (f32[4,16,128]{2,1,0:T(8,128)S(1)}, f32[4,16,128]{2,1,0:T(8,128)S(1)}, u32[]{:S(2)}, u32[]{:S(2)}) collective-permute-start(f32[4,16,128]{2,1,0:T(8,128)S(1)} %get-tuple-element.66), channel_id=1, source_target_pairs={{0,12},{1,13},{2,14},{3,15},{4,0},{5,1},{6,2},{7,3},{8,4},{9,5},{1... | collective-permute-start | bytes 98312 | tf_op jit(solution)/shard_map/ppermute | solution.py:360
  36.4 4.0 %collective-permute-start.15 = (f32[4,16,128]{2,1,0:T(8,128)S(1)}, f32[4,16,128]{2,1,0:T(8,128)S(1)}, u32[]{:S(2)}, u32[]{:S(2)}) collective-permute-start(f32[4,16,128]{2,1,0:T(8,128)S(1)} %get-tuple-element.67), channel_id=1, source_target_pairs={{0,1},{1,2},{2,3},{3,0},{4,5},{5,6},{6,7},{7,4},{8,9},{9,10},{10,1... | collective-permute-start | bytes 98312 | tf_op jit(solution)/shard_map/ppermute | solution.py:360
  37.4 3.0 %collective-permute-start.16 = (f32[4,16,128]{2,1,0:T(8,128)S(1)}, f32[4,16,128]{2,1,0:T(8,128)S(1)}, u32[]{:S(2)}, u32[]{:S(2)}) collective-permute-start(f32[4,16,128]{2,1,0:T(8,128)S(1)} %get-tuple-element.68), channel_id=1, source_target_pairs={{0,3},{1,0},{2,1},{3,2},{4,7},{5,4},{6,5},{7,6},{8,11},{9,8},{10,9... | collective-permute-start | bytes 98312 | tf_op jit(solution)/shard_map/ppermute | solution.py:360
  66.8 3.0 %collective-permute-start.17 = (f32[2,144,128]{2,1,0:T(8,128)S(1)}, f32[2,144,128]{2,1,0:T(8,128)S(1)}, u32[]{:S(2)}, u32[]{:S(2)}) collective-permute-start(f32[2,144,128]{2,1,0:T(8,128)S(1)} %get-tuple-element.71), channel_id=1, source_target_pairs={{0,16},{16,1},{1,17},{17,2},{2,18},{18,3},{3,19},{19,7},{7,23},{23... | collective-permute-start | bytes 442376 | tf_op jit(solution)/shard_map/ppermute | solution.py:360
  67.6 4.6 %collective-permute-start.18 = (f32[2,144,128]{2,1,0:T(8,128)S(1)}, f32[2,144,128]{2,1,0:T(8,128)S(1)}, u32[]{:S(2)}, u32[]{:S(2)}) collective-permute-start(f32[2,144,128]{2,1,0:T(8,128)S(1)} %get-tuple-element.72), channel_id=1, source_target_pairs={{0,48},{16,0},{1,16},{17,1},{2,17},{18,2},{3,18},{19,3},{7,19},{23... | collective-permute-start | bytes 442376 | tf_op jit(solution)/shard_map/ppermute | solution.py:360
  73.4 1.3 collective-permute-start.19
  73.5 3.2 %collective-permute-start.20 = (f32[2,16,128]{2,1,0:T(8,128)S(1)}, f32[2,16,128]{2,1,0:T(8,128)S(1)}, u32[]{:S(2)}, u32[]{:S(2)}) collective-permute-start(f32[2,16,128]{2,1,0:T(8,128)S(1)} %get-tuple-element.75), channel_id=1, source_target_pairs={{0,48},{16,0},{1,16},{17,1},{2,17},{18,2},{3,18},{19,3},{7,19},{23... | collective-permute-start | bytes 49160 | tf_op jit(solution)/shard_map/ppermute | solution.py:360
  77.6 3.9 %collective-permute-start.22 = (f32[2,80,128]{2,1,0:T(8,128)S(1)}, f32[2,80,128]{2,1,0:T(8,128)S(1)}, u32[]{:S(2)}, u32[]{:S(2)}) collective-permute-start(f32[2,80,128]{2,1,0:T(8,128)S(1)} %get-tuple-element.77), channel_id=1, source_target_pairs={{0,16},{16,1},{1,17},{17,2},{2,18},{18,3},{3,19},{19,7},{7,23},{23... | collective-permute-start | bytes 245768 | tf_op jit(solution)/shard_map/ppermute | solution.py:360
  77.7 3.9 %collective-permute-start.23 = (f32[2,80,128]{2,1,0:T(8,128)S(1)}, f32[2,80,128]{2,1,0:T(8,128)S(1)}, u32[]{:S(2)}, u32[]{:S(2)}) collective-permute-start(f32[2,80,128]{2,1,0:T(8,128)S(1)} %get-tuple-element.78), channel_id=1, source_target_pairs={{0,48},{16,0},{1,16},{17,1},{2,17},{18,2},{3,18},{19,3},{7,19},{23... | collective-permute-start | bytes 245768 | tf_op jit(solution)/shard_map/ppermute | solution.py:360
  78.2 6.6 %collective-permute-start.21 = (f32[4,64,128]{2,1,0:T(8,128)S(1)}, f32[4,64,128]{2,1,0:T(8,128)S(1)}, u32[]{:S(2)}, u32[]{:S(2)}) collective-permute-start(f32[4,64,128]{2,1,0:T(8,128)S(1)} %get-tuple-element.76.v.own.e3), channel_id=1, source_target_pairs={{0,64},{1,65},{2,66},{3,67},{4,68},{5,69},{6,70},{7,71},{8,72},{9,... | collective-permute-start | bytes 393224 | tf_op jit(solution)/shard_map/ppermute | solution.py:360
  82.8 3.0 %collective-permute-start.24 = (f32[2,80,128]{2,1,0:T(8,128)S(1)}, f32[2,80,128]{2,1,0:T(8,128)S(1)}, u32[]{:S(2)}, u32[]{:S(2)}) collective-permute-start(f32[2,80,128]{2,1,0:T(8,128)S(1)} %get-tuple-element.80), channel_id=1, source_target_pairs={{0,16},{16,1},{1,17},{17,2},{2,18},{18,3},{3,19},{19,7},{7,23},{23... | collective-permute-start | bytes 245768 | tf_op jit(solution)/shard_map/ppermute | solution.py:360
  84.4 4.2 %collective-permute-start.25 = (f32[2,80,128]{2,1,0:T(8,128)S(1)}, f32[2,80,128]{2,1,0:T(8,128)S(1)}, u32[]{:S(2)}, u32[]{:S(2)}) collective-permute-start(f32[2,80,128]{2,1,0:T(8,128)S(1)} %get-tuple-element.81), channel_id=1, source_target_pairs={{0,48},{16,0},{1,16},{17,1},{2,17},{18,2},{3,18},{19,3},{7,19},{23... | collective-permute-start | bytes 245768 | tf_op jit(solution)/shard_map/ppermute | solution.py:360
  89.7 5.1 %collective-permute-start.27 = (f32[2,80,128]{2,1,0:T(8,128)S(1)}, f32[2,80,128]{2,1,0:T(8,128)S(1)}, u32[]{:S(2)}, u32[]{:S(2)}) collective-permute-start(f32[2,80,128]{2,1,0:T(8,128)S(1)} %get-tuple-element.84), channel_id=1, source_target_pairs={{0,16},{16,1},{1,17},{17,2},{2,18},{18,3},{3,19},{19,7},{7,23},{23... | collective-permute-start | bytes 245768 | tf_op jit(solution)/shard_map/ppermute | solution.py:360
  90.8 4.0 %collective-permute-start.28 = (f32[2,80,128]{2,1,0:T(8,128)S(1)}, f32[2,80,128]{2,1,0:T(8,128)S(1)}, u32[]{:S(2)}, u32[]{:S(2)}) collective-permute-start(f32[2,80,128]{2,1,0:T(8,128)S(1)} %get-tuple-element.85), channel_id=1, source_target_pairs={{0,48},{16,0},{1,16},{17,1},{2,17},{18,2},{3,18},{19,3},{7,19},{23... | collective-permute-start | bytes 245768 | tf_op jit(solution)/shard_map/ppermute | solution.py:360
  91.0 12.0 %collective-permute-start.26 = (f32[4,64,128]{2,1,0:T(8,128)S(1)}, f32[4,64,128]{2,1,0:T(8,128)S(1)}, u32[]{:S(2)}, u32[]{:S(2)}) collective-permute-start(f32[4,64,128]{2,1,0:T(8,128)S(1)} %get-tuple-element.82), channel_id=1, source_target_pairs={{0,128},{1,129},{2,130},{3,131},{4,132},{5,133},{6,134},{7,135},{8... | collective-permute-start | bytes 393224 | tf_op jit(solution)/shard_map/ppermute | solution.py:360
  96.1 6.9 %collective-permute-start.29 = (f32[2,80,128]{2,1,0:T(8,128)S(1)}, f32[2,80,128]{2,1,0:T(8,128)S(1)}, u32[]{:S(2)}, u32[]{:S(2)}) collective-permute-start(f32[2,80,128]{2,1,0:T(8,128)S(1)} %get-tuple-element.87), channel_id=1, source_target_pairs={{0,16},{16,1},{1,17},{17,2},{2,18},{18,3},{3,19},{19,7},{7,23},{23... | collective-permute-start | bytes 245768 | tf_op jit(solution)/shard_map/ppermute | solution.py:360
  98.2 4.8 %collective-permute-start.30 = (f32[2,80,128]{2,1,0:T(8,128)S(1)}, f32[2,80,128]{2,1,0:T(8,128)S(1)}, u32[]{:S(2)}, u32[]{:S(2)}) collective-permute-start(f32[2,80,128]{2,1,0:T(8,128)S(1)} %get-tuple-element.88), channel_id=1, source_target_pairs={{0,48},{16,0},{1,16},{17,1},{2,17},{18,2},{3,18},{19,3},{7,19},{23... | collective-permute-start | bytes 245768 | tf_op jit(solution)/shard_map/ppermute | solution.py:360
  104.9 6.0 %collective-permute-start.31 = (f32[4,64,128]{2,1,0:T(8,128)S(1)}, f32[4,64,128]{2,1,0:T(8,128)S(1)}, u32[]{:S(2)}, u32[]{:S(2)}) collective-permute-start(f32[4,64,128]{2,1,0:T(8,128)S(1)} %get-tuple-element.89), channel_id=1, source_target_pairs={{0,192},{1,193},{2,194},{3,195},{4,196},{5,197},{6,198},{7,199},{8... | collective-permute-start | bytes 393224 | tf_op jit(solution)/shard_map/ppermute | solution.py:360
  111.5 3.9 %collective-permute-start.32 = (f32[2,80,128]{2,1,0:T(8,128)S(1)}, f32[2,80,128]{2,1,0:T(8,128)S(1)}, u32[]{:S(2)}, u32[]{:S(2)}) collective-permute-start(f32[2,80,128]{2,1,0:T(8,128)S(1)} %get-tuple-element.91), channel_id=1, source_target_pairs={{0,16},{16,1},{1,17},{17,2},{2,18},{18,3},{3,19},{19,7},{7,23},{23... | collective-permute-start | bytes 245768 | tf_op jit(solution)/shard_map/ppermute | solution.py:360
  113.9 3.9 %collective-permute-start.33 = (f32[2,80,128]{2,1,0:T(8,128)S(1)}, f32[2,80,128]{2,1,0:T(8,128)S(1)}, u32[]{:S(2)}, u32[]{:S(2)}) collective-permute-start(f32[2,80,128]{2,1,0:T(8,128)S(1)} %get-tuple-element.92), channel_id=1, source_target_pairs={{0,48},{16,0},{1,16},{17,1},{2,17},{18,2},{3,18},{19,3},{7,19},{23... | collective-permute-start | bytes 245768 | tf_op jit(solution)/shard_map/ppermute | solution.py:360
  119.0 2.5 %collective-permute-start.34 = (f32[2,80,128]{2,1,0:T(8,128)S(1)}, f32[2,80,128]{2,1,0:T(8,128)S(1)}, u32[]{:S(2)}, u32[]{:S(2)}) collective-permute-start(f32[2,80,128]{2,1,0:T(8,128)S(1)} %get-tuple-element.94), channel_id=1, source_target_pairs={{0,16},{16,1},{1,17},{17,2},{2,18},{18,3},{3,19},{19,7},{7,23},{23... | collective-permute-start | bytes 245768 | tf_op jit(solution)/shard_map/ppermute | solution.py:360
  119.1 3.9 %collective-permute-start.35 = (f32[2,80,128]{2,1,0:T(8,128)S(1)}, f32[2,80,128]{2,1,0:T(8,128)S(1)}, u32[]{:S(2)}, u32[]{:S(2)}) collective-permute-start(f32[2,80,128]{2,1,0:T(8,128)S(1)} %get-tuple-element.95), channel_id=1, source_target_pairs={{0,48},{16,0},{1,16},{17,1},{2,17},{18,2},{3,18},{19,3},{7,19},{23... | collective-permute-start | bytes 245768 | tf_op jit(solution)/shard_map/ppermute | solution.py:360
where the time goes:
time: 144 us
  starting transfers between devices  47.4 us (33%)
  blocking collectives  42.2 us (29%)
  waiting for transfers between devices  31.6 us (22%)
  Pallas kernels  18.7 us (13%)
  local copies, waits for them, and re-layouts  2.96 us (2%)
    ppermute x36, starting transfers between devices, send(): return lax.ppermute(value, AXES, pairs)  47.4 us
    all_to_all x2, blocking collectives, traded(): lax.all_to_all(value, AXES, 0, 0, axis_index_groups=peers, tiled=True)  42.2 us
    ppermute x36, waiting for transfers between devices, send(): return lax.ppermute(value, AXES, pairs)  31.6 us
    pallas_call x17, Pallas kernels, run(): pl.pallas_call(kernel, out_shape=[jax.ShapeDtypeStruct(s, d) for s, d in...  18.7 us
  transfers between devices with their start and end apart: 36, of which 17 were waited for; matrix products, arithmetic and copies ran while one was open for 0% of the time, Pallas kernels for 2%

commit v1 on v0

--- a/solution.py
+++ b/solution.py
@@ -9,10 +9,10 @@
 
 F32, BF16 = jnp.float32, jnp.bfloat16
 AXES = ("tg", "tj", "sx", "sy")
-FLAG = pl.BlockSpec(memory_space=pltpu.SMEM)
 VM = pl.BlockSpec(memory_space=pltpu.VMEM)
+ANY = pl.BlockSpec(memory_space=pl.ANY)
 PARAMS = pltpu.CompilerParams(vmem_limit_bytes=40 << 20)
-XB, XA, YB, YA, ZB, ZA, G0, G1, G2, G3, FIRST, LAST = range(12)
+XB, XA, YB, YA, ZB, ZA, FROM_1, FROM_2, FROM_3, FIRST, LAST = range(11)
 
 
 def ring_of_slabs():
@@ -27,15 +27,12 @@
 SLAB = [DEVICE.index(d) for d in range(64)]
 
 
-def call(kernel, out, flops, nbytes, scratch=(), smem=True):
+def call(kernel, out, flops, nbytes, scratch=(), specs=None):
     def run(*args):
-        specs = [VM] * len(args)
-        if smem:
-            specs[0] = FLAG
         return pl.pallas_call(
             kernel,
             out_shape=[jax.ShapeDtypeStruct(s, d) for s, d in out],
-            in_specs=specs,
+            in_specs=specs or [VM] * len(args),
             out_specs=[VM] * len(out),
             scratch_shapes=list(scratch),
             compiler_params=PARAMS,
@@ -72,6 +69,10 @@
 
 def tiles(ref, rows, which):
     return jnp.concatenate([ref[t, rows, :] for t in which], 1)
+
+
+def flag(flags, which, wide=1):
+    return jnp.concatenate([flags[which : which + 1, :]] * wide, 1)
 
 
 def lanes(shape):
@@ -94,15 +95,9 @@
 
 
 def gather(flags, which, initial, state, held):
-    @pl.when(flags[which] == 1.0)
-    def _():
-        for t in range(16):
-            held[t] = given(initial, t)
-
-    @pl.when(flags[which] == 0.0)
-    def _():
-        for t in range(16):
-            held[t] = given(state, t)
+    chosen = flag(flags, which) > 0.5
+    for t in range(16):
+        held[t] = jnp.where(chosen, given(initial, t), given(state, t))
 
 
 def faces_kernel(flags, initial, state, xp, xm, yp, ym, held):
@@ -117,15 +112,15 @@
         row = [4 * i + j for j in range(4)]
         own = tiles(v, ALL, row)
         if i == 0:
-            below_x = tiles(xb, ALL, range(4)) * flags[XB]
+            below_x = tiles(xb, ALL, range(4)) * flag(flags, XB, 4)
         else:
             below_x = tiles(v, slice(48, 64), [t - 4 for t in row])
         if i == 3:
-            above_x = tiles(xa, ALL, range(4)) * flags[XA]
+            above_x = tiles(xa, ALL, range(4)) * flag(flags, XA, 4)
         else:
             above_x = tiles(v, slice(0, 16), [t + 4 for t in row])
-        below_y = jnp.concatenate([yb[i] * flags[YB]] + [y_trace(v, 3, t) for t in row[:3]], 1)
-        above_y = jnp.concatenate([y_trace(v, 0, t) for t in row[1:]] + [ya[i] * flags[YA]], 1)
+        below_y = jnp.concatenate([yb[i] * flag(flags, YB)] + [y_trace(v, 3, t) for t in row[:3]], 1)
+        above_y = jnp.concatenate([y_trace(v, 0, t) for t in row[1:]] + [ya[i] * flag(flags, YA)], 1)
         below_z = [jnp.where(lane == 0, 0.0, pltpu.roll(z_trace(v, 3, t), 1, 1)) for t in row]
         above_z = [jnp.where(lane == 127, 0.0, pltpu.roll(z_trace(v, 0, t), 127, 1)) for t in row]
         mixed = product(
@@ -220,7 +215,7 @@
 
 def pair_steps(flags, v, below, above, w, extended, first, add_first, add_second, add_halo):
     weight = w[...]
-    has_below, has_above = flags[ZB], flags[ZA]
+    has_below, has_above = flag(flags, ZB, 2), flag(flags, ZA, 2)
     both = (0, 1)
     put(extended, 0, tiles(below, slice(0, 64), both) * has_below)
     put(extended, 1, plane(v, 0))
@@ -278,13 +273,12 @@
     put(down, 0, z_plane(out, 0, 4))
 
 
-def local_last_kernel(flags, e, r, below, above, w, out, up, down):
+def local_last_kernel(flags, e, r, below, above, w, out):
     weight = w[...]
     for p in range(2):
-        lower = plane(below, 0) * flags[ZB] if p == 0 else z_plane(e, 3, 4)
-        upper = plane(above, 0) * flags[ZA] if p == 1 else z_plane(e, 0, 5)
+        lower = plane(below, 0) * flag(flags, ZB, 2) if p == 0 else z_plane(e, 3, 4)
+        upper = plane(above, 0) * flag(flags, ZA, 2) if p == 1 else z_plane(e, 0, 5)
         put(out, p, coarse_plane(weight, e, 4 + p, lower, upper) + plane(r, 6 + p))
-    emit_wide(out, up, down)
 
 
 def chain_kernel(flags, v, below, above, w, out, up, down, extended, first):
@@ -294,18 +288,20 @@
     emit_wide(out, up, down)
 
 
-def chain_add_kernel(flags, v, below, above, w, add, own, out, ship, up, down, extended, first):
+def chain_add_kernel(which, flags, v, below, above, w, add, out, up, down, extended, first):
+    chosen = flag(flags, which, 2) > 0.5
     result = pair_steps(
-        flags, v, below, above, w, extended, first, None, lambda p: plane(add, p), False
+        flags, v, below, above, w, extended, first, None,
+        lambda p: jnp.where(chosen, plane(add, p), 0.0), False,
     )
     for p in range(2):
         put(out, p, result[p])
-        put(ship, p, result[p] * flags[G0] + plane(own, p) * (1.0 - flags[G0]))
     emit_wide(out, up, down)
 
 
-def pick_kernel(flags, one, two, three, out, up, down):
-    out[...] = one[...] * flags[G1] + two[...] * flags[G2] + three[...] * flags[G3]
+def begin_kernel(flags, v, waited, out, up, down):
+    for t in range(4):
+        out[t] = jnp.where(flag(flags, FROM_3) > 0.5, v[t], 0.0)
     emit_wide(out, up, down)
 
 
@@ -346,14 +342,12 @@
     ]
 
 
-def slab_ring(ds):
+def slab_ring(ds, dg=0):
     return [
-        (64 * g + DEVICE[s], 64 * g + DEVICE[(s + ds) % 64]) for g in range(4) for s in range(64)
+        (64 * g + DEVICE[s], 64 * ((g + dg) % 4) + DEVICE[(s + ds) % 64])
+        for g in range(4)
+        for s in range(64)
     ]
-
-
-def group_swap(mask):
-    return [(64 * g + s, 64 * (g ^ mask) + s) for g in range(4) for s in range(64)]
 
 
 def send(value, pairs):
@@ -367,13 +361,14 @@
     tm = tg * 4 + tj
     flags = jnp.stack(
         [sx > 0, sx < 3, sy > 0, sy < 3, ~(corner & (tj == 0)), ~(corner & (tj == 3))]
-        + [tg == 0, tg == 1, tg == 2, tg == 3, tm == 0, tm == 15]
+        + [tg >= 1, tg >= 2, tg >= 3, tm == 0, tm == 15]
     ).astype(F32)
+    flags = jnp.broadcast_to(flags[:, None], (11, 128))
     lift_flat = jnp.transpose(lift, (1, 0, 2)).reshape(64, 96)
     w = jnp.concatenate([volume, lift_flat], 1)
     face, wide, trace = ((4, 16, 128), F32), ((2, 80, 128), F32), ((2, 16, 128), F32)
     whole, two, rows = ((16, 64, 128), F32), ((4, 64, 128), F32), ((1024, 128), F32)
-    (w,) = call(weights_kernel, [((64, 480), BF16)], 0, 1 << 17, smem=False)(w)
+    (w,) = call(weights_kernel, [((64, 480), BF16)], 0, 1 << 17)(w)
 
     state = slices_state.reshape(1024, 128)
     source = forcing.reshape(1024, 128)
@@ -411,26 +406,24 @@
     pair_cost = (2 * 64 * 480 * 1536, 1 << 19)
     scratch = [pltpu.VMEM((8, 64, 128), F32), pltpu.VMEM((8, 64, 128), F32)]
     r, *pair = call(
-        local_first_kernel, [whole] + [((2, 144, 128), F32)] * 2, 0, 1 << 20, smem=False
+        local_first_kernel, [whole] + [((2, 144, 128), F32)] * 2, 0, 1 << 20
     )(received)
     e, *pair = call(local_pair_kernel, [((12, 64, 128), F32), trace, trace], *pair_cost, scratch)(
         flags, r, *exchange(pair), w
     )
-    e3, *pair = call(local_last_kernel, [two, wide, wide], *pair_cost)(
-        flags, e, r, *exchange(pair), w
-    )
-    halo = exchange(pair)
-    swap_1 = send(e3, group_swap(1))
+    (e3,) = call(local_last_kernel, [two], *pair_cost)(flags, e, r, *exchange(pair), w)
+    from_3 = send(e3, slab_ring(0, 3))
+    from_1 = send(e3, slab_ring(0, 1))
     chain = call(chain_kernel, [two, wide, wide], *pair_cost, scratch)
-    chain_add = call(chain_add_kernel, [two, two, wide, wide], *pair_cost, scratch)
-    x, *pair = chain(flags, e3, *halo, w)
-    e7, ship, *pair = chain_add(flags, x, *exchange(pair), w, swap_1, e3)
-    halo = exchange(pair)
-    swap_2 = send(ship, group_swap(2))
-    x, *pair = chain(flags, e7, *halo, w)
-    e11, ship, *pair = chain_add(flags, x, *exchange(pair), w, swap_2, e3)
-    swap_3 = send(ship, group_swap(3))
-    x, *pair = call(pick_kernel, [two, wide, wide], 0, 1 << 18)(flags, swap_1, swap_2, swap_3)
+    begin = call(begin_kernel, [two, wide, wide], 0, 1 << 18, (), [VM, VM, ANY])
+    x, *pair = begin(flags, from_3, from_1)
+    from_2 = send(from_1, slab_ring(0, 1))
+    for which, add in ((FROM_2, from_2), (FROM_1, from_1)):
+        x, *pair = chain(flags, x, *exchange(pair), w)
+        kernel = functools.partial(chain_add_kernel, which)
+        x, *pair = call(kernel, [two, wide, wide], *pair_cost, scratch)(
+            flags, x, *exchange(pair), w, add
+        )
     head, x, *pair = call(
         last_first_kernel, [((8, 64, 128), F32), two, wide, wide], *pair_cost, scratch
     )(flags, x, *exchange(pair), w, e)
@@ -438,7 +431,7 @@
         flags, x, *exchange(pair), w, e, e3, head
     )
     received = traded(packed)
-    (corrected,) = call(corrected_kernel, [rows], 0, 3 << 19, smem=False)(received, state)
+    (corrected,) = call(corrected_kernel, [rows], 0, 3 << 19)(received, state)
     shape = (1, 64, 4, 4, 128)
     return corrected.reshape(shape), resid.reshape(shape)
 

time: 144 us -> 136 us (0.944)
  Pallas kernels: 18.7 us -> 10.4 us
  waiting for transfers between devices: 31.6 us -> 37.6 us
  starting transfers between devices: 47.4 us -> 43.8 us
  blocking collectives: 42.2 us -> 39.8 us
    pallas_call x17, Pallas kernels: 18.7 us -> 10.4 us  [run(): pl.pallas_call(kernel, out_shape=[jax.ShapeDtypeStruct(s, d) for s, d in...]
    ppermute x36, waiting for transfers between devices: 31.6 us -> 37.6 us  [send(): return lax.ppermute(value, AXES, pairs)]
    ppermute x36, starting transfers between devices: 47.4 us -> 43.8 us  [send(): return lax.ppermute(value, AXES, pairs)]
    all_to_all x2, blocking collectives: 42.2 us -> 39.8 us  [traded(): lax.all_to_all(value, AXES, 0, 0, axis_index_groups=peers, tiled=True)]
  transfers between devices with their start and end apart: 36 -> 36, of which waited for: 17 -> 21; matrix products, arithmetic and copies ran while one was open for 0% -> 0% of each run, Pallas kernels for 2% -> 1%
where the time goes in v1:
time: 136 us
  starting transfers between devices  43.8 us (32%)
  blocking collectives  39.8 us (29%)
  waiting for transfers between devices  37.6 us (28%)
  Pallas kernels  10.4 us (8%)
  local copies, waits for them, and re-layouts  3.04 us (2%)
    ppermute x36, starting transfers between devices, send(): return lax.ppermute(value, AXES, pairs)  43.8 us
    all_to_all x2, blocking collectives, traded(): lax.all_to_all(value, AXES, 0, 0, axis_index_groups=peers, tiled=True)  39.8 us
    ppermute x36, waiting for transfers between devices, send(): return lax.ppermute(value, AXES, pairs)  37.6 us
    pallas_call x17, Pallas kernels, run(): pl.pallas_call(kernel, out_shape=[jax.ShapeDtypeStruct(s, d) for s, d in...  10.4 us
    unnamed x14, local copies, waits for them, and re-layouts  2.79 us
  transfers between devices with their start and end apart: 36, of which 21 were waited for; matrix products, arithmetic and copies ran while one was open for 0% of the time, Pallas kernels for 1%

profile of v1, /device:TPU:1, one launch (start us, length us, event | category | flops | bytes accessed | tf_op | source)
XLA Modules:
  0.0 135.6 jit_solution(9276622369298546007)
XLA Ops:
  0.6 3.0 %collective-permute-start = (f32[1024,128]{1,0:T(8,128)}, f32[1024,128]{1,0:T(8,128)S(1)}, u32[]{:S(2)}, u32[]{:S(2)}) collective-permute-start(f32[1024,128]{1,0:T(8,128)} %bitcast.27), channel_id=1, source_target_pairs={{0,16},{1,17},{2,18},{3,19},{4,20},{5,21},{6,22},{7,23},{8,24},{9,... | collective-permute-start | bytes 1572872 | tf_op jit(solution)/shard_map/ppermute | solution.py:354
  3.9 1.0 copy-done.1
  4.9 1.0 copy-done.3
  6.1 1.1 collective-permute-start.1
  7.1 3.3 %collective-permute-start.2 = (f32[4,16,128]{2,1,0:T(8,128)S(1)}, f32[4,16,128]{2,1,0:T(8,128)S(1)}, u32[]{:S(2)}, u32[]{:S(2)}) collective-permute-start(f32[4,16,128]{2,1,0:T(8,128)S(1)} %get-tuple-element.49), channel_id=1, source_target_pairs={{0,28},{1,29},{2,30},{3,31},{4,16},{5,17},{6,18},{7,19},{8,20},{9,... | collective-permute-start | bytes 98312 | tf_op jit(solution)/shard_map/ppermute | solution.py:354
  10.5 1.2 collective-permute-start.3
  11.7 3.1 %collective-permute-start.4 = (f32[4,16,128]{2,1,0:T(8,128)S(1)}, f32[4,16,128]{2,1,0:T(8,128)S(1)}, u32[]{:S(2)}, u32[]{:S(2)}) collective-permute-start(f32[4,16,128]{2,1,0:T(8,128)S(1)} %get-tuple-element.51), channel_id=1, source_target_pairs={{0,19},{1,16},{2,17},{3,18},{4,23},{5,20},{6,21},{7,22},{8,27},{9,... | collective-permute-start | bytes 98312 | tf_op jit(solution)/shard_map/ppermute | solution.py:354
  14.9 0.7 copy-done.6
  15.8 1.0 shard_map.70
  16.9 2.7 %collective-permute-start.6 = (f32[4,16,128]{2,1,0:T(8,128)S(1)}, f32[4,16,128]{2,1,0:T(8,128)S(1)}, u32[]{:S(2)}, u32[]{:S(2)}) collective-permute-start(f32[4,16,128]{2,1,0:T(8,128)S(1)} %get-tuple-element.54), channel_id=1, source_target_pairs={{0,12},{1,13},{2,14},{3,15},{4,0},{5,1},{6,2},{7,3},{8,4},{9,5},{1... | collective-permute-start | bytes 98312 | tf_op jit(solution)/shard_map/ppermute | solution.py:354
  19.5 0.8 collective-permute-start.7
  20.3 1.9 %collective-permute-start.8 = (f32[4,16,128]{2,1,0:T(8,128)S(1)}, f32[4,16,128]{2,1,0:T(8,128)S(1)}, u32[]{:S(2)}, u32[]{:S(2)}) collective-permute-start(f32[4,16,128]{2,1,0:T(8,128)S(1)} %get-tuple-element.56), channel_id=1, source_target_pairs={{0,3},{1,0},{2,1},{3,2},{4,7},{5,4},{6,5},{7,6},{8,11},{9,8},{10,9... | collective-permute-start | bytes 98312 | tf_op jit(solution)/shard_map/ppermute | solution.py:354
  22.2 1.6 %collective-permute-done.7.yb = f32[4,16,128]{2,1,0:T(8,128)S(1)} collective-permute-done((f32[4,16,128]{2,1,0:T(8,128)S(1)}, f32[4,16,128]{2,1,0:T(8,128)S(1)}, u32[]{:S(2)}, u32[]{:S(2)}) %collective-permute-start.7) | collective-permute-done | bytes 32800 | tf_op jit(solution)/shard_map/ppermute | solution.py:354
  23.8 0.6 shard_map.71
  24.5 2.7 %collective-permute-start.10 = (f32[4,16,128]{2,1,0:T(8,128)S(1)}, f32[4,16,128]{2,1,0:T(8,128)S(1)}, u32[]{:S(2)}, u32[]{:S(2)}) collective-permute-start(f32[4,16,128]{2,1,0:T(8,128)S(1)} %get-tuple-element.59), channel_id=1, source_target_pairs={{0,12},{1,13},{2,14},{3,15},{4,0},{5,1},{6,2},{7,3},{8,4},{9,5},{1... | collective-permute-start | bytes 98312 | tf_op jit(solution)/shard_map/ppermute | solution.py:354
  27.2 0.6 collective-permute-start.11
  27.8 2.1 %collective-permute-start.12 = (f32[4,16,128]{2,1,0:T(8,128)S(1)}, f32[4,16,128]{2,1,0:T(8,128)S(1)}, u32[]{:S(2)}, u32[]{:S(2)}) collective-permute-start(f32[4,16,128]{2,1,0:T(8,128)S(1)} %get-tuple-element.61), channel_id=1, source_target_pairs={{0,3},{1,0},{2,1},{3,2},{4,7},{5,4},{6,5},{7,6},{8,11},{9,8},{10,9... | collective-permute-start | bytes 98312 | tf_op jit(solution)/shard_map/ppermute | solution.py:354
  29.9 1.3 collective-permute-done.11.yb
  31.2 0.6 shard_map.72
  31.8 0.3 collective-permute-start.13
  32.1 2.7 %collective-permute-start.14 = (f32[4,16,128]{2,1,0:T(8,128)S(1)}, f32[4,16,128]{2,1,0:T(8,128)S(1)}, u32[]{:S(2)}, u32[]{:S(2)}) collective-permute-start(f32[4,16,128]{2,1,0:T(8,128)S(1)} %get-tuple-element.64), channel_id=1, source_target_pairs={{0,12},{1,13},{2,14},{3,15},{4,0},{5,1},{6,2},{7,3},{8,4},{9,5},{1... | collective-permute-start | bytes 98312 | tf_op jit(solution)/shard_map/ppermute | solution.py:354
  34.7 0.7 collective-permute-start.15
  35.4 2.0 %collective-permute-start.16 = (f32[4,16,128]{2,1,0:T(8,128)S(1)}, f32[4,16,128]{2,1,0:T(8,128)S(1)}, u32[]{:S(2)}, u32[]{:S(2)}) collective-permute-start(f32[4,16,128]{2,1,0:T(8,128)S(1)} %get-tuple-element.66), channel_id=1, source_target_pairs={{0,3},{1,0},{2,1},{3,2},{4,7},{5,4},{6,5},{7,6},{8,11},{9,8},{10,9... | collective-permute-start | bytes 98312 | tf_op jit(solution)/shard_map/ppermute | solution.py:354
  37.4 1.3 collective-permute-done.15.yb
  38.7 1.7 %shard_map.73 = (f32[1024,128]{1,0:T(8,128)}, f32[1024,128]{1,0:T(8,128)S(1)}) custom-call(f32[11,128]{1,0:T(8,128)S(1)} %broadcast_in_dim.2.flags, f32[16,64,128]{2,1,0:T(8,128)S(1)} %get-tuple-element.62.v, f32[1024,128]{1,0:T(8,128)S(1)} %bitcast.26, f32[4,16,128]{2,1,0:T(8,128)S(1)} %collective-permute-done.13.xb, ...), custom_call_target="tpu_custom_call" | custom-call | flops 125829120 | bytes 1572864 | tf_op jit(solution)/shard_map/pallas_call | solution.py:32
  40.4 23.6 %all_to_all.22 = f32[64,16,128]{2,1,0:T(8,128)S(1)} all-to-all(f32[64,16,128]{2,1,0:T(8,128)S(1)} %bitcast.36), channel_id=1, replica_groups={{0,16,1,17,2,18,3,19,7,23,6,22,5,21,4,20,8,24,9,25,10,26,11,27,15,31,14..., dimensions={0} | all-to-all | bytes 1048576 | tf_op jit(solution)/shard_map/all_to_all | solution.py:396
  64.0 0.2 shard_map.74
  64.2 0.9 collective-permute-start.17
  65.2 2.0 %collective-permute-done.17.below = f32[2,144,128]{2,1,0:T(8,128)S(1)} collective-permute-done((f32[2,144,128]{2,1,0:T(8,128)S(1)}, f32[2,144,128]{2,1,0:T(8,128)S(1)}, u32[]{:S(2)}, u32[]{:S(2)}) %collective-permute-start.17) | collective-permute-done | bytes 147488 | tf_op jit(solution)/shard_map/ppermute | solution.py:354
  67.1 2.5 %collective-permute-done.18.above = f32[2,144,128]{2,1,0:T(8,128)S(1)} collective-permute-done((f32[2,144,128]{2,1,0:T(8,128)S(1)}, f32[2,144,128]{2,1,0:T(8,128)S(1)}, u32[]{:S(2)}, u32[]{:S(2)}) %collective-permute-start.18) | collective-permute-done | bytes 147488 | tf_op jit(solution)/shard_map/ppermute | solution.py:354
  69.6 0.7 shard_map.75
  70.4 0.5 collective-permute-start.20
  70.9 0.7 collective-permute-done.19.below
  71.5 2.1 %collective-permute-done.20.above = f32[2,16,128]{2,1,0:T(8,128)S(1)} collective-permute-done((f32[2,16,128]{2,1,0:T(8,128)S(1)}, f32[2,16,128]{2,1,0:T(8,128)S(1)}, u32[]{:S(2)}, u32[]{:S(2)}) %collective-permute-start.20) | collective-permute-done | bytes 16416 | tf_op jit(solution)/shard_map/ppermute | solution.py:354
  73.6 0.3 shard_map.76.e3
  73.9 3.4 %collective-permute-start.22 = (f32[4,64,128]{2,1,0:T(8,128)S(1)}, f32[4,64,128]{2,1,0:T(8,128)S(1)}, u32[]{:S(2)}, u32[]{:S(2)}) collective-permute-start(f32[4,64,128]{2,1,0:T(8,128)S(1)} %shard_map.76.e3), channel_id=1, source_target_pairs={{0,64},{16,80},{1,65},{17,81},{2,66},{18,82},{3,67},{19,83},{7,71}... | collective-permute-start | bytes 393224 | tf_op jit(solution)/shard_map/ppermute | solution.py:354
  77.3 0.3 collective-permute-start.21
  77.6 3.7 %collective-permute-done.22.waited.add = f32[4,64,128]{2,1,0:T(8,128)S(1)} collective-permute-done((f32[4,64,128]{2,1,0:T(8,128)S(1)}, f32[4,64,128]{2,1,0:T(8,128)S(1)}, u32[]{:S(2)}, u32[]{:S(2)}) %collective-permute-start.22) | collective-permute-done | bytes 131104 | tf_op jit(solution)/shard_map/ppermute | solution.py:354
  81.2 3.6 %collective-permute-done.21.v = f32[4,64,128]{2,1,0:T(8,128)S(1)} collective-permute-done((f32[4,64,128]{2,1,0:T(8,128)S(1)}, f32[4,64,128]{2,1,0:T(8,128)S(1)}, u32[]{:S(2)}, u32[]{:S(2)}) %collective-permute-start.21) | collective-permute-done | bytes 131104 | tf_op jit(solution)/shard_map/ppermute | solution.py:354
  84.8 3.0 %collective-permute-start.23 = (f32[2,80,128]{2,1,0:T(8,128)S(1)}, f32[2,80,128]{2,1,0:T(8,128)S(1)}, u32[]{:S(2)}, u32[]{:S(2)}) collective-permute-start(f32[2,80,128]{2,1,0:T(8,128)S(1)} %get-tuple-element.75), channel_id=1, source_target_pairs={{0,16},{16,1},{1,17},{17,2},{2,18},{18,3},{3,19},{19,7},{7,23},{23... | collective-permute-start | bytes 245768 | tf_op jit(solution)/shard_map/ppermute | solution.py:354
  87.8 3.1 %collective-permute-start.27 = (f32[4,64,128]{2,1,0:T(8,128)S(1)}, f32[4,64,128]{2,1,0:T(8,128)S(1)}, u32[]{:S(2)}, u32[]{:S(2)}) collective-permute-start(f32[4,64,128]{2,1,0:T(8,128)S(1)} %collective-permute-done.22.waited.add), channel_id=1, source_target_pairs={{0,64},{16,80},{1,65},{17,81},{2,66},{18,82},{3,67},{19,83},{7,71}... | collective-permute-start | bytes 393224 | tf_op jit(solution)/shard_map/ppermute | solution.py:354
  90.9 0.7 collective-permute-done.24.above
  91.7 0.6 shard_map.78
  92.3 1.6 %collective-permute-start.25 = (f32[2,80,128]{2,1,0:T(8,128)S(1)}, f32[2,80,128]{2,1,0:T(8,128)S(1)}, u32[]{:S(2)}, u32[]{:S(2)}) collective-permute-start(f32[2,80,128]{2,1,0:T(8,128)S(1)} %get-tuple-element.78), channel_id=1, source_target_pairs={{0,16},{16,1},{1,17},{17,2},{2,18},{18,3},{3,19},{19,7},{7,23},{23... | collective-permute-start | bytes 245768 | tf_op jit(solution)/shard_map/ppermute | solution.py:354
  93.9 3.9 %collective-permute-done.27.add = f32[4,64,128]{2,1,0:T(8,128)S(1)} collective-permute-done((f32[4,64,128]{2,1,0:T(8,128)S(1)}, f32[4,64,128]{2,1,0:T(8,128)S(1)}, u32[]{:S(2)}, u32[]{:S(2)}) %collective-permute-start.27) | collective-permute-done | bytes 131104 | tf_op jit(solution)/shard_map/ppermute | solution.py:354
  98.0 0.6 shard_map.79
  98.6 0.9 collective-permute-start.28
  99.6 1.5 %collective-permute-done.28.below = f32[2,80,128]{2,1,0:T(8,128)S(1)} collective-permute-done((f32[2,80,128]{2,1,0:T(8,128)S(1)}, f32[2,80,128]{2,1,0:T(8,128)S(1)}, u32[]{:S(2)}, u32[]{:S(2)}) %collective-permute-start.28) | collective-permute-done | bytes 81952 | tf_op jit(solution)/shard_map/ppermute | solution.py:354
  101.1 2.4 %collective-permute-done.29.above = f32[2,80,128]{2,1,0:T(8,128)S(1)} collective-permute-done((f32[2,80,128]{2,1,0:T(8,128)S(1)}, f32[2,80,128]{2,1,0:T(8,128)S(1)}, u32[]{:S(2)}, u32[]{:S(2)}) %collective-permute-start.29) | collective-permute-done | bytes 81952 | tf_op jit(solution)/shard_map/ppermute | solution.py:354
  103.5 0.6 shard_map.80
  104.2 0.5 collective-permute-start.31
  104.7 1.0 collective-permute-done.30.below
  105.7 2.5 %collective-permute-done.31.above = f32[2,80,128]{2,1,0:T(8,128)S(1)} collective-permute-done((f32[2,80,128]{2,1,0:T(8,128)S(1)}, f32[2,80,128]{2,1,0:T(8,128)S(1)}, u32[]{:S(2)}, u32[]{:S(2)}) %collective-permute-start.31) | collective-permute-done | bytes 81952 | tf_op jit(solution)/shard_map/ppermute | solution.py:354
  108.1 0.6 shard_map.81
  108.9 0.5 collective-permute-start.33
  109.4 1.0 collective-permute-done.32.below
  110.4 2.5 %collective-permute-done.33.above = f32[2,80,128]{2,1,0:T(8,128)S(1)} collective-permute-done((f32[2,80,128]{2,1,0:T(8,128)S(1)}, f32[2,80,128]{2,1,0:T(8,128)S(1)}, u32[]{:S(2)}, u32[]{:S(2)}) %collective-permute-start.33) | collective-permute-done | bytes 81952 | tf_op jit(solution)/shard_map/ppermute | solution.py:354
  112.8 0.7 shard_map.82
  113.6 0.5 collective-permute-start.35
  114.1 1.0 collective-permute-done.34.below
  115.1 2.5 %collective-permute-done.35.above = f32[2,80,128]{2,1,0:T(8,128)S(1)} collective-permute-done((f32[2,80,128]{2,1,0:T(8,128)S(1)}, f32[2,80,128]{2,1,0:T(8,128)S(1)}, u32[]{:S(2)}, u32[]{:S(2)}) %collective-permute-start.35) | collective-permute-done | bytes 81952 | tf_op jit(solution)/shard_map/ppermute | solution.py:354
  117.5 0.7 shard_map.83
  118.3 16.2 %all_to_all.23 = f32[64,16,128]{2,1,0:T(8,128)S(1)} all-to-all(f32[64,16,128]{2,1,0:T(8,128)S(1)} %bitcast.33), channel_id=1, replica_groups={{0,16,1,17,2,18,3,19,7,23,6,22,5,21,4,20,8,24,9,25,10,26,11,27,15,31,14..., dimensions={0} | all-to-all | bytes 1048576 | tf_op jit(solution)/shard_map/all_to_all | solution.py:396
  134.4 1.1 shard_map.84
  (46 shorter events, 1.5 us)
Async XLA Ops:
  0.6 15.2 %collective-permute-start = (f32[1024,128]{1,0:T(8,128)}, f32[1024,128]{1,0:T(8,128)S(1)}, u32[]{:S(2)}, u32[]{:S(2)}) collective-permute-start(f32[1024,128]{1,0:T(8,128)} %bitcast.27), channel_id=1, source_target_pairs={{0,16},{1,17},{2,18},{3,19},{4,20},{5,21},{6,22},{7,23},{8,24},{9,... | collective-permute-start | bytes 1572872 | tf_op jit(solution)/shard_map/ppermute | solution.py:354
  3.7 11.1 %copy-start.5 = (f32[6,64,16]{1,2,0:T(8,128)S(1)}, f32[6,64,16]{1,2,0:T(8,128)}, u32[]{:S(2)}) copy-start(f32[6,64,16]{1,2,0:T(8,128)} %param.9) | copy-start | bytes 73732
  3.9 1.0 copy-start.1
  4.9 1.0 copy-start.3
  6.0 9.9 %copy-start = (f32[1,64,4,4,128]{4,3,2,1,0:T(4,128)S(1)}, f32[1,64,4,4,128]{4,3,2,1,0:T(4,128)}, u32[]{:S(2)}) copy-start(f32[1,64,4,4,128]{4,3,2,1,0:T(4,128)} %param.6) | copy-start | bytes 1572868
  6.0 9.9 %copy-start.4 = (f32[64,4,4,128]{3,2,1,0:T(4,128)S(1)}, f32[64,4,4,128]{3,2,1,0:T(4,128)}, u32[]{:S(2)}) copy-start(f32[64,4,4,128]{3,2,1,0:T(4,128)} %param.7) | copy-start | bytes 1572868
  6.1 9.6 %collective-permute-start.1 = (f32[4,16,128]{2,1,0:T(8,128)S(1)}, f32[4,16,128]{2,1,0:T(8,128)S(1)}, u32[]{:S(2)}, u32[]{:S(2)}) collective-permute-start(f32[4,16,128]{2,1,0:T(8,128)S(1)} %get-tuple-element.48), channel_id=1, source_target_pairs={{0,20},{1,21},{2,22},{3,23},{4,24},{5,25},{6,26},{7,27},{8,28},{9,... | collective-permute-start | bytes 98312 | tf_op jit(solution)/shard_map/ppermute | solution.py:354
  7.1 8.6 %collective-permute-start.2 = (f32[4,16,128]{2,1,0:T(8,128)S(1)}, f32[4,16,128]{2,1,0:T(8,128)S(1)}, u32[]{:S(2)}, u32[]{:S(2)}) collective-permute-start(f32[4,16,128]{2,1,0:T(8,128)S(1)} %get-tuple-element.49), channel_id=1, source_target_pairs={{0,28},{1,29},{2,30},{3,31},{4,16},{5,17},{6,18},{7,19},{8,20},{9,... | collective-permute-start | bytes 98312 | tf_op jit(solution)/shard_map/ppermute | solution.py:354
  10.5 5.3 %collective-permute-start.3 = (f32[4,16,128]{2,1,0:T(8,128)S(1)}, f32[4,16,128]{2,1,0:T(8,128)S(1)}, u32[]{:S(2)}, u32[]{:S(2)}) collective-permute-start(f32[4,16,128]{2,1,0:T(8,128)S(1)} %get-tuple-element.50), channel_id=1, source_target_pairs={{0,17},{1,18},{2,19},{3,16},{4,21},{5,22},{6,23},{7,20},{8,25},{9,... | collective-permute-start | bytes 98312 | tf_op jit(solution)/shard_map/ppermute | solution.py:354
  11.7 4.1 %collective-permute-start.4 = (f32[4,16,128]{2,1,0:T(8,128)S(1)}, f32[4,16,128]{2,1,0:T(8,128)S(1)}, u32[]{:S(2)}, u32[]{:S(2)}) collective-permute-start(f32[4,16,128]{2,1,0:T(8,128)S(1)} %get-tuple-element.51), channel_id=1, source_target_pairs={{0,19},{1,16},{2,17},{3,18},{4,23},{5,20},{6,21},{7,22},{8,27},{9,... | collective-permute-start | bytes 98312 | tf_op jit(solution)/shard_map/ppermute | solution.py:354
  14.8 0.8 copy-start.6
  16.8 5.4 %collective-permute-start.5 = (f32[4,16,128]{2,1,0:T(8,128)S(1)}, f32[4,16,128]{2,1,0:T(8,128)S(1)}, u32[]{:S(2)}, u32[]{:S(2)}) collective-permute-start(f32[4,16,128]{2,1,0:T(8,128)S(1)} %get-tuple-element.53), channel_id=1, source_target_pairs={{0,4},{1,5},{2,6},{3,7},{4,8},{5,9},{6,10},{7,11},{8,12},{9,13},{1... | collective-permute-start | bytes 98312 | tf_op jit(solution)/shard_map/ppermute | solution.py:354
  16.9 5.3 %collective-permute-start.6 = (f32[4,16,128]{2,1,0:T(8,128)S(1)}, f32[4,16,128]{2,1,0:T(8,128)S(1)}, u32[]{:S(2)}, u32[]{:S(2)}) collective-permute-start(f32[4,16,128]{2,1,0:T(8,128)S(1)} %get-tuple-element.54), channel_id=1, source_target_pairs={{0,12},{1,13},{2,14},{3,15},{4,0},{5,1},{6,2},{7,3},{8,4},{9,5},{1... | collective-permute-start | bytes 98312 | tf_op jit(solution)/shard_map/ppermute | solution.py:354
  19.5 4.3 %collective-permute-start.7 = (f32[4,16,128]{2,1,0:T(8,128)S(1)}, f32[4,16,128]{2,1,0:T(8,128)S(1)}, u32[]{:S(2)}, u32[]{:S(2)}) collective-permute-start(f32[4,16,128]{2,1,0:T(8,128)S(1)} %get-tuple-element.55), channel_id=1, source_target_pairs={{0,1},{1,2},{2,3},{3,0},{4,5},{5,6},{6,7},{7,4},{8,9},{9,10},{10,1... | collective-permute-start | bytes 98312 | tf_op jit(solution)/shard_map/ppermute | solution.py:354
  20.3 3.5 %collective-permute-start.8 = (f32[4,16,128]{2,1,0:T(8,128)S(1)}, f32[4,16,128]{2,1,0:T(8,128)S(1)}, u32[]{:S(2)}, u32[]{:S(2)}) collective-permute-start(f32[4,16,128]{2,1,0:T(8,128)S(1)} %get-tuple-element.56), channel_id=1, source_target_pairs={{0,3},{1,0},{2,1},{3,2},{4,7},{5,4},{6,5},{7,6},{8,11},{9,8},{10,9... | collective-permute-start | bytes 98312 | tf_op jit(solution)/shard_map/ppermute | solution.py:354
  24.4 5.4 %collective-permute-start.9 = (f32[4,16,128]{2,1,0:T(8,128)S(1)}, f32[4,16,128]{2,1,0:T(8,128)S(1)}, u32[]{:S(2)}, u32[]{:S(2)}) collective-permute-start(f32[4,16,128]{2,1,0:T(8,128)S(1)} %get-tuple-element.58), channel_id=1, source_target_pairs={{0,4},{1,5},{2,6},{3,7},{4,8},{5,9},{6,10},{7,11},{8,12},{9,13},{1... | collective-permute-start | bytes 98312 | tf_op jit(solution)/shard_map/ppermute | solution.py:354
  24.5 5.3 %collective-permute-start.10 = (f32[4,16,128]{2,1,0:T(8,128)S(1)}, f32[4,16,128]{2,1,0:T(8,128)S(1)}, u32[]{:S(2)}, u32[]{:S(2)}) collective-permute-start(f32[4,16,128]{2,1,0:T(8,128)S(1)} %get-tuple-element.59), channel_id=1, source_target_pairs={{0,12},{1,13},{2,14},{3,15},{4,0},{5,1},{6,2},{7,3},{8,4},{9,5},{1... | collective-permute-start | bytes 98312 | tf_op jit(solution)/shard_map/ppermute | solution.py:354
  27.2 4.0 %collective-permute-start.11 = (f32[4,16,128]{2,1,0:T(8,128)S(1)}, f32[4,16,128]{2,1,0:T(8,128)S(1)}, u32[]{:S(2)}, u32[]{:S(2)}) collective-permute-start(f32[4,16,128]{2,1,0:T(8,128)S(1)} %get-tuple-element.60), channel_id=1, source_target_pairs={{0,1},{1,2},{2,3},{3,0},{4,5},{5,6},{6,7},{7,4},{8,9},{9,10},{10,1... | collective-permute-start | bytes 98312 | tf_op jit(solution)/shard_map/ppermute | solution.py:354
  27.8 3.4 %collective-permute-start.12 = (f32[4,16,128]{2,1,0:T(8,128)S(1)}, f32[4,16,128]{2,1,0:T(8,128)S(1)}, u32[]{:S(2)}, u32[]{:S(2)}) collective-permute-start(f32[4,16,128]{2,1,0:T(8,128)S(1)} %get-tuple-element.61), channel_id=1, source_target_pairs={{0,3},{1,0},{2,1},{3,2},{4,7},{5,4},{6,5},{7,6},{8,11},{9,8},{10,9... | collective-permute-start | bytes 98312 | tf_op jit(solution)/shard_map/ppermute | solution.py:354
  31.2 7.5 %copy-start.2 = (f32[1,64,4,4,128]{4,3,2,1,0:T(4,128)S(1)}, f32[1,64,4,4,128]{4,3,2,1,0:T(4,128)}, u32[]{:S(2)}) copy-start(f32[1,64,4,4,128]{4,3,2,1,0:T(4,128)} %param.5) | copy-start | bytes 1572868
  31.8 5.6 %collective-permute-start.13 = (f32[4,16,128]{2,1,0:T(8,128)S(1)}, f32[4,16,128]{2,1,0:T(8,128)S(1)}, u32[]{:S(2)}, u32[]{:S(2)}) collective-permute-start(f32[4,16,128]{2,1,0:T(8,128)S(1)} %get-tuple-element.63), channel_id=1, source_target_pairs={{0,4},{1,5},{2,6},{3,7},{4,8},{5,9},{6,10},{7,11},{8,12},{9,13},{1... | collective-permute-start | bytes 98312 | tf_op jit(solution)/shard_map/ppermute | solution.py:354
  32.1 5.3 %collective-permute-start.14 = (f32[4,16,128]{2,1,0:T(8,128)S(1)}, f32[4,16,128]{2,1,0:T(8,128)S(1)}, u32[]{:S(2)}, u32[]{:S(2)}) collective-permute-start(f32[4,16,128]{2,1,0:T(8,128)S(1)} %get-tuple-element.64), channel_id=1, source_target_pairs={{0,12},{1,13},{2,14},{3,15},{4,0},{5,1},{6,2},{7,3},{8,4},{9,5},{1... | collective-permute-start | bytes 98312 | tf_op jit(solution)/shard_map/ppermute | solution.py:354
  34.7 4.0 %collective-permute-start.15 = (f32[4,16,128]{2,1,0:T(8,128)S(1)}, f32[4,16,128]{2,1,0:T(8,128)S(1)}, u32[]{:S(2)}, u32[]{:S(2)}) collective-permute-start(f32[4,16,128]{2,1,0:T(8,128)S(1)} %get-tuple-element.65), channel_id=1, source_target_pairs={{0,1},{1,2},{2,3},{3,0},{4,5},{5,6},{6,7},{7,4},{8,9},{9,10},{10,1... | collective-permute-start | bytes 98312 | tf_op jit(solution)/shard_map/ppermute | solution.py:354
  35.4 3.3 %collective-permute-start.16 = (f32[4,16,128]{2,1,0:T(8,128)S(1)}, f32[4,16,128]{2,1,0:T(8,128)S(1)}, u32[]{:S(2)}, u32[]{:S(2)}) collective-permute-start(f32[4,16,128]{2,1,0:T(8,128)S(1)} %get-tuple-element.66), channel_id=1, source_target_pairs={{0,3},{1,0},{2,1},{3,2},{4,7},{5,4},{6,5},{7,6},{8,11},{9,8},{10,9... | collective-permute-start | bytes 98312 | tf_op jit(solution)/shard_map/ppermute | solution.py:354
  64.2 3.0 %collective-permute-start.17 = (f32[2,144,128]{2,1,0:T(8,128)S(1)}, f32[2,144,128]{2,1,0:T(8,128)S(1)}, u32[]{:S(2)}, u32[]{:S(2)}) collective-permute-start(f32[2,144,128]{2,1,0:T(8,128)S(1)} %get-tuple-element.69), channel_id=1, source_target_pairs={{0,16},{16,1},{1,17},{17,2},{2,18},{18,3},{3,19},{19,7},{7,23},{23... | collective-permute-start | bytes 442376 | tf_op jit(solution)/shard_map/ppermute | solution.py:354
  65.0 4.6 %collective-permute-start.18 = (f32[2,144,128]{2,1,0:T(8,128)S(1)}, f32[2,144,128]{2,1,0:T(8,128)S(1)}, u32[]{:S(2)}, u32[]{:S(2)}) collective-permute-start(f32[2,144,128]{2,1,0:T(8,128)S(1)} %get-tuple-element.70), channel_id=1, source_target_pairs={{0,48},{16,0},{1,16},{17,1},{2,17},{18,2},{3,18},{19,3},{7,19},{23... | collective-permute-start | bytes 442376 | tf_op jit(solution)/shard_map/ppermute | solution.py:354
  70.3 1.3 collective-permute-start.19
  70.4 3.2 %collective-permute-start.20 = (f32[2,16,128]{2,1,0:T(8,128)S(1)}, f32[2,16,128]{2,1,0:T(8,128)S(1)}, u32[]{:S(2)}, u32[]{:S(2)}) collective-permute-start(f32[2,16,128]{2,1,0:T(8,128)S(1)} %get-tuple-element.73), channel_id=1, source_target_pairs={{0,48},{16,0},{1,16},{17,1},{2,17},{18,2},{3,18},{19,3},{7,19},{23... | collective-permute-start | bytes 49160 | tf_op jit(solution)/shard_map/ppermute | solution.py:354
  73.9 7.3 %collective-permute-start.22 = (f32[4,64,128]{2,1,0:T(8,128)S(1)}, f32[4,64,128]{2,1,0:T(8,128)S(1)}, u32[]{:S(2)}, u32[]{:S(2)}) collective-permute-start(f32[4,64,128]{2,1,0:T(8,128)S(1)} %shard_map.76.e3), channel_id=1, source_target_pairs={{0,64},{16,80},{1,65},{17,81},{2,66},{18,82},{3,67},{19,83},{7,71}... | collective-permute-start | bytes 393224 | tf_op jit(solution)/shard_map/ppermute | solution.py:354
  77.3 7.5 %collective-permute-start.21 = (f32[4,64,128]{2,1,0:T(8,128)S(1)}, f32[4,64,128]{2,1,0:T(8,128)S(1)}, u32[]{:S(2)}, u32[]{:S(2)}) collective-permute-start(f32[4,64,128]{2,1,0:T(8,128)S(1)} %shard_map.76.e3), channel_id=1, source_target_pairs={{0,192},{16,208},{1,193},{17,209},{2,194},{18,210},{3,195},{19,211... | collective-permute-start | bytes 393224 | tf_op jit(solution)/shard_map/ppermute | solution.py:354
  84.8 6.1 %collective-permute-start.23 = (f32[2,80,128]{2,1,0:T(8,128)S(1)}, f32[2,80,128]{2,1,0:T(8,128)S(1)}, u32[]{:S(2)}, u32[]{:S(2)}) collective-permute-start(f32[2,80,128]{2,1,0:T(8,128)S(1)} %get-tuple-element.75), channel_id=1, source_target_pairs={{0,16},{16,1},{1,17},{17,2},{2,18},{18,3},{3,19},{19,7},{7,23},{23... | collective-permute-start | bytes 245768 | tf_op jit(solution)/shard_map/ppermute | solution.py:354
  87.8 3.9 %collective-permute-start.24 = (f32[2,80,128]{2,1,0:T(8,128)S(1)}, f32[2,80,128]{2,1,0:T(8,128)S(1)}, u32[]{:S(2)}, u32[]{:S(2)}) collective-permute-start(f32[2,80,128]{2,1,0:T(8,128)S(1)} %get-tuple-element.76), channel_id=1, source_target_pairs={{0,48},{16,0},{1,16},{17,1},{2,17},{18,2},{3,18},{19,3},{7,19},{23... | collective-permute-start | bytes 245768 | tf_op jit(solution)/shard_map/ppermute | solution.py:354
  87.8 10.0 %collective-permute-start.27 = (f32[4,64,128]{2,1,0:T(8,128)S(1)}, f32[4,64,128]{2,1,0:T(8,128)S(1)}, u32[]{:S(2)}, u32[]{:S(2)}) collective-permute-start(f32[4,64,128]{2,1,0:T(8,128)S(1)} %collective-permute-done.22.waited.add), channel_id=1, source_target_pairs={{0,64},{16,80},{1,65},{17,81},{2,66},{18,82},{3,67},{19,83},{7,71}... | collective-permute-start | bytes 393224 | tf_op jit(solution)/shard_map/ppermute | solution.py:354
  92.3 5.5 %collective-permute-start.25 = (f32[2,80,128]{2,1,0:T(8,128)S(1)}, f32[2,80,128]{2,1,0:T(8,128)S(1)}, u32[]{:S(2)}, u32[]{:S(2)}) collective-permute-start(f32[2,80,128]{2,1,0:T(8,128)S(1)} %get-tuple-element.78), channel_id=1, source_target_pairs={{0,16},{16,1},{1,17},{17,2},{2,18},{18,3},{3,19},{19,7},{7,23},{23... | collective-permute-start | bytes 245768 | tf_op jit(solution)/shard_map/ppermute | solution.py:354
  93.9 4.1 %collective-permute-start.26 = (f32[2,80,128]{2,1,0:T(8,128)S(1)}, f32[2,80,128]{2,1,0:T(8,128)S(1)}, u32[]{:S(2)}, u32[]{:S(2)}) collective-permute-start(f32[2,80,128]{2,1,0:T(8,128)S(1)} %get-tuple-element.79), channel_id=1, source_target_pairs={{0,48},{16,0},{1,16},{17,1},{2,17},{18,2},{3,18},{19,3},{7,19},{23... | collective-permute-start | bytes 245768 | tf_op jit(solution)/shard_map/ppermute | solution.py:354
  98.6 2.4 %collective-permute-start.28 = (f32[2,80,128]{2,1,0:T(8,128)S(1)}, f32[2,80,128]{2,1,0:T(8,128)S(1)}, u32[]{:S(2)}, u32[]{:S(2)}) collective-permute-start(f32[2,80,128]{2,1,0:T(8,128)S(1)} %get-tuple-element.81), channel_id=1, source_target_pairs={{0,16},{16,1},{1,17},{17,2},{2,18},{18,3},{3,19},{19,7},{7,23},{23... | collective-permute-start | bytes 245768 | tf_op jit(solution)/shard_map/ppermute | solution.py:354
  99.6 3.9 %collective-permute-start.29 = (f32[2,80,128]{2,1,0:T(8,128)S(1)}, f32[2,80,128]{2,1,0:T(8,128)S(1)}, u32[]{:S(2)}, u32[]{:S(2)}) collective-permute-start(f32[2,80,128]{2,1,0:T(8,128)S(1)} %get-tuple-element.82), channel_id=1, source_target_pairs={{0,48},{16,0},{1,16},{17,1},{2,17},{18,2},{3,18},{19,3},{7,19},{23... | collective-permute-start | bytes 245768 | tf_op jit(solution)/shard_map/ppermute | solution.py:354
  104.1 1.6 %collective-permute-start.30 = (f32[2,80,128]{2,1,0:T(8,128)S(1)}, f32[2,80,128]{2,1,0:T(8,128)S(1)}, u32[]{:S(2)}, u32[]{:S(2)}) collective-permute-start(f32[2,80,128]{2,1,0:T(8,128)S(1)} %get-tuple-element.84), channel_id=1, source_target_pairs={{0,16},{16,1},{1,17},{17,2},{2,18},{18,3},{3,19},{19,7},{7,23},{23... | collective-permute-start | bytes 245768 | tf_op jit(solution)/shard_map/ppermute | solution.py:354
  104.2 3.9 %collective-permute-start.31 = (f32[2,80,128]{2,1,0:T(8,128)S(1)}, f32[2,80,128]{2,1,0:T(8,128)S(1)}, u32[]{:S(2)}, u32[]{:S(2)}) collective-permute-start(f32[2,80,128]{2,1,0:T(8,128)S(1)} %get-tuple-element.85), channel_id=1, source_target_pairs={{0,48},{16,0},{1,16},{17,1},{2,17},{18,2},{3,18},{19,3},{7,19},{23... | collective-permute-start | bytes 245768 | tf_op jit(solution)/shard_map/ppermute | solution.py:354
  108.8 1.6 %collective-permute-start.32 = (f32[2,80,128]{2,1,0:T(8,128)S(1)}, f32[2,80,128]{2,1,0:T(8,128)S(1)}, u32[]{:S(2)}, u32[]{:S(2)}) collective-permute-start(f32[2,80,128]{2,1,0:T(8,128)S(1)} %get-tuple-element.87), channel_id=1, source_target_pairs={{0,16},{16,1},{1,17},{17,2},{2,18},{18,3},{3,19},{19,7},{7,23},{23... | collective-permute-start | bytes 245768 | tf_op jit(solution)/shard_map/ppermute | solution.py:354
  108.9 3.9 %collective-permute-start.33 = (f32[2,80,128]{2,1,0:T(8,128)S(1)}, f32[2,80,128]{2,1,0:T(8,128)S(1)}, u32[]{:S(2)}, u32[]{:S(2)}) collective-permute-start(f32[2,80,128]{2,1,0:T(8,128)S(1)} %get-tuple-element.88), channel_id=1, source_target_pairs={{0,48},{16,0},{1,16},{17,1},{2,17},{18,2},{3,18},{19,3},{7,19},{23... | collective-permute-start | bytes 245768 | tf_op jit(solution)/shard_map/ppermute | solution.py:354
  113.5 1.6 %collective-permute-start.34 = (f32[2,80,128]{2,1,0:T(8,128)S(1)}, f32[2,80,128]{2,1,0:T(8,128)S(1)}, u32[]{:S(2)}, u32[]{:S(2)}) collective-permute-start(f32[2,80,128]{2,1,0:T(8,128)S(1)} %get-tuple-element.90), channel_id=1, source_target_pairs={{0,16},{16,1},{1,17},{17,2},{2,18},{18,3},{3,19},{19,7},{7,23},{23... | collective-permute-start | bytes 245768 | tf_op jit(solution)/shard_map/ppermute | solution.py:354
  113.6 3.9 %collective-permute-start.35 = (f32[2,80,128]{2,1,0:T(8,128)S(1)}, f32[2,80,128]{2,1,0:T(8,128)S(1)}, u32[]{:S(2)}, u32[]{:S(2)}) collective-permute-start(f32[2,80,128]{2,1,0:T(8,128)S(1)} %get-tuple-element.91), channel_id=1, source_target_pairs={{0,48},{16,0},{1,16},{17,1},{2,17},{18,2},{3,18},{19,3},{7,19},{23... | collective-permute-start | bytes 245768 | tf_op jit(solution)/shard_map/ppermute | solution.py:354

commit v2 on v1

--- a/solution.py
+++ b/solution.py
@@ -12,7 +12,7 @@
 VM = pl.BlockSpec(memory_space=pltpu.VMEM)
 ANY = pl.BlockSpec(memory_space=pl.ANY)
 PARAMS = pltpu.CompilerParams(vmem_limit_bytes=40 << 20)
-XB, XA, YB, YA, ZB, ZA, FROM_1, FROM_2, FROM_3, FIRST, LAST = range(11)
+XB, XA, YB, YA, ZB, ZA, FROM_1, FROM_2, FROM_3, FIRST, LAST, EX, EY, EZ = range(14)
 
 
 def ring_of_slabs():
@@ -27,14 +27,42 @@
 SLAB = [DEVICE.index(d) for d in range(64)]
 
 
-def call(kernel, out, flops, nbytes, scratch=(), specs=None):
+def call(kernel, out, flops, nbytes, scratch=(), specs=None, ins=(), outs=()):
     def run(*args):
+        extra = [pltpu.VMEM(args[i].shape, F32) for i, j, _ in ins for _ in range(2)]
+        extra += [pltpu.VMEM(out[i][0], F32) for i, j, _ in outs for _ in range(2)]
+
+        def body(*refs):
+            inner = list(refs[: len(args)])
+            outer = list(refs[len(args) : len(args) + len(out)])
+            own = refs[len(args) + len(out) : len(args) + len(out) + len(scratch)]
+            spare = list(refs[len(args) + len(out) + len(scratch) :])
+            flags = inner[0]
+            sent = []
+            for i, j, row in ins:
+                first, second = inner[i], inner[j]
+                inner[i], inner[j] = spare.pop(0), spare.pop(0)
+                even = flags[row : row + 1, :] > 0.5
+                for t in range(first.shape[0]):
+                    inner[i][t] = jnp.where(even, second[t], first[t])
+                    inner[j][t] = jnp.where(even, first[t], second[t])
+            for i, j, row in outs:
+                up, down = spare.pop(0), spare.pop(0)
+                sent.append((outer[i], outer[j], up, down, row))
+                outer[i], outer[j] = up, down
+            kernel(*inner, *outer, *own)
+            for first, second, up, down, row in sent:
+                even = flags[row : row + 1, :] > 0.5
+                for t in range(first.shape[0]):
+                    first[t] = jnp.where(even, up[t], down[t])
+                    second[t] = jnp.where(even, down[t], up[t])
+
         return pl.pallas_call(
-            kernel,
+            body,
             out_shape=[jax.ShapeDtypeStruct(s, d) for s, d in out],
             in_specs=specs or [VM] * len(args),
             out_specs=[VM] * len(out),
-            scratch_shapes=list(scratch),
+            scratch_shapes=list(scratch) + extra,
             compiler_params=PARAMS,
             cost_estimate=pl.CostEstimate(flops=flops, bytes_accessed=nbytes, transcendentals=0),
         )(*args)
@@ -249,7 +277,7 @@
     return result
 
 
-def local_first_kernel(received, r, up, down):
+def local_first_kernel(flags, received, r, up, down):
     for q in range(8):
         at = [SLAB[q // 2 * 16 + s] * 16 + 8 * (q % 2) for s in range(16)]
         block = jnp.concatenate([received[a : a + 8, :] for a in at], 0).T
@@ -333,13 +361,38 @@
     return (t * 4 + x) * 4 + y
 
 
-def ring(dt, dx, dy):
+def partner(v, first, size):
+    return (v + 1) % size if (v - first) % 2 == 0 else (v - 1) % size
+
+
+def swap_x(dt, first):
     return [
-        (index_of(t, x, y), index_of((t + dt) % 16, (x + dx) % 4, (y + dy) % 4))
+        (index_of(t, x, y), index_of((t + dt) % 16, partner(x, first, 4), y))
         for t in range(16)
         for x in range(4)
         for y in range(4)
     ]
+
+
+def swap_y(dt, first):
+    return [
+        (index_of(t, x, y), index_of((t + dt) % 16, x, partner(y, first, 4)))
+        for t in range(16)
+        for x in range(4)
+        for y in range(4)
+    ]
+
+
+def swap_slabs(first):
+    return [
+        (64 * g + DEVICE[s], 64 * g + DEVICE[partner(s, first, 64)])
+        for g in range(4)
+        for s in range(64)
+    ]
+
+
+def later():
+    return [(d, (d + 16) % 256) for d in range(256)]
 
 
 def slab_ring(ds, dg=0):
@@ -362,8 +415,9 @@
     flags = jnp.stack(
         [sx > 0, sx < 3, sy > 0, sy < 3, ~(corner & (tj == 0)), ~(corner & (tj == 3))]
         + [tg >= 1, tg >= 2, tg >= 3, tm == 0, tm == 15]
+        + [sx % 2 == 0, sy % 2 == 0, tj % 2 == 0]
     ).astype(F32)
-    flags = jnp.broadcast_to(flags[:, None], (11, 128))
+    flags = jnp.broadcast_to(flags[:, None], (14, 128))
     lift_flat = jnp.transpose(lift, (1, 0, 2)).reshape(64, 96)
     w = jnp.concatenate([volume, lift_flat], 1)
     face, wide, trace = ((4, 16, 128), F32), ((2, 80, 128), F32), ((2, 16, 128), F32)
@@ -374,19 +428,23 @@
     source = forcing.reshape(1024, 128)
     start = initial.reshape(1024, 128)
     block = pltpu.VMEM((16, 64, 128), F32)
-    faces = call(faces_kernel, [face] * 4, 0, 1 << 19, [block])(flags, start, state)
+    faces = call(faces_kernel, [face] * 4, 0, 1 << 19, [block], outs=[(0, 1, EX), (2, 3, EY)])(flags, start, state)
     fine_cost = (2 * 64 * 480 * 2048, 3 << 19)
-    v = send(state, ring(1, 0, 0))
-    hops = (ring(1, 1, 0), ring(1, -1, 0), ring(1, 0, 1), ring(1, 0, -1))
+    v = send(state, later())
+    hops = (swap_x(1, 0), swap_x(1, 1), swap_y(1, 0), swap_y(1, 1))
+    sides = [(3, 4, EX), (5, 6, EY)]
     for step in range(3):
         xb, xa, yb, ya = [send(f, pairs) for f, pairs in zip(faces, hops)]
         kernel, held, more = (fine_kernel, [], []) if step else (first_fine_kernel, [block], [start])
-        v, *faces = call(kernel, [whole] + [face] * 4, *fine_cost, held)(
+        v, *faces = call(
+            kernel, [whole] + [face] * 4, *fine_cost, held,
+            ins=sides, outs=[(1, 2, EX), (3, 4, EY)],
+        )(
             flags, v, source, xb, xa, yb, ya, w, *more
         )
-        hops = (ring(0, 1, 0), ring(0, -1, 0), ring(0, 0, 1), ring(0, 0, -1))
+        hops = (swap_x(0, 0), swap_x(0, 1), swap_y(0, 0), swap_y(0, 1))
     xb, xa, yb, ya = [send(f, pairs) for f, pairs in zip(faces, hops)]
-    resid, packed = call(residual_kernel, [rows, rows], *fine_cost, [block])(
+    resid, packed = call(residual_kernel, [rows, rows], *fine_cost, [block], ins=sides)(
         flags, v, source, xb, xa, yb, ya, w, state
     )
 
@@ -397,37 +455,43 @@
 
     received = traded(packed)
 
-    up_ring, down_ring = slab_ring(1), slab_ring(-1)
+    first_swap, second_swap = swap_slabs(0), swap_slabs(1)
+    halo_in, halo_out = [(2, 3, EZ)], [(1, 2, EZ)]
 
     def exchange(pair):
-        up, down = pair
-        return send(up, up_ring), send(down, down_ring)
+        first, second = pair
+        return send(first, first_swap), send(second, second_swap)
 
     pair_cost = (2 * 64 * 480 * 1536, 1 << 19)
     scratch = [pltpu.VMEM((8, 64, 128), F32), pltpu.VMEM((8, 64, 128), F32)]
     r, *pair = call(
-        local_first_kernel, [whole] + [((2, 144, 128), F32)] * 2, 0, 1 << 20
-    )(received)
-    e, *pair = call(local_pair_kernel, [((12, 64, 128), F32), trace, trace], *pair_cost, scratch)(
+        local_first_kernel, [whole] + [((2, 144, 128), F32)] * 2, 0, 1 << 20, outs=halo_out
+    )(flags, received)
+    e, *pair = call(
+        local_pair_kernel, [((12, 64, 128), F32), trace, trace], *pair_cost, scratch,
+        ins=halo_in, outs=halo_out,
+    )(
         flags, r, *exchange(pair), w
     )
-    (e3,) = call(local_last_kernel, [two], *pair_cost)(flags, e, r, *exchange(pair), w)
+    (e3,) = call(local_last_kernel, [two], *pair_cost, ins=[(3, 4, EZ)])(flags, e, r, *exchange(pair), w)
     from_3 = send(e3, slab_ring(0, 3))
     from_1 = send(e3, slab_ring(0, 1))
-    chain = call(chain_kernel, [two, wide, wide], *pair_cost, scratch)
-    begin = call(begin_kernel, [two, wide, wide], 0, 1 << 18, (), [VM, VM, ANY])
+    halos = dict(ins=halo_in, outs=halo_out)
+    chain = call(chain_kernel, [two, wide, wide], *pair_cost, scratch, **halos)
+    begin = call(begin_kernel, [two, wide, wide], 0, 1 << 18, (), [VM, VM, ANY], outs=halo_out)
     x, *pair = begin(flags, from_3, from_1)
     from_2 = send(from_1, slab_ring(0, 1))
     for which, add in ((FROM_2, from_2), (FROM_1, from_1)):
         x, *pair = chain(flags, x, *exchange(pair), w)
         kernel = functools.partial(chain_add_kernel, which)
-        x, *pair = call(kernel, [two, wide, wide], *pair_cost, scratch)(
+        x, *pair = call(kernel, [two, wide, wide], *pair_cost, scratch, **halos)(
             flags, x, *exchange(pair), w, add
         )
     head, x, *pair = call(
-        last_first_kernel, [((8, 64, 128), F32), two, wide, wide], *pair_cost, scratch
+        last_first_kernel, [((8, 64, 128), F32), two, wide, wide], *pair_cost, scratch,
+        ins=halo_in, outs=[(2, 3, EZ)],
     )(flags, x, *exchange(pair), w, e)
-    (packed,) = call(last_second_kernel, [rows], *pair_cost, scratch)(
+    (packed,) = call(last_second_kernel, [rows], *pair_cost, scratch, ins=halo_in)(
         flags, x, *exchange(pair), w, e, e3, head
     )
     received = traded(packed)

time: 136 us -> 135 us (level)
  starting transfers between devices: 43.8 us -> 37.3 us
  waiting for transfers between devices: 37.6 us -> 41.5 us
  blocking collectives: 39.8 us -> 41.3 us
    ppermute x36, starting transfers between devices: 43.8 us -> 37.3 us  [send(): return lax.ppermute(value, AXES, pairs)]
    ppermute x36, waiting for transfers between devices: 37.6 us -> 41.5 us  [send(): return lax.ppermute(value, AXES, pairs)]
    all_to_all x2, blocking collectives: 39.8 us -> 41.3 us  [traded(): lax.all_to_all(value, AXES, 0, 0, axis_index_groups=peers, tiled=True)]
  transfers between devices with their start and end apart: 36 -> 36, of which waited for: 21 -> 25; matrix products, arithmetic and copies ran while one was open for 0% -> 0% of each run, Pallas kernels for 1% -> 1%
where the time goes in v2:
time: 135 us
  waiting for transfers between devices  41.5 us (31%)
  blocking collectives  41.3 us (31%)
  starting transfers between devices  37.3 us (28%)
  Pallas kernels  10.5 us (8%)
  local copies, waits for them, and re-layouts  3.04 us (2%)
    ppermute x36, waiting for transfers between devices, send(): return lax.ppermute(value, AXES, pairs)  41.5 us
    all_to_all x2, blocking collectives, traded(): lax.all_to_all(value, AXES, 0, 0, axis_index_groups=peers, tiled=True)  41.3 us
    ppermute x36, starting transfers between devices, send(): return lax.ppermute(value, AXES, pairs)  37.3 us
    pallas_call x17, Pallas kernels, run(): pl.pallas_call(body, out_shape=[jax.ShapeDtypeStruct(s, d) for s, d in ou...  10.5 us
    unnamed x14, local copies, waits for them, and re-layouts  2.8 us
  transfers between devices with their start and end apart: 36, of which 25 were waited for; matrix products, arithmetic and copies ran while one was open for 0% of the time, Pallas kernels for 1%

profile of v2, /device:TPU:1, one launch (start us, length us, event | category | flops | bytes accessed | tf_op | source)
XLA Modules:
  0.0 134.5 jit_solution(15465909733496445496)
XLA Ops:
  0.6 3.0 %collective-permute-start = (f32[1024,128]{1,0:T(8,128)}, f32[1024,128]{1,0:T(8,128)S(1)}, u32[]{:S(2)}, u32[]{:S(2)}) collective-permute-start(f32[1024,128]{1,0:T(8,128)} %bitcast.30), channel_id=1, source_target_pairs={{0,16},{1,17},{2,18},{3,19},{4,20},{5,21},{6,22},{7,23},{8,24},{9,... | collective-permute-start | bytes 1572872 | tf_op jit(solution)/shard_map/ppermute | solution.py:407
  3.9 1.0 copy-done.1
  4.9 1.0 copy-done.3
  6.1 1.1 collective-permute-start.1
  7.2 3.6 %collective-permute-start.2 = (f32[4,16,128]{2,1,0:T(8,128)S(1)}, f32[4,16,128]{2,1,0:T(8,128)S(1)}, u32[]{:S(2)}, u32[]{:S(2)}) collective-permute-start(f32[4,16,128]{2,1,0:T(8,128)S(1)} %get-tuple-element.49), channel_id=1, source_target_pairs={{0,28},{1,29},{2,30},{3,31},{4,24},{5,25},{6,26},{7,27},{8,20},{9,... | collective-permute-start | bytes 98312 | tf_op jit(solution)/shard_map/ppermute | solution.py:407
  10.8 1.1 collective-permute-start.3
  11.9 3.7 %collective-permute-start.4 = (f32[4,16,128]{2,1,0:T(8,128)S(1)}, f32[4,16,128]{2,1,0:T(8,128)S(1)}, u32[]{:S(2)}, u32[]{:S(2)}) collective-permute-start(f32[4,16,128]{2,1,0:T(8,128)S(1)} %get-tuple-element.51), channel_id=1, source_target_pairs={{0,19},{1,18},{2,17},{3,16},{4,23},{5,22},{6,21},{7,20},{8,27},{9,... | collective-permute-start | bytes 98312 | tf_op jit(solution)/shard_map/ppermute | solution.py:407
  15.7 0.7 copy-done.6
  16.8 1.0 shard_map.70
  17.8 0.4 collective-permute-start.5
  18.2 0.8 collective-permute-start.6
  19.1 1.8 %collective-permute-start.8 = (f32[4,16,128]{2,1,0:T(8,128)S(1)}, f32[4,16,128]{2,1,0:T(8,128)S(1)}, u32[]{:S(2)}, u32[]{:S(2)}) collective-permute-start(f32[4,16,128]{2,1,0:T(8,128)S(1)} %get-tuple-element.56), channel_id=1, source_target_pairs={{0,3},{1,2},{2,1},{3,0},{4,7},{5,6},{6,5},{7,4},{8,11},{9,10},{10,... | collective-permute-start | bytes 98312 | tf_op jit(solution)/shard_map/ppermute | solution.py:407
  20.9 1.3 collective-permute-done.6.refs_4_
  22.1 0.9 collective-permute-done.8.refs_6_
  23.1 0.6 shard_map.71
  23.7 0.8 collective-permute-start.9
  24.6 1.8 %collective-permute-start.10 = (f32[4,16,128]{2,1,0:T(8,128)S(1)}, f32[4,16,128]{2,1,0:T(8,128)S(1)}, u32[]{:S(2)}, u32[]{:S(2)}) collective-permute-start(f32[4,16,128]{2,1,0:T(8,128)S(1)} %get-tuple-element.59), channel_id=1, source_target_pairs={{0,12},{1,13},{2,14},{3,15},{4,8},{5,9},{6,10},{7,11},{8,4},{9,5},... | collective-permute-start | bytes 98312 | tf_op jit(solution)/shard_map/ppermute | solution.py:407
  26.6 1.4 %collective-permute-start.12 = (f32[4,16,128]{2,1,0:T(8,128)S(1)}, f32[4,16,128]{2,1,0:T(8,128)S(1)}, u32[]{:S(2)}, u32[]{:S(2)}) collective-permute-start(f32[4,16,128]{2,1,0:T(8,128)S(1)} %get-tuple-element.61), channel_id=1, source_target_pairs={{0,3},{1,2},{2,1},{3,0},{4,7},{5,6},{6,5},{7,4},{8,11},{9,10},{10,... | collective-permute-start | bytes 98312 | tf_op jit(solution)/shard_map/ppermute | solution.py:407
  28.0 0.6 collective-permute-done.10.refs_4_
  28.6 0.6 collective-permute-done.11.refs_5_
  29.2 1.4 %collective-permute-done.12.refs_6_ = f32[4,16,128]{2,1,0:T(8,128)S(1)} collective-permute-done((f32[4,16,128]{2,1,0:T(8,128)S(1)}, f32[4,16,128]{2,1,0:T(8,128)S(1)}, u32[]{:S(2)}, u32[]{:S(2)}) %collective-permute-start.12) | collective-permute-done | bytes 32800 | tf_op jit(solution)/shard_map/ppermute | solution.py:407
  30.6 0.6 shard_map.72
  31.2 0.4 collective-permute-start.13
  31.6 0.7 collective-permute-start.14
  32.3 2.0 %collective-permute-start.16 = (f32[4,16,128]{2,1,0:T(8,128)S(1)}, f32[4,16,128]{2,1,0:T(8,128)S(1)}, u32[]{:S(2)}, u32[]{:S(2)}) collective-permute-start(f32[4,16,128]{2,1,0:T(8,128)S(1)} %get-tuple-element.66), channel_id=1, source_target_pairs={{0,3},{1,2},{2,1},{3,0},{4,7},{5,6},{6,5},{7,4},{8,11},{9,10},{10,... | collective-permute-start | bytes 98312 | tf_op jit(solution)/shard_map/ppermute | solution.py:407
  34.4 1.2 collective-permute-done.14.refs_4_
  35.6 0.8 collective-permute-done.16.refs_6_
  36.4 1.7 %shard_map.73 = (f32[1024,128]{1,0:T(8,128)}, f32[1024,128]{1,0:T(8,128)S(1)}) custom-call(f32[14,128]{1,0:T(8,128)S(1)} %broadcast_in_dim.2.refs_0_, f32[16,64,128]{2,1,0:T(8,128)S(1)} %get-tuple-element.62.refs_1_, f32[1024,128]{1,0:T(8,128)S(1)} %bitcast.29, f32[4,16,128]{2,1,0:T(8,128)S(1)} %collective-permute-done.13.refs_3_, ...), custom_call_target="tpu_custom_call" | custom-call | flops 125829120 | bytes 1572864 | tf_op jit(solution)/shard_map/pallas_call | solution.py:60
  38.0 25.3 %all_to_all.22 = f32[64,16,128]{2,1,0:T(8,128)S(1)} all-to-all(f32[64,16,128]{2,1,0:T(8,128)S(1)} %bitcast.39), channel_id=1, replica_groups={{0,16,1,17,2,18,3,19,7,23,6,22,5,21,4,20,8,24,9,25,10,26,11,27,15,31,14..., dimensions={0} | all-to-all | bytes 1048576 | tf_op jit(solution)/shard_map/all_to_all | solution.py:454
  63.5 0.9 collective-permute-start.17
  64.6 0.9 collective-permute-done.17.refs_2_
  65.5 3.6 %collective-permute-done.18.refs_3_ = f32[2,144,128]{2,1,0:T(8,128)S(1)} collective-permute-done((f32[2,144,128]{2,1,0:T(8,128)S(1)}, f32[2,144,128]{2,1,0:T(8,128)S(1)}, u32[]{:S(2)}, u32[]{:S(2)}) %collective-permute-start.18) | collective-permute-done | bytes 147488 | tf_op jit(solution)/shard_map/ppermute | solution.py:407
  69.0 0.7 shard_map.75
  69.9 0.4 collective-permute-start.20
  70.2 0.7 collective-permute-done.19.refs_3_
  71.0 2.1 %collective-permute-done.20.refs_4_ = f32[2,16,128]{2,1,0:T(8,128)S(1)} collective-permute-done((f32[2,16,128]{2,1,0:T(8,128)S(1)}, f32[2,16,128]{2,1,0:T(8,128)S(1)}, u32[]{:S(2)}, u32[]{:S(2)}) %collective-permute-start.20) | collective-permute-done | bytes 16416 | tf_op jit(solution)/shard_map/ppermute | solution.py:407
  73.4 3.4 %collective-permute-start.22 = (f32[4,64,128]{2,1,0:T(8,128)S(1)}, f32[4,64,128]{2,1,0:T(8,128)S(1)}, u32[]{:S(2)}, u32[]{:S(2)}) collective-permute-start(f32[4,64,128]{2,1,0:T(8,128)S(1)} %shard_map.76.refs_6_), channel_id=1, source_target_pairs={{0,64},{16,80},{1,65},{17,81},{2,66},{18,82},{3,67},{19,83},{7,71}... | collective-permute-start | bytes 393224 | tf_op jit(solution)/shard_map/ppermute | solution.py:407
  77.0 3.8 %collective-permute-done.22.refs_2_.refs_5_ = f32[4,64,128]{2,1,0:T(8,128)S(1)} collective-permute-done((f32[4,64,128]{2,1,0:T(8,128)S(1)}, f32[4,64,128]{2,1,0:T(8,128)S(1)}, u32[]{:S(2)}, u32[]{:S(2)}) %collective-permute-start.22) | collective-permute-done | bytes 131104 | tf_op jit(solution)/shard_map/ppermute | solution.py:407
  80.8 4.6 %collective-permute-done.21.refs_1_ = f32[4,64,128]{2,1,0:T(8,128)S(1)} collective-permute-done((f32[4,64,128]{2,1,0:T(8,128)S(1)}, f32[4,64,128]{2,1,0:T(8,128)S(1)}, u32[]{:S(2)}, u32[]{:S(2)}) %collective-permute-start.21) | collective-permute-done | bytes 131104 | tf_op jit(solution)/shard_map/ppermute | solution.py:407
  85.4 1.1 collective-permute-start.23
  86.6 3.2 %collective-permute-start.27 = (f32[4,64,128]{2,1,0:T(8,128)S(1)}, f32[4,64,128]{2,1,0:T(8,128)S(1)}, u32[]{:S(2)}, u32[]{:S(2)}) collective-permute-start(f32[4,64,128]{2,1,0:T(8,128)S(1)} %collective-permute-done.22.refs_2_.refs_5_), channel_id=1, source_target_pairs={{0,64},{16,80},{1,65},{17,81},{2,66},{18,82},{3,67},{19,83},{7,71}... | collective-permute-start | bytes 393224 | tf_op jit(solution)/shard_map/ppermute | solution.py:407
  89.7 0.6 collective-permute-done.24.refs_3_
  90.4 0.7 shard_map.78
  91.2 1.3 collective-permute-start.26
  92.5 2.5 %collective-permute-done.27.refs_5_ = f32[4,64,128]{2,1,0:T(8,128)S(1)} collective-permute-done((f32[4,64,128]{2,1,0:T(8,128)S(1)}, f32[4,64,128]{2,1,0:T(8,128)S(1)}, u32[]{:S(2)}, u32[]{:S(2)}) %collective-permute-start.27) | collective-permute-done | bytes 131104 | tf_op jit(solution)/shard_map/ppermute | solution.py:407
  95.0 0.3 collective-permute-done.26.refs_3_
  95.4 0.7 shard_map.79
  96.0 2.0 %collective-permute-start.28 = (f32[2,80,128]{2,1,0:T(8,128)S(1)}, f32[2,80,128]{2,1,0:T(8,128)S(1)}, u32[]{:S(2)}, u32[]{:S(2)}) collective-permute-start(f32[2,80,128]{2,1,0:T(8,128)S(1)} %get-tuple-element.81), channel_id=1, source_target_pairs={{0,16},{16,0},{1,17},{17,1},{2,18},{18,2},{3,19},{19,3},{7,23},{23... | collective-permute-start | bytes 245768 | tf_op jit(solution)/shard_map/ppermute | solution.py:407
  98.1 0.9 collective-permute-done.28.refs_2_
  99.0 2.9 %collective-permute-done.29.refs_3_ = f32[2,80,128]{2,1,0:T(8,128)S(1)} collective-permute-done((f32[2,80,128]{2,1,0:T(8,128)S(1)}, f32[2,80,128]{2,1,0:T(8,128)S(1)}, u32[]{:S(2)}, u32[]{:S(2)}) %collective-permute-start.29) | collective-permute-done | bytes 81952 | tf_op jit(solution)/shard_map/ppermute | solution.py:407
  101.9 0.7 shard_map.80
  102.6 0.4 collective-permute-start.30
  103.0 1.2 collective-permute-done.30.refs_2_
  104.2 2.7 %collective-permute-done.31.refs_3_ = f32[2,80,128]{2,1,0:T(8,128)S(1)} collective-permute-done((f32[2,80,128]{2,1,0:T(8,128)S(1)}, f32[2,80,128]{2,1,0:T(8,128)S(1)}, u32[]{:S(2)}, u32[]{:S(2)}) %collective-permute-start.31) | collective-permute-done | bytes 81952 | tf_op jit(solution)/shard_map/ppermute | solution.py:407
  106.9 0.7 shard_map.81
  107.5 0.5 collective-permute-start.32
  108.0 0.9 collective-permute-done.32.refs_2_
  108.9 2.9 %collective-permute-done.33.refs_3_ = f32[2,80,128]{2,1,0:T(8,128)S(1)} collective-permute-done((f32[2,80,128]{2,1,0:T(8,128)S(1)}, f32[2,80,128]{2,1,0:T(8,128)S(1)}, u32[]{:S(2)}, u32[]{:S(2)}) %collective-permute-start.33) | collective-permute-done | bytes 81952 | tf_op jit(solution)/shard_map/ppermute | solution.py:407
  111.9 0.7 shard_map.82
  112.8 1.2 collective-permute-done.34.refs_2_
  113.9 2.7 %collective-permute-done.35.refs_3_ = f32[2,80,128]{2,1,0:T(8,128)S(1)} collective-permute-done((f32[2,80,128]{2,1,0:T(8,128)S(1)}, f32[2,80,128]{2,1,0:T(8,128)S(1)}, u32[]{:S(2)}, u32[]{:S(2)}) %collective-permute-start.35) | collective-permute-done | bytes 81952 | tf_op jit(solution)/shard_map/ppermute | solution.py:407
  116.6 0.7 shard_map.83
  117.4 16.0 %all_to_all.23 = f32[64,16,128]{2,1,0:T(8,128)S(1)} all-to-all(f32[64,16,128]{2,1,0:T(8,128)S(1)} %bitcast.36), channel_id=1, replica_groups={{0,16,1,17,2,18,3,19,7,23,6,22,5,21,4,20,8,24,9,25,10,26,11,27,15,31,14..., dimensions={0} | all-to-all | bytes 1048576 | tf_op jit(solution)/shard_map/all_to_all | solution.py:454
  133.4 1.1 shard_map.84
  (46 shorter events, 2.7 us)
Async XLA Ops:
  0.6 16.1 %collective-permute-start = (f32[1024,128]{1,0:T(8,128)}, f32[1024,128]{1,0:T(8,128)S(1)}, u32[]{:S(2)}, u32[]{:S(2)}) collective-permute-start(f32[1024,128]{1,0:T(8,128)} %bitcast.30), channel_id=1, source_target_pairs={{0,16},{1,17},{2,18},{3,19},{4,20},{5,21},{6,22},{7,23},{8,24},{9,... | collective-permute-start | bytes 1572872 | tf_op jit(solution)/shard_map/ppermute | solution.py:407
  3.7 12.0 %copy-start.5 = (f32[6,64,16]{1,2,0:T(8,128)S(1)}, f32[6,64,16]{1,2,0:T(8,128)}, u32[]{:S(2)}) copy-start(f32[6,64,16]{1,2,0:T(8,128)} %param.9) | copy-start | bytes 73732
  3.9 1.1 copy-start.1
  4.9 1.0 copy-start.3
  6.0 10.8 %copy-start = (f32[1,64,4,4,128]{4,3,2,1,0:T(4,128)S(1)}, f32[1,64,4,4,128]{4,3,2,1,0:T(4,128)}, u32[]{:S(2)}) copy-start(f32[1,64,4,4,128]{4,3,2,1,0:T(4,128)} %param.6) | copy-start | bytes 1572868
  6.0 10.8 %copy-start.4 = (f32[64,4,4,128]{3,2,1,0:T(4,128)S(1)}, f32[64,4,4,128]{3,2,1,0:T(4,128)}, u32[]{:S(2)}) copy-start(f32[64,4,4,128]{3,2,1,0:T(4,128)} %param.7) | copy-start | bytes 1572868
  6.1 10.5 %collective-permute-start.1 = (f32[4,16,128]{2,1,0:T(8,128)S(1)}, f32[4,16,128]{2,1,0:T(8,128)S(1)}, u32[]{:S(2)}, u32[]{:S(2)}) collective-permute-start(f32[4,16,128]{2,1,0:T(8,128)S(1)} %get-tuple-element.48), channel_id=1, source_target_pairs={{0,20},{1,21},{2,22},{3,23},{4,16},{5,17},{6,18},{7,19},{8,28},{9,... | collective-permute-start | bytes 98312 | tf_op jit(solution)/shard_map/ppermute | solution.py:407
  7.2 9.4 %collective-permute-start.2 = (f32[4,16,128]{2,1,0:T(8,128)S(1)}, f32[4,16,128]{2,1,0:T(8,128)S(1)}, u32[]{:S(2)}, u32[]{:S(2)}) collective-permute-start(f32[4,16,128]{2,1,0:T(8,128)S(1)} %get-tuple-element.49), channel_id=1, source_target_pairs={{0,28},{1,29},{2,30},{3,31},{4,24},{5,25},{6,26},{7,27},{8,20},{9,... | collective-permute-start | bytes 98312 | tf_op jit(solution)/shard_map/ppermute | solution.py:407
  10.8 5.8 %collective-permute-start.3 = (f32[4,16,128]{2,1,0:T(8,128)S(1)}, f32[4,16,128]{2,1,0:T(8,128)S(1)}, u32[]{:S(2)}, u32[]{:S(2)}) collective-permute-start(f32[4,16,128]{2,1,0:T(8,128)S(1)} %get-tuple-element.50), channel_id=1, source_target_pairs={{0,17},{1,16},{2,19},{3,18},{4,21},{5,20},{6,23},{7,22},{8,25},{9,... | collective-permute-start | bytes 98312 | tf_op jit(solution)/shard_map/ppermute | solution.py:407
  11.9 4.8 %collective-permute-start.4 = (f32[4,16,128]{2,1,0:T(8,128)S(1)}, f32[4,16,128]{2,1,0:T(8,128)S(1)}, u32[]{:S(2)}, u32[]{:S(2)}) collective-permute-start(f32[4,16,128]{2,1,0:T(8,128)S(1)} %get-tuple-element.51), channel_id=1, source_target_pairs={{0,19},{1,18},{2,17},{3,16},{4,23},{5,22},{6,21},{7,20},{8,27},{9,... | collective-permute-start | bytes 98312 | tf_op jit(solution)/shard_map/ppermute | solution.py:407
  15.7 0.8 copy-start.6
  17.8 3.1 %collective-permute-start.5 = (f32[4,16,128]{2,1,0:T(8,128)S(1)}, f32[4,16,128]{2,1,0:T(8,128)S(1)}, u32[]{:S(2)}, u32[]{:S(2)}) collective-permute-start(f32[4,16,128]{2,1,0:T(8,128)S(1)} %get-tuple-element.53), channel_id=1, source_target_pairs={{0,4},{1,5},{2,6},{3,7},{4,0},{5,1},{6,2},{7,3},{8,12},{9,13},{10,... | collective-permute-start | bytes 98312 | tf_op jit(solution)/shard_map/ppermute | solution.py:407
  18.2 4.0 %collective-permute-start.6 = (f32[4,16,128]{2,1,0:T(8,128)S(1)}, f32[4,16,128]{2,1,0:T(8,128)S(1)}, u32[]{:S(2)}, u32[]{:S(2)}) collective-permute-start(f32[4,16,128]{2,1,0:T(8,128)S(1)} %get-tuple-element.54), channel_id=1, source_target_pairs={{0,12},{1,13},{2,14},{3,15},{4,8},{5,9},{6,10},{7,11},{8,4},{9,5},... | collective-permute-start | bytes 98312 | tf_op jit(solution)/shard_map/ppermute | solution.py:407
  19.0 3.2 %collective-permute-start.7 = (f32[4,16,128]{2,1,0:T(8,128)S(1)}, f32[4,16,128]{2,1,0:T(8,128)S(1)}, u32[]{:S(2)}, u32[]{:S(2)}) collective-permute-start(f32[4,16,128]{2,1,0:T(8,128)S(1)} %get-tuple-element.55), channel_id=1, source_target_pairs={{0,1},{1,0},{2,3},{3,2},{4,5},{5,4},{6,7},{7,6},{8,9},{9,8},{10,11... | collective-permute-start | bytes 98312 | tf_op jit(solution)/shard_map/ppermute | solution.py:407
  19.1 4.0 %collective-permute-start.8 = (f32[4,16,128]{2,1,0:T(8,128)S(1)}, f32[4,16,128]{2,1,0:T(8,128)S(1)}, u32[]{:S(2)}, u32[]{:S(2)}) collective-permute-start(f32[4,16,128]{2,1,0:T(8,128)S(1)} %get-tuple-element.56), channel_id=1, source_target_pairs={{0,3},{1,2},{2,1},{3,0},{4,7},{5,6},{6,5},{7,4},{8,11},{9,10},{10,... | collective-permute-start | bytes 98312 | tf_op jit(solution)/shard_map/ppermute | solution.py:407
  23.7 4.2 %collective-permute-start.9 = (f32[4,16,128]{2,1,0:T(8,128)S(1)}, f32[4,16,128]{2,1,0:T(8,128)S(1)}, u32[]{:S(2)}, u32[]{:S(2)}) collective-permute-start(f32[4,16,128]{2,1,0:T(8,128)S(1)} %get-tuple-element.58), channel_id=1, source_target_pairs={{0,4},{1,5},{2,6},{3,7},{4,0},{5,1},{6,2},{7,3},{8,12},{9,13},{10,... | collective-permute-start | bytes 98312 | tf_op jit(solution)/shard_map/ppermute | solution.py:407
  24.6 4.0 %collective-permute-start.10 = (f32[4,16,128]{2,1,0:T(8,128)S(1)}, f32[4,16,128]{2,1,0:T(8,128)S(1)}, u32[]{:S(2)}, u32[]{:S(2)}) collective-permute-start(f32[4,16,128]{2,1,0:T(8,128)S(1)} %get-tuple-element.59), channel_id=1, source_target_pairs={{0,12},{1,13},{2,14},{3,15},{4,8},{5,9},{6,10},{7,11},{8,4},{9,5},... | collective-permute-start | bytes 98312 | tf_op jit(solution)/shard_map/ppermute | solution.py:407
  26.4 2.8 %collective-permute-start.11 = (f32[4,16,128]{2,1,0:T(8,128)S(1)}, f32[4,16,128]{2,1,0:T(8,128)S(1)}, u32[]{:S(2)}, u32[]{:S(2)}) collective-permute-start(f32[4,16,128]{2,1,0:T(8,128)S(1)} %get-tuple-element.60), channel_id=1, source_target_pairs={{0,1},{1,0},{2,3},{3,2},{4,5},{5,4},{6,7},{7,6},{8,9},{9,8},{10,11... | collective-permute-start | bytes 98312 | tf_op jit(solution)/shard_map/ppermute | solution.py:407
  26.6 4.0 %collective-permute-start.12 = (f32[4,16,128]{2,1,0:T(8,128)S(1)}, f32[4,16,128]{2,1,0:T(8,128)S(1)}, u32[]{:S(2)}, u32[]{:S(2)}) collective-permute-start(f32[4,16,128]{2,1,0:T(8,128)S(1)} %get-tuple-element.61), channel_id=1, source_target_pairs={{0,3},{1,2},{2,1},{3,0},{4,7},{5,6},{6,5},{7,4},{8,11},{9,10},{10,... | collective-permute-start | bytes 98312 | tf_op jit(solution)/shard_map/ppermute | solution.py:407
  30.6 5.8 %copy-start.2 = (f32[1,64,4,4,128]{4,3,2,1,0:T(4,128)S(1)}, f32[1,64,4,4,128]{4,3,2,1,0:T(4,128)}, u32[]{:S(2)}) copy-start(f32[1,64,4,4,128]{4,3,2,1,0:T(4,128)} %param.5) | copy-start | bytes 1572868
  31.2 3.2 %collective-permute-start.13 = (f32[4,16,128]{2,1,0:T(8,128)S(1)}, f32[4,16,128]{2,1,0:T(8,128)S(1)}, u32[]{:S(2)}, u32[]{:S(2)}) collective-permute-start(f32[4,16,128]{2,1,0:T(8,128)S(1)} %get-tuple-element.63), channel_id=1, source_target_pairs={{0,4},{1,5},{2,6},{3,7},{4,0},{5,1},{6,2},{7,3},{8,12},{9,13},{10,... | collective-permute-start | bytes 98312 | tf_op jit(solution)/shard_map/ppermute | solution.py:407
  31.6 4.0 %collective-permute-start.14 = (f32[4,16,128]{2,1,0:T(8,128)S(1)}, f32[4,16,128]{2,1,0:T(8,128)S(1)}, u32[]{:S(2)}, u32[]{:S(2)}) collective-permute-start(f32[4,16,128]{2,1,0:T(8,128)S(1)} %get-tuple-element.64), channel_id=1, source_target_pairs={{0,12},{1,13},{2,14},{3,15},{4,8},{5,9},{6,10},{7,11},{8,4},{9,5},... | collective-permute-start | bytes 98312 | tf_op jit(solution)/shard_map/ppermute | solution.py:407
  32.3 3.3 %collective-permute-start.15 = (f32[4,16,128]{2,1,0:T(8,128)S(1)}, f32[4,16,128]{2,1,0:T(8,128)S(1)}, u32[]{:S(2)}, u32[]{:S(2)}) collective-permute-start(f32[4,16,128]{2,1,0:T(8,128)S(1)} %get-tuple-element.65), channel_id=1, source_target_pairs={{0,1},{1,0},{2,3},{3,2},{4,5},{5,4},{6,7},{7,6},{8,9},{9,8},{10,11... | collective-permute-start | bytes 98312 | tf_op jit(solution)/shard_map/ppermute | solution.py:407
  32.3 4.0 %collective-permute-start.16 = (f32[4,16,128]{2,1,0:T(8,128)S(1)}, f32[4,16,128]{2,1,0:T(8,128)S(1)}, u32[]{:S(2)}, u32[]{:S(2)}) collective-permute-start(f32[4,16,128]{2,1,0:T(8,128)S(1)} %get-tuple-element.66), channel_id=1, source_target_pairs={{0,3},{1,2},{2,1},{3,0},{4,7},{5,6},{6,5},{7,4},{8,11},{9,10},{10,... | collective-permute-start | bytes 98312 | tf_op jit(solution)/shard_map/ppermute | solution.py:407
  63.5 1.9 %collective-permute-start.17 = (f32[2,144,128]{2,1,0:T(8,128)S(1)}, f32[2,144,128]{2,1,0:T(8,128)S(1)}, u32[]{:S(2)}, u32[]{:S(2)}) collective-permute-start(f32[2,144,128]{2,1,0:T(8,128)S(1)} %get-tuple-element.69), channel_id=1, source_target_pairs={{0,16},{16,0},{1,17},{17,1},{2,18},{18,2},{3,19},{19,3},{7,23},{23... | collective-permute-start | bytes 442376 | tf_op jit(solution)/shard_map/ppermute | solution.py:407
  64.5 4.6 %collective-permute-start.18 = (f32[2,144,128]{2,1,0:T(8,128)S(1)}, f32[2,144,128]{2,1,0:T(8,128)S(1)}, u32[]{:S(2)}, u32[]{:S(2)}) collective-permute-start(f32[2,144,128]{2,1,0:T(8,128)S(1)} %get-tuple-element.70), channel_id=1, source_target_pairs={{0,48},{16,1},{1,16},{17,2},{2,17},{18,3},{3,18},{19,7},{7,19},{23... | collective-permute-start | bytes 442376 | tf_op jit(solution)/shard_map/ppermute | solution.py:407
  69.7 1.3 collective-permute-start.19
  69.9 3.2 %collective-permute-start.20 = (f32[2,16,128]{2,1,0:T(8,128)S(1)}, f32[2,16,128]{2,1,0:T(8,128)S(1)}, u32[]{:S(2)}, u32[]{:S(2)}) collective-permute-start(f32[2,16,128]{2,1,0:T(8,128)S(1)} %get-tuple-element.73), channel_id=1, source_target_pairs={{0,48},{16,1},{1,16},{17,2},{2,17},{18,3},{3,18},{19,7},{7,19},{23... | collective-permute-start | bytes 49160 | tf_op jit(solution)/shard_map/ppermute | solution.py:407
  73.4 7.4 %collective-permute-start.22 = (f32[4,64,128]{2,1,0:T(8,128)S(1)}, f32[4,64,128]{2,1,0:T(8,128)S(1)}, u32[]{:S(2)}, u32[]{:S(2)}) collective-permute-start(f32[4,64,128]{2,1,0:T(8,128)S(1)} %shard_map.76.refs_6_), channel_id=1, source_target_pairs={{0,64},{16,80},{1,65},{17,81},{2,66},{18,82},{3,67},{19,83},{7,71}... | collective-permute-start | bytes 393224 | tf_op jit(solution)/shard_map/ppermute | solution.py:407
  76.7 8.6 %collective-permute-start.21 = (f32[4,64,128]{2,1,0:T(8,128)S(1)}, f32[4,64,128]{2,1,0:T(8,128)S(1)}, u32[]{:S(2)}, u32[]{:S(2)}) collective-permute-start(f32[4,64,128]{2,1,0:T(8,128)S(1)} %shard_map.76.refs_6_), channel_id=1, source_target_pairs={{0,192},{16,208},{1,193},{17,209},{2,194},{18,210},{3,195},{19,211... | collective-permute-start | bytes 393224 | tf_op jit(solution)/shard_map/ppermute | solution.py:407
  85.4 4.3 %collective-permute-start.23 = (f32[2,80,128]{2,1,0:T(8,128)S(1)}, f32[2,80,128]{2,1,0:T(8,128)S(1)}, u32[]{:S(2)}, u32[]{:S(2)}) collective-permute-start(f32[2,80,128]{2,1,0:T(8,128)S(1)} %get-tuple-element.75), channel_id=1, source_target_pairs={{0,16},{16,0},{1,17},{17,1},{2,18},{18,2},{3,19},{19,3},{7,23},{23... | collective-permute-start | bytes 245768 | tf_op jit(solution)/shard_map/ppermute | solution.py:407
  86.5 3.9 %collective-permute-start.24 = (f32[2,80,128]{2,1,0:T(8,128)S(1)}, f32[2,80,128]{2,1,0:T(8,128)S(1)}, u32[]{:S(2)}, u32[]{:S(2)}) collective-permute-start(f32[2,80,128]{2,1,0:T(8,128)S(1)} %get-tuple-element.76), channel_id=1, source_target_pairs={{0,48},{16,1},{1,16},{17,2},{2,17},{18,3},{3,18},{19,7},{7,19},{23... | collective-permute-start | bytes 245768 | tf_op jit(solution)/shard_map/ppermute | solution.py:407
  86.6 8.4 %collective-permute-start.27 = (f32[4,64,128]{2,1,0:T(8,128)S(1)}, f32[4,64,128]{2,1,0:T(8,128)S(1)}, u32[]{:S(2)}, u32[]{:S(2)}) collective-permute-start(f32[4,64,128]{2,1,0:T(8,128)S(1)} %collective-permute-done.22.refs_2_.refs_5_), channel_id=1, source_target_pairs={{0,64},{16,80},{1,65},{17,81},{2,66},{18,82},{3,67},{19,83},{7,71}... | collective-permute-start | bytes 393224 | tf_op jit(solution)/shard_map/ppermute | solution.py:407
  91.0 4.0 %collective-permute-start.25 = (f32[2,80,128]{2,1,0:T(8,128)S(1)}, f32[2,80,128]{2,1,0:T(8,128)S(1)}, u32[]{:S(2)}, u32[]{:S(2)}) collective-permute-start(f32[2,80,128]{2,1,0:T(8,128)S(1)} %get-tuple-element.78), channel_id=1, source_target_pairs={{0,16},{16,0},{1,17},{17,1},{2,18},{18,2},{3,19},{19,3},{7,23},{23... | collective-permute-start | bytes 245768 | tf_op jit(solution)/shard_map/ppermute | solution.py:407
  91.2 4.2 %collective-permute-start.26 = (f32[2,80,128]{2,1,0:T(8,128)S(1)}, f32[2,80,128]{2,1,0:T(8,128)S(1)}, u32[]{:S(2)}, u32[]{:S(2)}) collective-permute-start(f32[2,80,128]{2,1,0:T(8,128)S(1)} %get-tuple-element.79), channel_id=1, source_target_pairs={{0,48},{16,1},{1,16},{17,2},{2,17},{18,3},{3,18},{19,7},{7,19},{23... | collective-permute-start | bytes 245768 | tf_op jit(solution)/shard_map/ppermute | solution.py:407
  96.0 3.0 %collective-permute-start.28 = (f32[2,80,128]{2,1,0:T(8,128)S(1)}, f32[2,80,128]{2,1,0:T(8,128)S(1)}, u32[]{:S(2)}, u32[]{:S(2)}) collective-permute-start(f32[2,80,128]{2,1,0:T(8,128)S(1)} %get-tuple-element.81), channel_id=1, source_target_pairs={{0,16},{16,0},{1,17},{17,1},{2,18},{18,2},{3,19},{19,3},{7,23},{23... | collective-permute-start | bytes 245768 | tf_op jit(solution)/shard_map/ppermute | solution.py:407
  98.1 3.9 %collective-permute-start.29 = (f32[2,80,128]{2,1,0:T(8,128)S(1)}, f32[2,80,128]{2,1,0:T(8,128)S(1)}, u32[]{:S(2)}, u32[]{:S(2)}) collective-permute-start(f32[2,80,128]{2,1,0:T(8,128)S(1)} %get-tuple-element.82), channel_id=1, source_target_pairs={{0,48},{16,1},{1,16},{17,2},{2,17},{18,3},{3,18},{19,7},{7,19},{23... | collective-permute-start | bytes 245768 | tf_op jit(solution)/shard_map/ppermute | solution.py:407
  102.6 1.6 %collective-permute-start.30 = (f32[2,80,128]{2,1,0:T(8,128)S(1)}, f32[2,80,128]{2,1,0:T(8,128)S(1)}, u32[]{:S(2)}, u32[]{:S(2)}) collective-permute-start(f32[2,80,128]{2,1,0:T(8,128)S(1)} %get-tuple-element.84), channel_id=1, source_target_pairs={{0,16},{16,0},{1,17},{17,1},{2,18},{18,2},{3,19},{19,3},{7,23},{23... | collective-permute-start | bytes 245768 | tf_op jit(solution)/shard_map/ppermute | solution.py:407
  103.0 3.9 %collective-permute-start.31 = (f32[2,80,128]{2,1,0:T(8,128)S(1)}, f32[2,80,128]{2,1,0:T(8,128)S(1)}, u32[]{:S(2)}, u32[]{:S(2)}) collective-permute-start(f32[2,80,128]{2,1,0:T(8,128)S(1)} %get-tuple-element.85), channel_id=1, source_target_pairs={{0,48},{16,1},{1,16},{17,2},{2,17},{18,3},{3,18},{19,7},{7,19},{23... | collective-permute-start | bytes 245768 | tf_op jit(solution)/shard_map/ppermute | solution.py:407
  107.5 1.4 %collective-permute-start.32 = (f32[2,80,128]{2,1,0:T(8,128)S(1)}, f32[2,80,128]{2,1,0:T(8,128)S(1)}, u32[]{:S(2)}, u32[]{:S(2)}) collective-permute-start(f32[2,80,128]{2,1,0:T(8,128)S(1)} %get-tuple-element.87), channel_id=1, source_target_pairs={{0,16},{16,0},{1,17},{17,1},{2,18},{18,2},{3,19},{19,3},{7,23},{23... | collective-permute-start | bytes 245768 | tf_op jit(solution)/shard_map/ppermute | solution.py:407
  108.0 3.9 %collective-permute-start.33 = (f32[2,80,128]{2,1,0:T(8,128)S(1)}, f32[2,80,128]{2,1,0:T(8,128)S(1)}, u32[]{:S(2)}, u32[]{:S(2)}) collective-permute-start(f32[2,80,128]{2,1,0:T(8,128)S(1)} %get-tuple-element.88), channel_id=1, source_target_pairs={{0,48},{16,1},{1,16},{17,2},{2,17},{18,3},{3,18},{19,7},{7,19},{23... | collective-permute-start | bytes 245768 | tf_op jit(solution)/shard_map/ppermute | solution.py:407
  112.6 1.4 %collective-permute-start.34 = (f32[2,80,128]{2,1,0:T(8,128)S(1)}, f32[2,80,128]{2,1,0:T(8,128)S(1)}, u32[]{:S(2)}, u32[]{:S(2)}) collective-permute-start(f32[2,80,128]{2,1,0:T(8,128)S(1)} %get-tuple-element.90), channel_id=1, source_target_pairs={{0,16},{16,0},{1,17},{17,1},{2,18},{18,2},{3,19},{19,3},{7,23},{23... | collective-permute-start | bytes 245768 | tf_op jit(solution)/shard_map/ppermute | solution.py:407
  112.8 3.9 %collective-permute-start.35 = (f32[2,80,128]{2,1,0:T(8,128)S(1)}, f32[2,80,128]{2,1,0:T(8,128)S(1)}, u32[]{:S(2)}, u32[]{:S(2)}) collective-permute-start(f32[2,80,128]{2,1,0:T(8,128)S(1)} %get-tuple-element.91), channel_id=1, source_target_pairs={{0,48},{16,1},{1,16},{17,2},{2,17},{18,3},{3,18},{19,7},{7,19},{23... | collective-permute-start | bytes 245768 | tf_op jit(solution)/shard_map/ppermute | solution.py:407

commit v3 on v2

--- a/solution.py
+++ b/solution.py
@@ -434,7 +434,7 @@
     hops = (swap_x(1, 0), swap_x(1, 1), swap_y(1, 0), swap_y(1, 1))
     sides = [(3, 4, EX), (5, 6, EY)]
     for step in range(3):
-        xb, xa, yb, ya = [send(f, pairs) for f, pairs in zip(faces, hops)]
+        xb, yb, xa, ya = [send(faces[i], hops[i]) for i in (0, 2, 1, 3)]
         kernel, held, more = (fine_kernel, [], []) if step else (first_fine_kernel, [block], [start])
         v, *faces = call(
             kernel, [whole] + [face] * 4, *fine_cost, held,
@@ -443,7 +443,7 @@
             flags, v, source, xb, xa, yb, ya, w, *more
         )
         hops = (swap_x(0, 0), swap_x(0, 1), swap_y(0, 0), swap_y(0, 1))
-    xb, xa, yb, ya = [send(f, pairs) for f, pairs in zip(faces, hops)]
+    xb, yb, xa, ya = [send(faces[i], hops[i]) for i in (0, 2, 1, 3)]
     resid, packed = call(residual_kernel, [rows, rows], *fine_cost, [block], ins=sides)(
         flags, v, source, xb, xa, yb, ya, w, state
     )

time: 135 us -> 135 us (level)
  no operation moved by 1% of the time
where the time goes in v3:
time: 135 us
  waiting for transfers between devices  41.5 us (31%)
  blocking collectives  41.3 us (31%)
  starting transfers between devices  37.3 us (28%)
  Pallas kernels  10.5 us (8%)
  local copies, waits for them, and re-layouts  3.04 us (2%)
    ppermute x36, waiting for transfers between devices, send(): return lax.ppermute(value, AXES, pairs)  41.5 us
    all_to_all x2, blocking collectives, traded(): lax.all_to_all(value, AXES, 0, 0, axis_index_groups=peers, tiled=True)  41.3 us
    ppermute x36, starting transfers between devices, send(): return lax.ppermute(value, AXES, pairs)  37.3 us
    pallas_call x17, Pallas kernels, run(): pl.pallas_call(body, out_shape=[jax.ShapeDtypeStruct(s, d) for s, d in ou...  10.5 us
    unnamed x14, local copies, waits for them, and re-layouts  2.8 us
  transfers between devices with their start and end apart: 36, of which 25 were waited for; matrix products, arithmetic and copies ran while one was open for 0% of the time, Pallas kernels for 1%

profile of v3, /device:TPU:1, one launch (start us, length us, event | category | flops | bytes accessed | tf_op | source)
XLA Modules:
  0.0 134.5 jit_solution(15465909733496445496)
XLA Ops:
  0.6 3.0 %collective-permute-start = (f32[1024,128]{1,0:T(8,128)}, f32[1024,128]{1,0:T(8,128)S(1)}, u32[]{:S(2)}, u32[]{:S(2)}) collective-permute-start(f32[1024,128]{1,0:T(8,128)} %bitcast.30), channel_id=1, source_target_pairs={{0,16},{1,17},{2,18},{3,19},{4,20},{5,21},{6,22},{7,23},{8,24},{9,... | collective-permute-start | bytes 1572872 | tf_op jit(solution)/shard_map/ppermute | solution.py:407
  3.9 1.0 copy-done.1
  4.9 1.0 copy-done.3
  6.1 1.1 collective-permute-start.1
  7.2 3.6 %collective-permute-start.2 = (f32[4,16,128]{2,1,0:T(8,128)S(1)}, f32[4,16,128]{2,1,0:T(8,128)S(1)}, u32[]{:S(2)}, u32[]{:S(2)}) collective-permute-start(f32[4,16,128]{2,1,0:T(8,128)S(1)} %get-tuple-element.49), channel_id=1, source_target_pairs={{0,28},{1,29},{2,30},{3,31},{4,24},{5,25},{6,26},{7,27},{8,20},{9,... | collective-permute-start | bytes 98312 | tf_op jit(solution)/shard_map/ppermute | solution.py:407
  10.8 1.1 collective-permute-start.3
  11.9 3.7 %collective-permute-start.4 = (f32[4,16,128]{2,1,0:T(8,128)S(1)}, f32[4,16,128]{2,1,0:T(8,128)S(1)}, u32[]{:S(2)}, u32[]{:S(2)}) collective-permute-start(f32[4,16,128]{2,1,0:T(8,128)S(1)} %get-tuple-element.51), channel_id=1, source_target_pairs={{0,19},{1,18},{2,17},{3,16},{4,23},{5,22},{6,21},{7,20},{8,27},{9,... | collective-permute-start | bytes 98312 | tf_op jit(solution)/shard_map/ppermute | solution.py:407
  15.7 0.7 copy-done.6
  16.8 1.0 shard_map.70
  17.8 0.4 collective-permute-start.5
  18.2 0.8 collective-permute-start.6
  19.1 1.8 %collective-permute-start.8 = (f32[4,16,128]{2,1,0:T(8,128)S(1)}, f32[4,16,128]{2,1,0:T(8,128)S(1)}, u32[]{:S(2)}, u32[]{:S(2)}) collective-permute-start(f32[4,16,128]{2,1,0:T(8,128)S(1)} %get-tuple-element.56), channel_id=1, source_target_pairs={{0,3},{1,2},{2,1},{3,0},{4,7},{5,6},{6,5},{7,4},{8,11},{9,10},{10,... | collective-permute-start | bytes 98312 | tf_op jit(solution)/shard_map/ppermute | solution.py:407
  20.9 1.3 collective-permute-done.6.refs_4_
  22.1 0.9 collective-permute-done.8.refs_6_
  23.1 0.6 shard_map.71
  23.7 0.8 collective-permute-start.9
  24.6 1.8 %collective-permute-start.10 = (f32[4,16,128]{2,1,0:T(8,128)S(1)}, f32[4,16,128]{2,1,0:T(8,128)S(1)}, u32[]{:S(2)}, u32[]{:S(2)}) collective-permute-start(f32[4,16,128]{2,1,0:T(8,128)S(1)} %get-tuple-element.59), channel_id=1, source_target_pairs={{0,12},{1,13},{2,14},{3,15},{4,8},{5,9},{6,10},{7,11},{8,4},{9,5},... | collective-permute-start | bytes 98312 | tf_op jit(solution)/shard_map/ppermute | solution.py:407
  26.6 1.4 %collective-permute-start.12 = (f32[4,16,128]{2,1,0:T(8,128)S(1)}, f32[4,16,128]{2,1,0:T(8,128)S(1)}, u32[]{:S(2)}, u32[]{:S(2)}) collective-permute-start(f32[4,16,128]{2,1,0:T(8,128)S(1)} %get-tuple-element.61), channel_id=1, source_target_pairs={{0,3},{1,2},{2,1},{3,0},{4,7},{5,6},{6,5},{7,4},{8,11},{9,10},{10,... | collective-permute-start | bytes 98312 | tf_op jit(solution)/shard_map/ppermute | solution.py:407
  28.0 0.6 collective-permute-done.10.refs_4_
  28.6 0.6 collective-permute-done.11.refs_5_
  29.2 1.4 %collective-permute-done.12.refs_6_ = f32[4,16,128]{2,1,0:T(8,128)S(1)} collective-permute-done((f32[4,16,128]{2,1,0:T(8,128)S(1)}, f32[4,16,128]{2,1,0:T(8,128)S(1)}, u32[]{:S(2)}, u32[]{:S(2)}) %collective-permute-start.12) | collective-permute-done | bytes 32800 | tf_op jit(solution)/shard_map/ppermute | solution.py:407
  30.6 0.6 shard_map.72
  31.2 0.4 collective-permute-start.13
  31.6 0.7 collective-permute-start.14
  32.3 2.0 %collective-permute-start.16 = (f32[4,16,128]{2,1,0:T(8,128)S(1)}, f32[4,16,128]{2,1,0:T(8,128)S(1)}, u32[]{:S(2)}, u32[]{:S(2)}) collective-permute-start(f32[4,16,128]{2,1,0:T(8,128)S(1)} %get-tuple-element.66), channel_id=1, source_target_pairs={{0,3},{1,2},{2,1},{3,0},{4,7},{5,6},{6,5},{7,4},{8,11},{9,10},{10,... | collective-permute-start | bytes 98312 | tf_op jit(solution)/shard_map/ppermute | solution.py:407
  34.4 1.2 collective-permute-done.14.refs_4_
  35.6 0.8 collective-permute-done.16.refs_6_
  36.4 1.7 %shard_map.73 = (f32[1024,128]{1,0:T(8,128)}, f32[1024,128]{1,0:T(8,128)S(1)}) custom-call(f32[14,128]{1,0:T(8,128)S(1)} %broadcast_in_dim.2.refs_0_, f32[16,64,128]{2,1,0:T(8,128)S(1)} %get-tuple-element.62.refs_1_, f32[1024,128]{1,0:T(8,128)S(1)} %bitcast.29, f32[4,16,128]{2,1,0:T(8,128)S(1)} %collective-permute-done.13.refs_3_, ...), custom_call_target="tpu_custom_call" | custom-call | flops 125829120 | bytes 1572864 | tf_op jit(solution)/shard_map/pallas_call | solution.py:60
  38.0 25.3 %all_to_all.22 = f32[64,16,128]{2,1,0:T(8,128)S(1)} all-to-all(f32[64,16,128]{2,1,0:T(8,128)S(1)} %bitcast.39), channel_id=1, replica_groups={{0,16,1,17,2,18,3,19,7,23,6,22,5,21,4,20,8,24,9,25,10,26,11,27,15,31,14..., dimensions={0} | all-to-all | bytes 1048576 | tf_op jit(solution)/shard_map/all_to_all | solution.py:454
  63.5 0.9 collective-permute-start.17
  64.6 0.9 collective-permute-done.17.refs_2_
  65.5 3.6 %collective-permute-done.18.refs_3_ = f32[2,144,128]{2,1,0:T(8,128)S(1)} collective-permute-done((f32[2,144,128]{2,1,0:T(8,128)S(1)}, f32[2,144,128]{2,1,0:T(8,128)S(1)}, u32[]{:S(2)}, u32[]{:S(2)}) %collective-permute-start.18) | collective-permute-done | bytes 147488 | tf_op jit(solution)/shard_map/ppermute | solution.py:407
  69.0 0.7 shard_map.75
  69.9 0.4 collective-permute-start.20
  70.2 0.7 collective-permute-done.19.refs_3_
  71.0 2.1 %collective-permute-done.20.refs_4_ = f32[2,16,128]{2,1,0:T(8,128)S(1)} collective-permute-done((f32[2,16,128]{2,1,0:T(8,128)S(1)}, f32[2,16,128]{2,1,0:T(8,128)S(1)}, u32[]{:S(2)}, u32[]{:S(2)}) %collective-permute-start.20) | collective-permute-done | bytes 16416 | tf_op jit(solution)/shard_map/ppermute | solution.py:407
  73.4 3.4 %collective-permute-start.22 = (f32[4,64,128]{2,1,0:T(8,128)S(1)}, f32[4,64,128]{2,1,0:T(8,128)S(1)}, u32[]{:S(2)}, u32[]{:S(2)}) collective-permute-start(f32[4,64,128]{2,1,0:T(8,128)S(1)} %shard_map.76.refs_6_), channel_id=1, source_target_pairs={{0,64},{16,80},{1,65},{17,81},{2,66},{18,82},{3,67},{19,83},{7,71}... | collective-permute-start | bytes 393224 | tf_op jit(solution)/shard_map/ppermute | solution.py:407
  77.0 3.8 %collective-permute-done.22.refs_2_.refs_5_ = f32[4,64,128]{2,1,0:T(8,128)S(1)} collective-permute-done((f32[4,64,128]{2,1,0:T(8,128)S(1)}, f32[4,64,128]{2,1,0:T(8,128)S(1)}, u32[]{:S(2)}, u32[]{:S(2)}) %collective-permute-start.22) | collective-permute-done | bytes 131104 | tf_op jit(solution)/shard_map/ppermute | solution.py:407
  80.8 4.6 %collective-permute-done.21.refs_1_ = f32[4,64,128]{2,1,0:T(8,128)S(1)} collective-permute-done((f32[4,64,128]{2,1,0:T(8,128)S(1)}, f32[4,64,128]{2,1,0:T(8,128)S(1)}, u32[]{:S(2)}, u32[]{:S(2)}) %collective-permute-start.21) | collective-permute-done | bytes 131104 | tf_op jit(solution)/shard_map/ppermute | solution.py:407
  85.4 1.1 collective-permute-start.23
  86.6 3.2 %collective-permute-start.27 = (f32[4,64,128]{2,1,0:T(8,128)S(1)}, f32[4,64,128]{2,1,0:T(8,128)S(1)}, u32[]{:S(2)}, u32[]{:S(2)}) collective-permute-start(f32[4,64,128]{2,1,0:T(8,128)S(1)} %collective-permute-done.22.refs_2_.refs_5_), channel_id=1, source_target_pairs={{0,64},{16,80},{1,65},{17,81},{2,66},{18,82},{3,67},{19,83},{7,71}... | collective-permute-start | bytes 393224 | tf_op jit(solution)/shard_map/ppermute | solution.py:407
  89.7 0.6 collective-permute-done.24.refs_3_
  90.4 0.7 shard_map.78
  91.2 1.3 collective-permute-start.26
  92.5 2.5 %collective-permute-done.27.refs_5_ = f32[4,64,128]{2,1,0:T(8,128)S(1)} collective-permute-done((f32[4,64,128]{2,1,0:T(8,128)S(1)}, f32[4,64,128]{2,1,0:T(8,128)S(1)}, u32[]{:S(2)}, u32[]{:S(2)}) %collective-permute-start.27) | collective-permute-done | bytes 131104 | tf_op jit(solution)/shard_map/ppermute | solution.py:407
  95.0 0.3 collective-permute-done.26.refs_3_
  95.4 0.7 shard_map.79
  96.0 2.0 %collective-permute-start.28 = (f32[2,80,128]{2,1,0:T(8,128)S(1)}, f32[2,80,128]{2,1,0:T(8,128)S(1)}, u32[]{:S(2)}, u32[]{:S(2)}) collective-permute-start(f32[2,80,128]{2,1,0:T(8,128)S(1)} %get-tuple-element.81), channel_id=1, source_target_pairs={{0,16},{16,0},{1,17},{17,1},{2,18},{18,2},{3,19},{19,3},{7,23},{23... | collective-permute-start | bytes 245768 | tf_op jit(solution)/shard_map/ppermute | solution.py:407
  98.1 0.9 collective-permute-done.28.refs_2_
  99.0 2.9 %collective-permute-done.29.refs_3_ = f32[2,80,128]{2,1,0:T(8,128)S(1)} collective-permute-done((f32[2,80,128]{2,1,0:T(8,128)S(1)}, f32[2,80,128]{2,1,0:T(8,128)S(1)}, u32[]{:S(2)}, u32[]{:S(2)}) %collective-permute-start.29) | collective-permute-done | bytes 81952 | tf_op jit(solution)/shard_map/ppermute | solution.py:407
  101.9 0.7 shard_map.80
  102.6 0.4 collective-permute-start.30
  103.0 1.2 collective-permute-done.30.refs_2_
  104.2 2.7 %collective-permute-done.31.refs_3_ = f32[2,80,128]{2,1,0:T(8,128)S(1)} collective-permute-done((f32[2,80,128]{2,1,0:T(8,128)S(1)}, f32[2,80,128]{2,1,0:T(8,128)S(1)}, u32[]{:S(2)}, u32[]{:S(2)}) %collective-permute-start.31) | collective-permute-done | bytes 81952 | tf_op jit(solution)/shard_map/ppermute | solution.py:407
  106.9 0.7 shard_map.81
  107.5 0.5 collective-permute-start.32
  108.0 0.9 collective-permute-done.32.refs_2_
  108.9 2.9 %collective-permute-done.33.refs_3_ = f32[2,80,128]{2,1,0:T(8,128)S(1)} collective-permute-done((f32[2,80,128]{2,1,0:T(8,128)S(1)}, f32[2,80,128]{2,1,0:T(8,128)S(1)}, u32[]{:S(2)}, u32[]{:S(2)}) %collective-permute-start.33) | collective-permute-done | bytes 81952 | tf_op jit(solution)/shard_map/ppermute | solution.py:407
  111.9 0.7 shard_map.82
  112.8 1.2 collective-permute-done.34.refs_2_
  113.9 2.7 %collective-permute-done.35.refs_3_ = f32[2,80,128]{2,1,0:T(8,128)S(1)} collective-permute-done((f32[2,80,128]{2,1,0:T(8,128)S(1)}, f32[2,80,128]{2,1,0:T(8,128)S(1)}, u32[]{:S(2)}, u32[]{:S(2)}) %collective-permute-start.35) | collective-permute-done | bytes 81952 | tf_op jit(solution)/shard_map/ppermute | solution.py:407
  116.6 0.7 shard_map.83
  117.4 16.0 %all_to_all.23 = f32[64,16,128]{2,1,0:T(8,128)S(1)} all-to-all(f32[64,16,128]{2,1,0:T(8,128)S(1)} %bitcast.36), channel_id=1, replica_groups={{0,16,1,17,2,18,3,19,7,23,6,22,5,21,4,20,8,24,9,25,10,26,11,27,15,31,14..., dimensions={0} | all-to-all | bytes 1048576 | tf_op jit(solution)/shard_map/all_to_all | solution.py:454
  133.4 1.1 shard_map.84
  (46 shorter events, 2.7 us)
Async XLA Ops:
  0.6 16.1 %collective-permute-start = (f32[1024,128]{1,0:T(8,128)}, f32[1024,128]{1,0:T(8,128)S(1)}, u32[]{:S(2)}, u32[]{:S(2)}) collective-permute-start(f32[1024,128]{1,0:T(8,128)} %bitcast.30), channel_id=1, source_target_pairs={{0,16},{1,17},{2,18},{3,19},{4,20},{5,21},{6,22},{7,23},{8,24},{9,... | collective-permute-start | bytes 1572872 | tf_op jit(solution)/shard_map/ppermute | solution.py:407
  3.7 12.0 %copy-start.5 = (f32[6,64,16]{1,2,0:T(8,128)S(1)}, f32[6,64,16]{1,2,0:T(8,128)}, u32[]{:S(2)}) copy-start(f32[6,64,16]{1,2,0:T(8,128)} %param.9) | copy-start | bytes 73732
  3.9 1.1 copy-start.1
  4.9 1.0 copy-start.3
  6.0 10.8 %copy-start = (f32[1,64,4,4,128]{4,3,2,1,0:T(4,128)S(1)}, f32[1,64,4,4,128]{4,3,2,1,0:T(4,128)}, u32[]{:S(2)}) copy-start(f32[1,64,4,4,128]{4,3,2,1,0:T(4,128)} %param.6) | copy-start | bytes 1572868
  6.0 10.8 %copy-start.4 = (f32[64,4,4,128]{3,2,1,0:T(4,128)S(1)}, f32[64,4,4,128]{3,2,1,0:T(4,128)}, u32[]{:S(2)}) copy-start(f32[64,4,4,128]{3,2,1,0:T(4,128)} %param.7) | copy-start | bytes 1572868
  6.1 10.5 %collective-permute-start.1 = (f32[4,16,128]{2,1,0:T(8,128)S(1)}, f32[4,16,128]{2,1,0:T(8,128)S(1)}, u32[]{:S(2)}, u32[]{:S(2)}) collective-permute-start(f32[4,16,128]{2,1,0:T(8,128)S(1)} %get-tuple-element.48), channel_id=1, source_target_pairs={{0,20},{1,21},{2,22},{3,23},{4,16},{5,17},{6,18},{7,19},{8,28},{9,... | collective-permute-start | bytes 98312 | tf_op jit(solution)/shard_map/ppermute | solution.py:407
  7.2 9.4 %collective-permute-start.2 = (f32[4,16,128]{2,1,0:T(8,128)S(1)}, f32[4,16,128]{2,1,0:T(8,128)S(1)}, u32[]{:S(2)}, u32[]{:S(2)}) collective-permute-start(f32[4,16,128]{2,1,0:T(8,128)S(1)} %get-tuple-element.49), channel_id=1, source_target_pairs={{0,28},{1,29},{2,30},{3,31},{4,24},{5,25},{6,26},{7,27},{8,20},{9,... | collective-permute-start | bytes 98312 | tf_op jit(solution)/shard_map/ppermute | solution.py:407
  10.8 5.8 %collective-permute-start.3 = (f32[4,16,128]{2,1,0:T(8,128)S(1)}, f32[4,16,128]{2,1,0:T(8,128)S(1)}, u32[]{:S(2)}, u32[]{:S(2)}) collective-permute-start(f32[4,16,128]{2,1,0:T(8,128)S(1)} %get-tuple-element.50), channel_id=1, source_target_pairs={{0,17},{1,16},{2,19},{3,18},{4,21},{5,20},{6,23},{7,22},{8,25},{9,... | collective-permute-start | bytes 98312 | tf_op jit(solution)/shard_map/ppermute | solution.py:407
  11.9 4.8 %collective-permute-start.4 = (f32[4,16,128]{2,1,0:T(8,128)S(1)}, f32[4,16,128]{2,1,0:T(8,128)S(1)}, u32[]{:S(2)}, u32[]{:S(2)}) collective-permute-start(f32[4,16,128]{2,1,0:T(8,128)S(1)} %get-tuple-element.51), channel_id=1, source_target_pairs={{0,19},{1,18},{2,17},{3,16},{4,23},{5,22},{6,21},{7,20},{8,27},{9,... | collective-permute-start | bytes 98312 | tf_op jit(solution)/shard_map/ppermute | solution.py:407
  15.7 0.8 copy-start.6
  17.8 3.1 %collective-permute-start.5 = (f32[4,16,128]{2,1,0:T(8,128)S(1)}, f32[4,16,128]{2,1,0:T(8,128)S(1)}, u32[]{:S(2)}, u32[]{:S(2)}) collective-permute-start(f32[4,16,128]{2,1,0:T(8,128)S(1)} %get-tuple-element.53), channel_id=1, source_target_pairs={{0,4},{1,5},{2,6},{3,7},{4,0},{5,1},{6,2},{7,3},{8,12},{9,13},{10,... | collective-permute-start | bytes 98312 | tf_op jit(solution)/shard_map/ppermute | solution.py:407
  18.2 4.0 %collective-permute-start.6 = (f32[4,16,128]{2,1,0:T(8,128)S(1)}, f32[4,16,128]{2,1,0:T(8,128)S(1)}, u32[]{:S(2)}, u32[]{:S(2)}) collective-permute-start(f32[4,16,128]{2,1,0:T(8,128)S(1)} %get-tuple-element.54), channel_id=1, source_target_pairs={{0,12},{1,13},{2,14},{3,15},{4,8},{5,9},{6,10},{7,11},{8,4},{9,5},... | collective-permute-start | bytes 98312 | tf_op jit(solution)/shard_map/ppermute | solution.py:407
  19.0 3.2 %collective-permute-start.7 = (f32[4,16,128]{2,1,0:T(8,128)S(1)}, f32[4,16,128]{2,1,0:T(8,128)S(1)}, u32[]{:S(2)}, u32[]{:S(2)}) collective-permute-start(f32[4,16,128]{2,1,0:T(8,128)S(1)} %get-tuple-element.55), channel_id=1, source_target_pairs={{0,1},{1,0},{2,3},{3,2},{4,5},{5,4},{6,7},{7,6},{8,9},{9,8},{10,11... | collective-permute-start | bytes 98312 | tf_op jit(solution)/shard_map/ppermute | solution.py:407
  19.1 4.0 %collective-permute-start.8 = (f32[4,16,128]{2,1,0:T(8,128)S(1)}, f32[4,16,128]{2,1,0:T(8,128)S(1)}, u32[]{:S(2)}, u32[]{:S(2)}) collective-permute-start(f32[4,16,128]{2,1,0:T(8,128)S(1)} %get-tuple-element.56), channel_id=1, source_target_pairs={{0,3},{1,2},{2,1},{3,0},{4,7},{5,6},{6,5},{7,4},{8,11},{9,10},{10,... | collective-permute-start | bytes 98312 | tf_op jit(solution)/shard_map/ppermute | solution.py:407
  23.7 4.2 %collective-permute-start.9 = (f32[4,16,128]{2,1,0:T(8,128)S(1)}, f32[4,16,128]{2,1,0:T(8,128)S(1)}, u32[]{:S(2)}, u32[]{:S(2)}) collective-permute-start(f32[4,16,128]{2,1,0:T(8,128)S(1)} %get-tuple-element.58), channel_id=1, source_target_pairs={{0,4},{1,5},{2,6},{3,7},{4,0},{5,1},{6,2},{7,3},{8,12},{9,13},{10,... | collective-permute-start | bytes 98312 | tf_op jit(solution)/shard_map/ppermute | solution.py:407
  24.6 4.0 %collective-permute-start.10 = (f32[4,16,128]{2,1,0:T(8,128)S(1)}, f32[4,16,128]{2,1,0:T(8,128)S(1)}, u32[]{:S(2)}, u32[]{:S(2)}) collective-permute-start(f32[4,16,128]{2,1,0:T(8,128)S(1)} %get-tuple-element.59), channel_id=1, source_target_pairs={{0,12},{1,13},{2,14},{3,15},{4,8},{5,9},{6,10},{7,11},{8,4},{9,5},... | collective-permute-start | bytes 98312 | tf_op jit(solution)/shard_map/ppermute | solution.py:407
  26.4 2.8 %collective-permute-start.11 = (f32[4,16,128]{2,1,0:T(8,128)S(1)}, f32[4,16,128]{2,1,0:T(8,128)S(1)}, u32[]{:S(2)}, u32[]{:S(2)}) collective-permute-start(f32[4,16,128]{2,1,0:T(8,128)S(1)} %get-tuple-element.60), channel_id=1, source_target_pairs={{0,1},{1,0},{2,3},{3,2},{4,5},{5,4},{6,7},{7,6},{8,9},{9,8},{10,11... | collective-permute-start | bytes 98312 | tf_op jit(solution)/shard_map/ppermute | solution.py:407
  26.6 4.0 %collective-permute-start.12 = (f32[4,16,128]{2,1,0:T(8,128)S(1)}, f32[4,16,128]{2,1,0:T(8,128)S(1)}, u32[]{:S(2)}, u32[]{:S(2)}) collective-permute-start(f32[4,16,128]{2,1,0:T(8,128)S(1)} %get-tuple-element.61), channel_id=1, source_target_pairs={{0,3},{1,2},{2,1},{3,0},{4,7},{5,6},{6,5},{7,4},{8,11},{9,10},{10,... | collective-permute-start | bytes 98312 | tf_op jit(solution)/shard_map/ppermute | solution.py:407
  30.6 5.8 %copy-start.2 = (f32[1,64,4,4,128]{4,3,2,1,0:T(4,128)S(1)}, f32[1,64,4,4,128]{4,3,2,1,0:T(4,128)}, u32[]{:S(2)}) copy-start(f32[1,64,4,4,128]{4,3,2,1,0:T(4,128)} %param.5) | copy-start | bytes 1572868
  31.2 3.2 %collective-permute-start.13 = (f32[4,16,128]{2,1,0:T(8,128)S(1)}, f32[4,16,128]{2,1,0:T(8,128)S(1)}, u32[]{:S(2)}, u32[]{:S(2)}) collective-permute-start(f32[4,16,128]{2,1,0:T(8,128)S(1)} %get-tuple-element.63), channel_id=1, source_target_pairs={{0,4},{1,5},{2,6},{3,7},{4,0},{5,1},{6,2},{7,3},{8,12},{9,13},{10,... | collective-permute-start | bytes 98312 | tf_op jit(solution)/shard_map/ppermute | solution.py:407
  31.6 4.0 %collective-permute-start.14 = (f32[4,16,128]{2,1,0:T(8,128)S(1)}, f32[4,16,128]{2,1,0:T(8,128)S(1)}, u32[]{:S(2)}, u32[]{:S(2)}) collective-permute-start(f32[4,16,128]{2,1,0:T(8,128)S(1)} %get-tuple-element.64), channel_id=1, source_target_pairs={{0,12},{1,13},{2,14},{3,15},{4,8},{5,9},{6,10},{7,11},{8,4},{9,5},... | collective-permute-start | bytes 98312 | tf_op jit(solution)/shard_map/ppermute | solution.py:407
  32.3 3.3 %collective-permute-start.15 = (f32[4,16,128]{2,1,0:T(8,128)S(1)}, f32[4,16,128]{2,1,0:T(8,128)S(1)}, u32[]{:S(2)}, u32[]{:S(2)}) collective-permute-start(f32[4,16,128]{2,1,0:T(8,128)S(1)} %get-tuple-element.65), channel_id=1, source_target_pairs={{0,1},{1,0},{2,3},{3,2},{4,5},{5,4},{6,7},{7,6},{8,9},{9,8},{10,11... | collective-permute-start | bytes 98312 | tf_op jit(solution)/shard_map/ppermute | solution.py:407
  32.3 4.0 %collective-permute-start.16 = (f32[4,16,128]{2,1,0:T(8,128)S(1)}, f32[4,16,128]{2,1,0:T(8,128)S(1)}, u32[]{:S(2)}, u32[]{:S(2)}) collective-permute-start(f32[4,16,128]{2,1,0:T(8,128)S(1)} %get-tuple-element.66), channel_id=1, source_target_pairs={{0,3},{1,2},{2,1},{3,0},{4,7},{5,6},{6,5},{7,4},{8,11},{9,10},{10,... | collective-permute-start | bytes 98312 | tf_op jit(solution)/shard_map/ppermute | solution.py:407
  63.5 1.9 %collective-permute-start.17 = (f32[2,144,128]{2,1,0:T(8,128)S(1)}, f32[2,144,128]{2,1,0:T(8,128)S(1)}, u32[]{:S(2)}, u32[]{:S(2)}) collective-permute-start(f32[2,144,128]{2,1,0:T(8,128)S(1)} %get-tuple-element.69), channel_id=1, source_target_pairs={{0,16},{16,0},{1,17},{17,1},{2,18},{18,2},{3,19},{19,3},{7,23},{23... | collective-permute-start | bytes 442376 | tf_op jit(solution)/shard_map/ppermute | solution.py:407
  64.5 4.6 %collective-permute-start.18 = (f32[2,144,128]{2,1,0:T(8,128)S(1)}, f32[2,144,128]{2,1,0:T(8,128)S(1)}, u32[]{:S(2)}, u32[]{:S(2)}) collective-permute-start(f32[2,144,128]{2,1,0:T(8,128)S(1)} %get-tuple-element.70), channel_id=1, source_target_pairs={{0,48},{16,1},{1,16},{17,2},{2,17},{18,3},{3,18},{19,7},{7,19},{23... | collective-permute-start | bytes 442376 | tf_op jit(solution)/shard_map/ppermute | solution.py:407
  69.7 1.3 collective-permute-start.19
  69.9 3.2 %collective-permute-start.20 = (f32[2,16,128]{2,1,0:T(8,128)S(1)}, f32[2,16,128]{2,1,0:T(8,128)S(1)}, u32[]{:S(2)}, u32[]{:S(2)}) collective-permute-start(f32[2,16,128]{2,1,0:T(8,128)S(1)} %get-tuple-element.73), channel_id=1, source_target_pairs={{0,48},{16,1},{1,16},{17,2},{2,17},{18,3},{3,18},{19,7},{7,19},{23... | collective-permute-start | bytes 49160 | tf_op jit(solution)/shard_map/ppermute | solution.py:407
  73.4 7.4 %collective-permute-start.22 = (f32[4,64,128]{2,1,0:T(8,128)S(1)}, f32[4,64,128]{2,1,0:T(8,128)S(1)}, u32[]{:S(2)}, u32[]{:S(2)}) collective-permute-start(f32[4,64,128]{2,1,0:T(8,128)S(1)} %shard_map.76.refs_6_), channel_id=1, source_target_pairs={{0,64},{16,80},{1,65},{17,81},{2,66},{18,82},{3,67},{19,83},{7,71}... | collective-permute-start | bytes 393224 | tf_op jit(solution)/shard_map/ppermute | solution.py:407
  76.7 8.6 %collective-permute-start.21 = (f32[4,64,128]{2,1,0:T(8,128)S(1)}, f32[4,64,128]{2,1,0:T(8,128)S(1)}, u32[]{:S(2)}, u32[]{:S(2)}) collective-permute-start(f32[4,64,128]{2,1,0:T(8,128)S(1)} %shard_map.76.refs_6_), channel_id=1, source_target_pairs={{0,192},{16,208},{1,193},{17,209},{2,194},{18,210},{3,195},{19,211... | collective-permute-start | bytes 393224 | tf_op jit(solution)/shard_map/ppermute | solution.py:407
  85.4 4.3 %collective-permute-start.23 = (f32[2,80,128]{2,1,0:T(8,128)S(1)}, f32[2,80,128]{2,1,0:T(8,128)S(1)}, u32[]{:S(2)}, u32[]{:S(2)}) collective-permute-start(f32[2,80,128]{2,1,0:T(8,128)S(1)} %get-tuple-element.75), channel_id=1, source_target_pairs={{0,16},{16,0},{1,17},{17,1},{2,18},{18,2},{3,19},{19,3},{7,23},{23... | collective-permute-start | bytes 245768 | tf_op jit(solution)/shard_map/ppermute | solution.py:407
  86.5 3.9 %collective-permute-start.24 = (f32[2,80,128]{2,1,0:T(8,128)S(1)}, f32[2,80,128]{2,1,0:T(8,128)S(1)}, u32[]{:S(2)}, u32[]{:S(2)}) collective-permute-start(f32[2,80,128]{2,1,0:T(8,128)S(1)} %get-tuple-element.76), channel_id=1, source_target_pairs={{0,48},{16,1},{1,16},{17,2},{2,17},{18,3},{3,18},{19,7},{7,19},{23... | collective-permute-start | bytes 245768 | tf_op jit(solution)/shard_map/ppermute | solution.py:407
  86.6 8.4 %collective-permute-start.27 = (f32[4,64,128]{2,1,0:T(8,128)S(1)}, f32[4,64,128]{2,1,0:T(8,128)S(1)}, u32[]{:S(2)}, u32[]{:S(2)}) collective-permute-start(f32[4,64,128]{2,1,0:T(8,128)S(1)} %collective-permute-done.22.refs_2_.refs_5_), channel_id=1, source_target_pairs={{0,64},{16,80},{1,65},{17,81},{2,66},{18,82},{3,67},{19,83},{7,71}... | collective-permute-start | bytes 393224 | tf_op jit(solution)/shard_map/ppermute | solution.py:407
  91.0 4.0 %collective-permute-start.25 = (f32[2,80,128]{2,1,0:T(8,128)S(1)}, f32[2,80,128]{2,1,0:T(8,128)S(1)}, u32[]{:S(2)}, u32[]{:S(2)}) collective-permute-start(f32[2,80,128]{2,1,0:T(8,128)S(1)} %get-tuple-element.78), channel_id=1, source_target_pairs={{0,16},{16,0},{1,17},{17,1},{2,18},{18,2},{3,19},{19,3},{7,23},{23... | collective-permute-start | bytes 245768 | tf_op jit(solution)/shard_map/ppermute | solution.py:407
  91.2 4.2 %collective-permute-start.26 = (f32[2,80,128]{2,1,0:T(8,128)S(1)}, f32[2,80,128]{2,1,0:T(8,128)S(1)}, u32[]{:S(2)}, u32[]{:S(2)}) collective-permute-start(f32[2,80,128]{2,1,0:T(8,128)S(1)} %get-tuple-element.79), channel_id=1, source_target_pairs={{0,48},{16,1},{1,16},{17,2},{2,17},{18,3},{3,18},{19,7},{7,19},{23... | collective-permute-start | bytes 245768 | tf_op jit(solution)/shard_map/ppermute | solution.py:407
  96.0 3.0 %collective-permute-start.28 = (f32[2,80,128]{2,1,0:T(8,128)S(1)}, f32[2,80,128]{2,1,0:T(8,128)S(1)}, u32[]{:S(2)}, u32[]{:S(2)}) collective-permute-start(f32[2,80,128]{2,1,0:T(8,128)S(1)} %get-tuple-element.81), channel_id=1, source_target_pairs={{0,16},{16,0},{1,17},{17,1},{2,18},{18,2},{3,19},{19,3},{7,23},{23... | collective-permute-start | bytes 245768 | tf_op jit(solution)/shard_map/ppermute | solution.py:407
  98.1 3.9 %collective-permute-start.29 = (f32[2,80,128]{2,1,0:T(8,128)S(1)}, f32[2,80,128]{2,1,0:T(8,128)S(1)}, u32[]{:S(2)}, u32[]{:S(2)}) collective-permute-start(f32[2,80,128]{2,1,0:T(8,128)S(1)} %get-tuple-element.82), channel_id=1, source_target_pairs={{0,48},{16,1},{1,16},{17,2},{2,17},{18,3},{3,18},{19,7},{7,19},{23... | collective-permute-start | bytes 245768 | tf_op jit(solution)/shard_map/ppermute | solution.py:407
  102.6 1.6 %collective-permute-start.30 = (f32[2,80,128]{2,1,0:T(8,128)S(1)}, f32[2,80,128]{2,1,0:T(8,128)S(1)}, u32[]{:S(2)}, u32[]{:S(2)}) collective-permute-start(f32[2,80,128]{2,1,0:T(8,128)S(1)} %get-tuple-element.84), channel_id=1, source_target_pairs={{0,16},{16,0},{1,17},{17,1},{2,18},{18,2},{3,19},{19,3},{7,23},{23... | collective-permute-start | bytes 245768 | tf_op jit(solution)/shard_map/ppermute | solution.py:407
  103.0 3.9 %collective-permute-start.31 = (f32[2,80,128]{2,1,0:T(8,128)S(1)}, f32[2,80,128]{2,1,0:T(8,128)S(1)}, u32[]{:S(2)}, u32[]{:S(2)}) collective-permute-start(f32[2,80,128]{2,1,0:T(8,128)S(1)} %get-tuple-element.85), channel_id=1, source_target_pairs={{0,48},{16,1},{1,16},{17,2},{2,17},{18,3},{3,18},{19,7},{7,19},{23... | collective-permute-start | bytes 245768 | tf_op jit(solution)/shard_map/ppermute | solution.py:407
  107.5 1.4 %collective-permute-start.32 = (f32[2,80,128]{2,1,0:T(8,128)S(1)}, f32[2,80,128]{2,1,0:T(8,128)S(1)}, u32[]{:S(2)}, u32[]{:S(2)}) collective-permute-start(f32[2,80,128]{2,1,0:T(8,128)S(1)} %get-tuple-element.87), channel_id=1, source_target_pairs={{0,16},{16,0},{1,17},{17,1},{2,18},{18,2},{3,19},{19,3},{7,23},{23... | collective-permute-start | bytes 245768 | tf_op jit(solution)/shard_map/ppermute | solution.py:407
  108.0 3.9 %collective-permute-start.33 = (f32[2,80,128]{2,1,0:T(8,128)S(1)}, f32[2,80,128]{2,1,0:T(8,128)S(1)}, u32[]{:S(2)}, u32[]{:S(2)}) collective-permute-start(f32[2,80,128]{2,1,0:T(8,128)S(1)} %get-tuple-element.88), channel_id=1, source_target_pairs={{0,48},{16,1},{1,16},{17,2},{2,17},{18,3},{3,18},{19,7},{7,19},{23... | collective-permute-start | bytes 245768 | tf_op jit(solution)/shard_map/ppermute | solution.py:407
  112.6 1.4 %collective-permute-start.34 = (f32[2,80,128]{2,1,0:T(8,128)S(1)}, f32[2,80,128]{2,1,0:T(8,128)S(1)}, u32[]{:S(2)}, u32[]{:S(2)}) collective-permute-start(f32[2,80,128]{2,1,0:T(8,128)S(1)} %get-tuple-element.90), channel_id=1, source_target_pairs={{0,16},{16,0},{1,17},{17,1},{2,18},{18,2},{3,19},{19,3},{7,23},{23... | collective-permute-start | bytes 245768 | tf_op jit(solution)/shard_map/ppermute | solution.py:407
  112.8 3.9 %collective-permute-start.35 = (f32[2,80,128]{2,1,0:T(8,128)S(1)}, f32[2,80,128]{2,1,0:T(8,128)S(1)}, u32[]{:S(2)}, u32[]{:S(2)}) collective-permute-start(f32[2,80,128]{2,1,0:T(8,128)S(1)} %get-tuple-element.91), channel_id=1, source_target_pairs={{0,48},{16,1},{1,16},{17,2},{2,17},{18,3},{3,18},{19,7},{7,19},{23... | collective-permute-start | bytes 245768 | tf_op jit(solution)/shard_map/ppermute | solution.py:407
